TPU v7x, 256 devices: a whole 4x4x8 slice. The times are simulated.
256 devices in a mesh: gx: 32 (over z, x), gy: 8 (over y, core).
Axes of the slice: x: 4, y: 4, z: 8, core: 2. Of those that a mesh axis runs over, the one named last changes fastest.
Arguments:
- field: float32 [36, 128, 4096], P(None, 'gx', 'gy'), may hold values from -6 to 6
- mix_weights: float32 [2, 36, 36, 32, 1024], P(None, None, None, 'gx', 'gy'), may hold values from -0.75 to 0.75
- kept_z: int32 [1024], P('gy'), may hold values from 1 to 32, as said below
- conv_kernels: float32 [3, 27, 36, 36], replicated, may hold values from -0.1875 to 0.1875
Outputs:
- layer_out: float32 [36, 128, 4096], P(None, 'gx', 'gy')
Inputs may be any that keep to these rules, and one draw needn't show every extreme that they name: kept_z[j * 32 + l] counts the lowest z modes kept for the j-th kept x mode and the l-th kept y mode; one entry equals 32.
All inputs are finite; a program needn't handle non-finite values.
Results may differ from a plain program's by a relative error of at most 0.0001.
Values sent between devices are 32-bit elements; how exact they have to be, the bound alone decides.
No kernel may reach another device: no remote copies, remote signals or barrier semaphores. Data moves between devices by JAX's collectives and lax.ppermute only.
A program may use at most 128 MiB of HBM per device.

v0:
```python
import math

import jax
import jax.numpy as jnp
from jax import lax
from jax.sharding import PartitionSpec as P

NZ = 64
KY = 32


precise = lax.Precision.HIGHEST


def with_halo(cells, sides, width):
    for axis, dim in sides:
        count = lax.axis_size(axis)
        ends = count - 1
        head = lax.slice_in_dim(cells, 0, width, axis=dim)
        tail = lax.slice_in_dim(cells, cells.shape[dim] - width, cells.shape[dim], axis=dim)
        cells = jnp.concatenate(
            [
                lax.ppermute(tail, axis, [(i, (i + 1) % count) for i in range(ends)]),
                cells,
                lax.ppermute(head, axis, [((i + 1) % count, i) for i in range(ends)]),
            ],
            axis=dim,
        )
    return cells


def contract(form, left, right):
    return jnp.einsum(form, left, right, precision=precise)


def phase_table(positions, frequencies, length):
    product = positions[:, None] * frequencies[None, :] % length
    angles = product.astype(jnp.float32) * (2.0 * math.pi / length)
    return (jnp.cos(angles), jnp.sin(angles))


def kept_frequencies(count, length):
    index = jnp.arange(count, dtype=jnp.int32)
    return jnp.where(index < count // 2, index, length - count + index)


def forward_pair(real_part, imag_part, cosine, sine_table, form):
    return (
        contract(form, real_part, cosine) + contract(form, imag_part, sine_table),
        contract(form, imag_part, cosine) - contract(form, real_part, sine_table),
    )


def inverse_pair(real_part, imag_part, cosine, sine_table, form):
    return (
        contract(form, real_part, cosine) - contract(form, imag_part, sine_table),
        contract(form, imag_part, cosine) + contract(form, real_part, sine_table),
    )


def convolve(padded, kernel):
    channels = padded.shape[0]
    width_x = padded.shape[1] - 2
    width_y = padded.shape[2] - 2
    depth_z = padded.shape[3]
    outputs = kernel.shape[2]
    flat = padded.reshape(channels, width_x + 2, (width_y + 2) * depth_z)
    length = width_y * depth_z
    z_position = jnp.arange(length, dtype=jnp.int32) % depth_z
    lower_mask = (z_position >= 1).astype(jnp.float32)
    upper_mask = (z_position <= depth_z - 2).astype(jnp.float32)
    result = None
    for shift_x in range(3):
        taps = kernel[9 * shift_x : 9 * shift_x + 9]
        tap_terms = contract("cxq,tco->toxq", flat[:, shift_x : shift_x + width_x], taps)
        tap_terms = jnp.pad(tap_terms, ((0, 0), (0, 0), (0, 0), (1, 1)))
        for shift_y in range(3):
            for shift_z in range(3):
                start = shift_y * depth_z + shift_z
                piece = tap_terms[3 * shift_y + shift_z, :, :, start : start + length]
                if shift_z == 0:
                    piece = piece * lower_mask
                elif shift_z == 2:
                    piece = piece * upper_mask
                result = piece if result is None else result + piece
    return result.reshape(outputs, width_x, width_y, depth_z)


def gelu_exact(values):
    return jax.nn.gelu(values, approximate=False)


def shards(field, mix_weights, kept_z, conv_kernels):
    channels = field.shape[0]
    cells_x = field.shape[1]
    cells_y = field.shape[2] // NZ
    size_x = lax.axis_size("gx")
    size_y = lax.axis_size("gy")
    full_x = cells_x * size_x
    full_y = cells_y * size_y
    mz_local = mix_weights.shape[3]
    modes_z = mz_local * size_x
    kx_local = mix_weights.shape[4] // KY
    modes_x = kx_local * size_y
    index_x = lax.axis_index("gx")
    volume = field.reshape(channels, cells_x, cells_y, NZ)
    scale_in = 1.0 / math.sqrt(full_x * full_y * NZ)
    scale_out = 1.0 / math.sqrt(modes_x * KY * modes_z)
    freq_x = kept_frequencies(modes_x, full_x)
    freq_y = kept_frequencies(KY, full_y)
    z_cells = jnp.arange(NZ, dtype=jnp.int32)
    cos_z, sin_z = phase_table(z_cells, jnp.arange(modes_z, dtype=jnp.int32), NZ)
    z_real = contract("cxyz,zk->kcxy", volume, cos_z) * scale_in
    z_imag = -contract("cxyz,zk->kcxy", volume, sin_z) * scale_in
    z_modes = jnp.stack([z_real, z_imag], 1)
    cos_x, sin_x = phase_table(jnp.arange(full_x, dtype=jnp.int32), freq_x, full_x)
    received = lax.all_to_all(z_modes, "gx", split_axis=0, concat_axis=3, tiled=True)
    real_x, imag_x = forward_pair(received[:, 0], received[:, 1], cos_x, sin_x, "kcxy,xj->kcjy")
    x_modes = jnp.stack([real_x, imag_x], 1)
    cos_y, sin_y = phase_table(jnp.arange(full_y, dtype=jnp.int32), freq_y, full_y)
    received = lax.all_to_all(x_modes, "gy", split_axis=3, concat_axis=4, tiled=True)
    real_y, imag_y = forward_pair(received[:, 0], received[:, 1], cos_y, sin_y, "kcjy,yl->kcjl")
    y_modes = jnp.stack([real_y, imag_y], 1)
    flat_modes = y_modes.reshape(mz_local, 2, channels, kx_local * KY)
    mixed_real = contract("cokm,kcm->kom", mix_weights[0], flat_modes[:, 0]) - contract(
        "cokm,kcm->kom", mix_weights[1], flat_modes[:, 1]
    )
    mixed_imag = contract("cokm,kcm->kom", mix_weights[0], flat_modes[:, 1]) + contract(
        "cokm,kcm->kom", mix_weights[1], flat_modes[:, 0]
    )
    z_global = index_x * mz_local + jnp.arange(mz_local, dtype=jnp.int32)
    keep_mask = (z_global[:, None] < kept_z[None, :]).astype(jnp.float32)[:, None, :]
    mixed = jnp.stack([mixed_real * keep_mask, mixed_imag * keep_mask], 1).reshape(
        mz_local, 2, channels, kx_local, KY
    )
    back_real, back_imag = inverse_pair(mixed[:, 0], mixed[:, 1], cos_y, sin_y, "kcjl,yl->kcjy")
    in_y = jnp.stack([back_real, back_imag], 1)
    x_again = lax.all_to_all(in_y, "gy", split_axis=4, concat_axis=3, tiled=True)
    cells_real, cells_imag = inverse_pair(
        x_again[:, 0], x_again[:, 1], cos_x, sin_x, "kcjy,xj->kcxy"
    )
    cells_modes = jnp.stack([cells_real, cells_imag], 1)
    z_index = jnp.arange(modes_z, dtype=jnp.int32)
    cos_back, sin_back = phase_table(z_index, z_cells, NZ)
    weighting = jnp.where(z_index == 0, 1.0, 2.0).astype(jnp.float32)[:, None] * scale_out
    received = lax.all_to_all(cells_modes, "gx", split_axis=3, concat_axis=0, tiled=True)
    spectral = contract("kcxy,kz->cxyz", received[:, 0], cos_back * weighting) - contract(
        "kcxy,kz->cxyz", received[:, 1], sin_back * weighting
    )

    def with_rim(values):
        return with_halo(values, (("gx", 1), ("gy", 2)), 1)

    first = gelu_exact(convolve(with_rim(volume), conv_kernels[0]))
    second = gelu_exact(convolve(with_rim(first), conv_kernels[1]))
    third = convolve(with_rim(second), conv_kernels[2])
    return gelu_exact(spectral + third).reshape(channels, cells_x, cells_y * NZ)


def solution(mesh):
    placed = (P(None, "gx", "gy"), P(None, None, None, "gx", "gy"), P("gy"), P())
    return jax.shard_map(
        shards, mesh=mesh, in_specs=placed, out_specs=P(None, "gx", "gy"), check_vma=False
    )
```

profile of v0, /device:TPU:1, one launch (start us, length us, event | category | flops | bytes accessed | tf_op | source)
XLA Modules:
  0.0 467.4 jit_solution(4625146706499879947)
XLA Ops:
  1.2 4.0 collective-permute-start
  14.6 12.9 %all-to-all-start = ((f32[32,1,2304]{2,1,0:T(1,128)}), f32[32,1,2304]{2,1,0:T(1,128)}, u32[]{:S(2)}, u32[]{:S(2)}) async-start(f32[32,1,2304]{2,1,0:T(1,128)} %reshape.434), calls=%async_computation | async-start | bytes 589824 | tf_op jit(solution)/shard_map/all_to_all | solution.py:117
  28.9 4.6 collective-permute-start.2
  35.7 4.3 collective-permute-done.3
  40.8 4.0 convolution_bitcast_fusion.6
  44.9 5.9 %convolution_bitcast_fusion.7 = f32[9,36,4,640]{3,1,0,2:T(8,128)} fusion(f32[36,6,640]{2,0,1:T(8,128)S(1)} %reshape.396, f32[3,27,36,36]{3,2,1,0:T(8,128)} %param.7), kind=kOutput, calls=%fused_computation.33 | convolution fusion | flops 358318080 | bytes 3911680 | tf_op jit(solution)/shard_map/cxq,tco->toxq/dot_general | solution.py:33
  50.7 5.9 %convolution_bitcast_fusion.8 = f32[9,36,4,640]{3,1,0,2:T(8,128)} fusion(f32[36,6,640]{2,0,1:T(8,128)S(1)} %reshape.396, f32[3,27,36,36]{3,2,1,0:T(8,128)} %param.7), kind=kOutput, calls=%fused_computation.34 | convolution fusion | flops 358318080 | bytes 3911680 | tf_op jit(solution)/shard_map/cxq,tco->toxq/dot_general | solution.py:33
  82.9 4.0 pad_slice_fusion.15
  121.0 4.0 pad_slice_fusion.17
  159.1 5.7 %fusion.20 = f32[36,4,8,64]{3,2,1,0:T(8,128)S(1)} fusion(f32[36,4,8,64]{3,2,1,0:T(8,128)S(1)} %squeeze.296, f32[36,4,8,64]{3,2,1,0:T(8,128)S(1)} %squeeze.295, f32[36,4,8,64]{3,2,1,0:T(8,128)S(1)} %squeeze.294, f32[36,4,8,64]{3,2,1,0:T(8,128)S(1)} %squeeze.293, f32[36,4,8,64]{3,2,1,0:T(8,128)S(1)} %squeeze.292, f32[36,4,8,64]{3,2,1,0:T(8,128)} %squeeze.291, ...), kind=kLoop, calls=%fused_computation.65 | loop fusion | flops 7962624 | bytes 8261632 | tf_op jit(solution)/shard_map/mul | solution.py:90
  184.8 4.0 convolution_bitcast_fusion.5
  203.3 4.0 convolution_bitcast_fusion.4
  225.5 4.0 convolution_bitcast_fusion.3
  253.8 6.2 %fusion.22 = f32[36,4,8,64]{3,2,1,0:T(8,128)S(1)} fusion(f32[36,4,8,64]{3,2,1,0:T(8,128)} %squeeze.323, f32[36,4,8,64]{3,2,1,0:T(8,128)} %squeeze.322, f32[36,4,8,64]{3,2,1,0:T(8,128)} %squeeze.321, f32[36,4,8,64]{3,2,1,0:T(8,128)} %squeeze.320, f32[36,4,8,64]{3,2,1,0:T(8,128)} %squeeze.319, f32[36,4,8,64]{3,2,1,0:T(8,128)} %squeeze.318, ...), kind=kLoop, calls=%fused_computation.67 | loop fusion | flops 7962624 | bytes 8261632 | tf_op jit(solution)/shard_map/mul | solution.py:90
  270.2 4.0 collective-permute-start.10
  289.3 5.8 %convolution_bitcast_fusion.2 = f32[9,36,4,640]{3,1,0,2:T(8,128)} fusion(f32[36,4,640]{2,1,0:T(4,128)S(1)} %get-tuple-element.96, f32[3,27,36,36]{3,2,1,0:T(8,128)} %param.7), kind=kOutput, calls=%fused_computation.28 | convolution fusion | flops 358318080 | bytes 3870720 | tf_op jit(solution)/shard_map/cxq,tco->toxq/dot_general | solution.py:33
  295.1 5.9 %convolution_bitcast_fusion.1 = f32[9,36,4,640]{3,1,0,2:T(8,128)} fusion(f32[36,4,640]{2,1,0:T(4,128)S(1)} %get-tuple-element.97, f32[3,27,36,36]{3,2,1,0:T(8,128)} %param.7), kind=kOutput, calls=%fused_computation.27 | convolution fusion | flops 358318080 | bytes 3870720 | tf_op jit(solution)/shard_map/cxq,tco->toxq/dot_general | solution.py:33
  314.3 5.6 %all-to-all-start.1 = ((f32[8,1,2304]{2,1,0:T(1,128)}), f32[8,1,2304]{2,1,0:T(1,128)S(1)}, u32[]{:S(2)}, u32[]{:S(2)}) async-start(f32[8,1,2304]{2,1,0:T(1,128)} %reshape.436), calls=%async_computation.1 | async-start | bytes 147456 | tf_op jit(solution)/shard_map/all_to_all | solution.py:121
  328.9 4.0 fusion
  343.5 4.0 all-to-all-start.2
  347.5 4.3 pad_slice_fusion.3
  405.1 13.6 %all-to-all-start.3 = ((f32[32,1,2304]{2,1,0:T(1,128)}), f32[32,1,2304]{2,1,0:T(1,128)}, u32[]{:S(2)}, u32[]{:S(2)}) async-start(f32[32,1,2304]{2,1,0:T(1,128)} %reshape.440), calls=%async_computation.3 | async-start | bytes 589824 | tf_op jit(solution)/shard_map/all_to_all | solution.py:146
  418.8 4.1 convolution_bitcast_fusion
  461.2 5.0 %fusion.24 = f32[36,4,8,64]{3,2,1,0:T(8,128)S(1)} fusion(f32[36,4,8,64]{3,2,1,0:T(8,128)} %squeeze.350, f32[36,4,8,64]{3,2,1,0:T(8,128)} %squeeze.349, f32[36,4,8,64]{3,2,1,0:T(8,128)} %squeeze.348, f32[36,4,8,64]{3,2,1,0:T(8,128)} %squeeze.347, f32[36,4,8,64]{3,2,1,0:T(8,128)} %squeeze.346, f32[36,4,8,64]{3,2,1,0:T(8,128)} %squeeze.345, ...), kind=kLoop, calls=%fused_computation.69 | loop fusion | flops 8110080 | bytes 8851456 | tf_op jit(solution)/shard_map/mul | solution.py:90
  (327 shorter events, 336.3 us)
Async XLA Ops:
  1.2 27.5 %collective-permute-start = (f32[36,1,8,64]{3,2,0,1:T(8,128)S(1)}, f32[36,1,8,64]{3,2,0,1:T(8,128)S(1)}, u32[]{:S(2)}, u32[]{:S(2)}) collective-permute-start(f32[36,1,8,64]{3,2,0,1:T(8,128)S(1)} %copy.591), channel_id=1, source_target_pairs={{0,8},{8,16},{16,24},{24,32},{32,40},{40,48},{48,56},{56,64},{64,7... | collective-permute-start | bytes 221192 | tf_op jit(solution)/shard_map/ppermute | solution.py:23
  5.2 23.5 %collective-permute-start.1 = (f32[36,1,8,64]{3,2,0,1:T(8,128)S(1)}, f32[36,1,8,64]{3,2,0,1:T(8,128)S(1)}, u32[]{:S(2)}, u32[]{:S(2)}) collective-permute-start(f32[36,1,8,64]{3,2,0,1:T(8,128)S(1)} %copy.592), channel_id=1, source_target_pairs={{8,0},{16,8},{24,16},{32,24},{40,32},{48,40},{56,48},{64,56},{72,6... | collective-permute-start | bytes 221192 | tf_op jit(solution)/shard_map/ppermute | solution.py:25
  11.9 15.6 %copy-start.9 = (f32[2,36,36,1,128]{4,3,2,1,0:T(1,128)S(1)}, f32[2,36,36,1,128]{4,3,2,1,0:T(1,128)}, u32[]{:S(2)}) copy-start(f32[2,36,36,1,128]{4,3,2,1,0:T(1,128)} %param.5) | copy-start | bytes 3981316
  14.6 286.4 %all-to-all-start = ((f32[32,1,2304]{2,1,0:T(1,128)}), f32[32,1,2304]{2,1,0:T(1,128)}, u32[]{:S(2)}, u32[]{:S(2)}) async-start(f32[32,1,2304]{2,1,0:T(1,128)} %reshape.434), calls=%async_computation | async-start | bytes 589824 | tf_op jit(solution)/shard_map/all_to_all | solution.py:117
  28.9 6.7 %collective-permute-start.2 = (f32[36,6,1,64]{3,2,0,1:T(1,128)S(1)}, f32[36,6,1,64]{3,2,0,1:T(1,128)S(1)}, u32[]{:S(2)}, u32[]{:S(2)}) collective-permute-start(f32[36,6,1,64]{3,2,0,1:T(1,128)S(1)} %get-tuple-element.94), channel_id=1, source_target_pairs={{0,1},{1,2},{2,3},{3,4},{4,5},{5,6},{6,7},{8,9},{9,10},{10,11},{11... | collective-permute-start | bytes 165896 | tf_op jit(solution)/shard_map/ppermute | solution.py:23
  33.6 6.5 %collective-permute-start.3 = (f32[36,6,1,64]{3,2,0,1:T(1,128)S(1)}, f32[36,6,1,64]{3,2,0,1:T(1,128)S(1)}, u32[]{:S(2)}, u32[]{:S(2)}) collective-permute-start(f32[36,6,1,64]{3,2,0,1:T(1,128)S(1)} %get-tuple-element.95), channel_id=1, source_target_pairs={{1,0},{2,1},{3,2},{4,3},{5,4},{6,5},{7,6},{9,8},{10,9},{11,10},{12... | collective-permute-start | bytes 165896 | tf_op jit(solution)/shard_map/ppermute | solution.py:25
  164.8 5.4 %collective-permute-start.4 = (f32[36,1,8,64]{3,2,1,0:T(8,128)S(1)}, f32[36,1,8,64]{3,2,1,0:T(8,128)S(1)}, u32[]{:S(2)}, u32[]{:S(2)}) collective-permute-start(f32[36,1,8,64]{3,2,1,0:T(8,128)S(1)} %get-tuple-element.104), channel_id=1, source_target_pairs={{0,8},{8,16},{16,24},{24,32},{32,40},{40,48},{48,56},{56,64},{64,7... | collective-permute-start | bytes 221192 | tf_op jit(solution)/shard_map/ppermute | solution.py:23
  168.2 5.9 %collective-permute-start.5 = (f32[36,1,8,64]{3,2,1,0:T(8,128)S(1)}, f32[36,1,8,64]{3,2,1,0:T(8,128)S(1)}, u32[]{:S(2)}, u32[]{:S(2)}) collective-permute-start(f32[36,1,8,64]{3,2,1,0:T(8,128)S(1)} %get-tuple-element.105), channel_id=1, source_target_pairs={{8,0},{16,8},{24,16},{32,24},{40,32},{48,40},{56,48},{64,56},{72,6... | collective-permute-start | bytes 221192 | tf_op jit(solution)/shard_map/ppermute | solution.py:25
  174.2 5.6 %collective-permute-start.6 = (f32[36,6,1,64]{3,2,1,0:T(1,128)S(1)}, f32[36,6,1,64]{3,2,1,0:T(1,128)S(1)}, u32[]{:S(2)}, u32[]{:S(2)}) collective-permute-start(f32[36,6,1,64]{3,2,1,0:T(1,128)S(1)} %get-tuple-element.92), channel_id=1, source_target_pairs={{0,1},{1,2},{2,3},{3,4},{4,5},{5,6},{6,7},{8,9},{9,10},{10,11},{11... | collective-permute-start | bytes 165896 | tf_op jit(solution)/shard_map/ppermute | solution.py:23
  177.7 6.1 %collective-permute-start.7 = (f32[36,6,1,64]{3,2,1,0:T(1,128)S(1)}, f32[36,6,1,64]{3,2,1,0:T(1,128)S(1)}, u32[]{:S(2)}, u32[]{:S(2)}) collective-permute-start(f32[36,6,1,64]{3,2,1,0:T(1,128)S(1)} %get-tuple-element.93), channel_id=1, source_target_pairs={{1,0},{2,1},{3,2},{4,3},{5,4},{6,5},{7,6},{9,8},{10,9},{11,10},{12... | collective-permute-start | bytes 165896 | tf_op jit(solution)/shard_map/ppermute | solution.py:25
  179.8 132.6 %copy-start.22 = (s32[32]{0:T(128)}, s32[32]{0:T(128)S(1)}, u32[]{:S(2)}) copy-start(s32[32]{0:T(128)S(1)} %compare_select_fusion.1) | copy-start | bytes 388
  253.7 22.9 %copy-start.1 = (f32[1,36,36,1,128]{4,3,2,1,0:T(1,128)S(1)}, f32[1,36,36,1,128]{4,3,2,1,0:T(1,128)}, u32[]{:S(2)}) copy-start(f32[1,36,36,1,128]{4,3,2,1,0:T(1,128)} %get-tuple-element.86) | copy-start | bytes 1990660
  260.0 5.6 %collective-permute-start.8 = (f32[36,1,8,64]{3,2,1,0:T(8,128)S(1)}, f32[36,1,8,64]{3,2,1,0:T(8,128)S(1)}, u32[]{:S(2)}, u32[]{:S(2)}) collective-permute-start(f32[36,1,8,64]{3,2,1,0:T(8,128)S(1)} %get-tuple-element.102), channel_id=1, source_target_pairs={{0,8},{8,16},{16,24},{24,32},{32,40},{40,48},{48,56},{56,64},{64,7... | collective-permute-start | bytes 221192 | tf_op jit(solution)/shard_map/ppermute | solution.py:23
  263.5 5.9 %collective-permute-start.9 = (f32[36,1,8,64]{3,2,1,0:T(8,128)S(1)}, f32[36,1,8,64]{3,2,1,0:T(8,128)S(1)}, u32[]{:S(2)}, u32[]{:S(2)}) collective-permute-start(f32[36,1,8,64]{3,2,1,0:T(8,128)S(1)} %get-tuple-element.103), channel_id=1, source_target_pairs={{8,0},{16,8},{24,16},{32,24},{40,32},{48,40},{56,48},{64,56},{72,6... | collective-permute-start | bytes 221192 | tf_op jit(solution)/shard_map/ppermute | solution.py:25
  270.2 13.7 %collective-permute-start.10 = (f32[36,6,1,64]{3,2,1,0:T(1,128)}, f32[36,6,1,64]{3,2,1,0:T(1,128)}, u32[]{:S(2)}, u32[]{:S(2)}) collective-permute-start(f32[36,6,1,64]{3,2,1,0:T(1,128)} %get-tuple-element.90), channel_id=1, source_target_pairs={{0,1},{1,2},{2,3},{3,4},{4,5},{5,6},{6,7},{8,9},{9,10},{10,11},{11... | collective-permute-start | bytes 165896 | tf_op jit(solution)/shard_map/ppermute | solution.py:23
  274.2 9.7 %collective-permute-start.11 = (f32[36,6,1,64]{3,2,1,0:T(1,128)}, f32[36,6,1,64]{3,2,1,0:T(1,128)}, u32[]{:S(2)}, u32[]{:S(2)}) collective-permute-start(f32[36,6,1,64]{3,2,1,0:T(1,128)} %get-tuple-element.91), channel_id=1, source_target_pairs={{1,0},{2,1},{3,2},{4,3},{5,4},{6,5},{7,6},{9,8},{10,9},{11,10},{12... | collective-permute-start | bytes 165896 | tf_op jit(solution)/shard_map/ppermute | solution.py:25
  314.3 10.4 %all-to-all-start.1 = ((f32[8,1,2304]{2,1,0:T(1,128)}), f32[8,1,2304]{2,1,0:T(1,128)S(1)}, u32[]{:S(2)}, u32[]{:S(2)}) async-start(f32[8,1,2304]{2,1,0:T(1,128)} %reshape.436), calls=%async_computation.1 | async-start | bytes 147456 | tf_op jit(solution)/shard_map/all_to_all | solution.py:121
  343.5 53.7 %all-to-all-start.2 = ((f32[8,1,2304]{2,1,0:T(1,128)}), f32[8,1,2304]{2,1,0:T(1,128)S(1)}, u32[]{:S(2)}, u32[]{:S(2)}) async-start(f32[8,1,2304]{2,1,0:T(1,128)} %reshape.438), calls=%async_computation.2 | async-start | bytes 147456 | tf_op jit(solution)/shard_map/all_to_all | solution.py:138
  366.0 12.9 %copy-start.21 = (f32[1,36,4,512]{3,1,0,2:T(8,128)S(1)}, f32[1,36,4,512]{3,1,0,2:T(8,128)}, u32[]{:S(2)}) copy-start(f32[1,36,4,512]{3,1,0,2:T(8,128)} %get-tuple-element.16) | copy-start | bytes 884740
  368.9 12.9 %copy-start.20 = (f32[1,36,4,512]{3,1,0,2:T(8,128)S(1)}, f32[1,36,4,512]{3,1,0,2:T(8,128)}, u32[]{:S(2)}) copy-start(f32[1,36,4,512]{3,1,0,2:T(8,128)} %get-tuple-element.17) | copy-start | bytes 884740
  372.9 11.9 %copy-start.19 = (f32[1,36,4,512]{3,1,0,2:T(8,128)S(1)}, f32[1,36,4,512]{3,1,0,2:T(8,128)}, u32[]{:S(2)}) copy-start(f32[1,36,4,512]{3,1,0,2:T(8,128)} %get-tuple-element.18) | copy-start | bytes 884740
  379.8 12.0 %copy-start.18 = (f32[1,36,4,512]{3,1,0,2:T(8,128)S(1)}, f32[1,36,4,512]{3,1,0,2:T(8,128)}, u32[]{:S(2)}) copy-start(f32[1,36,4,512]{3,1,0,2:T(8,128)} %get-tuple-element.20) | copy-start | bytes 884740
  382.8 12.0 %copy-start.17 = (f32[1,36,4,512]{3,1,0,2:T(8,128)S(1)}, f32[1,36,4,512]{3,1,0,2:T(8,128)}, u32[]{:S(2)}) copy-start(f32[1,36,4,512]{3,1,0,2:T(8,128)} %get-tuple-element.21) | copy-start | bytes 884740
  405.1 47.5 %all-to-all-start.3 = ((f32[32,1,2304]{2,1,0:T(1,128)}), f32[32,1,2304]{2,1,0:T(1,128)}, u32[]{:S(2)}, u32[]{:S(2)}) async-start(f32[32,1,2304]{2,1,0:T(1,128)} %reshape.440), calls=%async_computation.3 | async-start | bytes 589824 | tf_op jit(solution)/shard_map/all_to_all | solution.py:146
  (18 other events, 107.2 us)
where the time goes:
time: 477 us; the launch traced here: 467 us
  local copies, waits for them, and re-layouts  278 us (58%)
  matrix products  71.5 us (15%)
  starting transfers between devices  69 us (14%)
  other arithmetic  29.6 us (6%)
  waiting for transfers between devices  18.2 us (4%)
    squeeze x81, local copies, waits for them, and re-layouts, convolve(): piece = tap_terms[3 * shift_y + shift_z, :, :, start:start + length]  126 us
    slice x90, local copies, waits for them, and re-layouts, convolve(): piece = tap_terms[3 * shift_y + shift_z, :, :, start:start + length]  117 us
    dot_general x33, matrix products, contract(): return jnp.einsum(form, left, right, precision=precise)  71.5 us
    ppermute x6, starting transfers between devices, with_halo(): lax.ppermute(tail, axis, [(i, (i + 1) % count) for i in range(ends)])  22.8 us
    mul x3, other arithmetic, gelu_exact(): return jax.nn.gelu(values, approximate=False)  16.9 us
    ppermute x6, waiting for transfers between devices, with_halo(): lax.ppermute(head, axis, [((i + 1) % count, i) for i in range(ends)])  15.9 us
    unnamed x66, local copies, waits for them, and re-layouts  13.6 us
    all_to_all x1, starting transfers between devices, shards(): lax.all_to_all(cells_modes, 'gx', split_axis=3, concat_axis=0, tiled=True)  13.6 us
  transfers between devices with their start and end apart: 16, of which 7 were waited for; matrix products, arithmetic and copies ran while one was open for 69% of the time, Pallas kernels for 0%

commit v1 on v0

v1 whole, which is shorter than its diff:
```python
import math

import jax
import jax.numpy as jnp
import ml_dtypes
import numpy as np
from jax import lax
from jax.experimental import pallas as pl
from jax.experimental.pallas import tpu as pltpu
from jax.sharding import PartitionSpec as P

NZ = 64
KY = 32
CP = 40
LANES = 128
F32 = jnp.float32
BF16 = jnp.bfloat16


def split_table(table):
    high = table.astype(np.float32).astype(ml_dtypes.bfloat16)
    low = (table - high.astype(np.float64)).astype(np.float32).astype(ml_dtypes.bfloat16)
    return np.stack([high, low])


def split(values):
    high = values.astype(BF16)
    return high, (values - high.astype(F32)).astype(BF16)


def product(table, values, dims):
    high, low = split(values)
    numbers = (dims, ((), ()))

    def dot(left, right):
        return lax.dot_general(left, right, numbers, preferred_element_type=F32)

    return dot(table[0], high) + dot(table[0], low) + dot(table[1], high)


def frequencies(count, length):
    index = np.arange(count)
    return np.where(index < count // 2, index, length - count + index)


def tables(size_x, size_y, cells_x, cells_y, modes_x, modes_z):
    full_x, full_y = size_x * cells_x, size_y * cells_y
    scale_in = 1.0 / math.sqrt(full_x * full_y * NZ)
    scale_out = 1.0 / math.sqrt(modes_x * KY * modes_z)
    kx_local = modes_x // size_y
    z = np.arange(NZ)
    k = np.arange(modes_z)
    turn = 2.0 * np.pi * (np.outer(k, z) % NZ) / NZ
    eye_x = np.eye(cells_x)
    parts = np.stack([np.cos(turn), -np.sin(turn)], 1)
    z_in = np.einsum("kpz,xw->kpxwz", parts, eye_x).reshape(modes_z * 2 * cells_x, -1) * scale_in
    weight = np.where(k == 0, 1.0, 2.0)[:, None, None] * scale_out
    z_out = np.einsum("kpz,xw->kpxwz", parts * weight, eye_x).reshape(modes_z * 2 * cells_x, -1)

    def rotation(freq, positions, length):
        angle = 2.0 * np.pi * (np.outer(freq, positions) % length) / length
        cos, sin = np.cos(angle), np.sin(angle)
        return np.stack([np.stack([cos, -sin]), np.stack([sin, cos])])

    plus_x = rotation(frequencies(modes_x, full_x), np.arange(full_x), full_x)
    minus_x = plus_x.transpose(1, 0, 2, 3)
    x_in = minus_x.reshape(2, 2, modes_x, size_x, cells_x).transpose(2, 0, 3, 1, 4)
    x_in = x_in.reshape(modes_x * 2, -1)
    x_out = plus_x.reshape(2, 2, modes_x, size_x, cells_x).transpose(3, 0, 4, 2, 1)
    x_out = x_out.reshape(size_x * 2 * cells_x, -1)
    plus_y = rotation(frequencies(KY, full_y), np.arange(full_y), full_y)
    minus_y = plus_y.transpose(1, 0, 2, 3)
    eye_j = np.eye(kx_local)
    shape = (2, 2, KY, size_y, cells_y)
    y_in = np.einsum("pqlsy,jk->pjlyskq", minus_y.reshape(shape), eye_j)
    y_in = y_in.reshape(2 * kx_local * KY, -1)
    y_out = np.einsum("pqlsy,jk->ysjpqkl", plus_y.reshape(shape), eye_j)
    y_out = y_out.reshape(cells_y * size_y * kx_local * 2, -1)
    return [split_table(t) for t in (z_in, x_in, y_in, y_out, x_out, z_out)]


def params(vmem=16 << 20):
    return pltpu.CompilerParams(vmem_limit_bytes=vmem)


def call(body, out_shape, *args, scratch=(), flops=0, smem=()):
    space = [pl.BlockSpec(memory_space=pltpu.SMEM if i in smem else pltpu.VMEM) for i in range(len(args))]
    size = sum(a.size * a.dtype.itemsize for a in args)
    return pl.pallas_call(
        body,
        out_shape=out_shape,
        in_specs=space,
        out_specs=jax.tree.map(lambda _: pl.BlockSpec(memory_space=pltpu.VMEM), out_shape),
        scratch_shapes=list(scratch),
        compiler_params=params(),
        cost_estimate=pl.CostEstimate(flops=flops, bytes_accessed=size, transcendentals=0),
    )(*args)


def store_payload(ref, rows):
    count = ref.shape[0]
    for tile in range(3):
        width = min(LANES, rows.shape[1] - LANES * tile)
        block = rows[:, LANES * tile : LANES * tile + width]
        ref[:, 8 * tile : 8 * tile + 8, :width] = block.reshape(count, 8, width)
        if width < LANES:
            ref[:, 8 * tile : 8 * tile + 8, width:] = jnp.zeros((count, 8, LANES - width), F32)


def load_payload(ref):
    count = ref.shape[0]
    tiles = [ref[:, 8 * t : 8 * t + 8, :].reshape(count * 8, LANES) for t in range(3)]
    return jnp.concatenate(tiles, axis=1)


def z_in_body(grid_ref, table, out_ref):
    cells = grid_ref[...].reshape(-1, grid_ref.shape[2])
    store_payload(out_ref, product(table, cells, ((1,), (1,))))


def rows_body(received, table, out_ref):
    rows = product(table, load_payload(received), ((1,), (0,)))
    for tile in range(3):
        block = rows[:, LANES * tile : LANES * tile + LANES]
        out_ref[:, 8 * tile : 8 * tile + 8, :] = block.reshape(out_ref.shape[0], 8, LANES)


def mix_body(received, weights, kept, place, y_in, y_out, out_ref, stacked, s_re, s_im):
    cells_y = received.shape[0]
    rows = load_payload(received)
    block = rows.shape[0]
    for y in range(cells_y):
        stacked[y * block : (y + 1) * block, :CP] = rows[:, CP * y : CP * y + CP]
        stacked[y * block : (y + 1) * block, CP:] = jnp.zeros((block, LANES - CP), F32)
    modes = product(y_in, stacked[...], ((1,), (0,)))
    count = modes.shape[0] // 2
    s_re[...] = modes[:count].T
    s_im[...] = modes[count:].T
    channels = 36
    pair = 2 * channels
    row = lax.broadcasted_iota(jnp.int32, (8, count), 0)

    def spread(ref, c):
        first = jnp.broadcast_to(ref[c : c + 1, :], (8, count))
        second = jnp.broadcast_to(ref[c + 1 : c + 2, :], (8, count))
        middle = jnp.where(row < 4, first, second)
        return jnp.concatenate([first] * 4 + [middle] + [second] * 4, axis=0)

    total_re = jnp.zeros((pair, count), F32)
    total_im = jnp.zeros((pair, count), F32)
    for c in range(0, channels, 2):
        w_re = weights[0, channels * c : channels * c + pair, :]
        w_im = weights[1, channels * c : channels * c + pair, :]
        f_re, f_im = spread(s_re, c), spread(s_im, c)
        total_re += w_re * f_re - w_im * f_im
        total_im += w_re * f_im + w_im * f_re
    keep = place[0] < kept[...]

    def fold(total):
        total = total[:channels] + total[channels:]
        return jnp.concatenate([jnp.where(keep, total, 0.0), jnp.zeros((CP - channels, count), F32)], axis=0)

    mixed = jnp.concatenate([fold(total_re), fold(total_im)], axis=1)
    back = product(y_out, mixed, ((1,), (1,)))
    lanes = jnp.concatenate([back[y * block : (y + 1) * block] for y in range(cells_y)], axis=1)
    store_payload(out_ref, lanes)


def gelu_exact(values):
    return 0.5 * values * (1.0 + lax.erf(values * math.sqrt(0.5)))


ROW = 368


def taps_body(kernels, out_ref, scratch):
    channels = kernels.shape[2]
    for r in range(3):
        scratch[...] = jnp.zeros(scratch.shape, F32)
        for tap in range(27):
            row, lane = CP * (tap % 3), CP * (tap // 3)
            scratch[row : row + channels, lane : lane + channels] = kernels[r, tap]
        high, low = split(scratch[...].T[:ROW])
        out_ref[r, :ROW, :128] = high
        out_ref[r, :ROW, 128:] = high
        out_ref[r, ROW:, :128] = low
        out_ref[r, ROW:, 128:] = jnp.zeros((ROW, 128), BF16)


def convolve_rows(load_row, rows_in, width, taps, refs, finish):
    stack_a, stack_b, first_sum, second_sum, whole = refs
    z_position = lax.broadcasted_iota(jnp.int32, (CP, LANES), 1) % NZ
    has_lower = z_position >= 1
    has_upper = z_position <= NZ - 2
    low_half = lax.broadcasted_iota(jnp.int32, (CP, LANES), 1) < NZ
    tiles = width // LANES

    def prepare(index, stack):
        cells = load_row(index)
        for t in range(tiles):
            piece = cells[:, LANES * t : LANES * t + LANES]
            lower = jnp.where(has_lower, pltpu.roll(piece, 1, 1), 0.0)
            upper = jnp.where(has_upper, pltpu.roll(piece, LANES - 1, 1), 0.0)
            rows = jnp.concatenate([lower, piece, upper, jnp.zeros((8, LANES), F32)], axis=0)
            high, low = split(rows)
            stack[:128, LANES * t : LANES * t + LANES] = high
            stack[128:, LANES * t : LANES * t + LANES] = low

    def emit(row):
        sums = [[whole[CP * a : CP * a + CP, LANES * t : LANES * t + LANES] for t in range(tiles)] for a in range(3)]
        out = []
        for t in range(tiles):
            low_part = sums[0][t]
            if t + 1 < tiles:
                low_part = low_part + sums[2][t + 1]
            high_part = sums[2][t]
            if t > 0:
                high_part = high_part + sums[0][t - 1]
            turned = pltpu.roll(jnp.where(low_half, low_part, high_part), NZ, 1)
            out.append(sums[1][t] + turned)
        finish(row, out)

    def step(index, here, there):
        prepare(jnp.minimum(index + 1, rows_in - 1), there)
        emit(jnp.maximum(index - 3, 0))
        for t in range(tiles // 2):
            lanes = slice(2 * LANES * t, 2 * LANES * t + 2 * LANES)
            terms = lax.dot_general(
                taps[...], here[:, lanes], (((1,), (0,)), ((), ())), preferred_element_type=F32
            )
            for a in range(3):
                rows = slice(CP * a, CP * a + CP)
                piece = []
                for b in range(3):
                    first = CP * (3 * a + b)
                    piece.append(terms[first : first + CP] + terms[ROW + first : ROW + first + CP])
                whole[rows, lanes] = second_sum[rows, lanes] + piece[2]
                second_sum[rows, lanes] = first_sum[rows, lanes] + piece[1]
                first_sum[rows, lanes] = piece[0]

    def pair(j, carry):
        step(2 * j, stack_a, stack_b)
        step(2 * j + 1, stack_b, stack_a)
        return carry

    prepare(0, stack_a)
    lax.fori_loop(0, rows_in // 2, pair, 0)
    emit(rows_in - 3)


def conv_scratch(width):
    return [pltpu.VMEM((256, width), BF16)] * 2 + [pltpu.VMEM((3 * CP, width), F32)] * 3


def inside(place, first_x, first_y, sizes, width):
    cells_x, cells_y, full_x, full_y = sizes
    x = place[0] * cells_x + first_x + lax.broadcasted_iota(jnp.int32, (CP, width), 1) // NZ
    in_x = (x >= 0) & (x < full_x)

    def at(row):
        y = place[1] * cells_y + first_y + row
        return in_x & ((y >= 0) & (y < full_y))

    return at


def first_body(sizes, wide, before, after, place, taps, out_ref, rows, *refs):
    cells_y = wide.shape[0]
    rows[0:3] = before[...]
    rows[3 : 3 + cells_y] = wide[...]
    rows[3 + cells_y :] = after[...]
    keep = inside(place, -2, -2, sizes, 512)

    def finish(row, tiles):
        values = jnp.concatenate(tiles[1:5], axis=1)
        out_ref[row] = jnp.where(keep(row), gelu_exact(values), 0.0)

    convolve_rows(lambda i: rows[i], cells_y + 6, 768, taps, refs, finish)


def second_body(sizes, cells, place, taps, out_ref, *refs):
    keep = inside(place, -2, -1, sizes, 512)

    def finish(row, tiles):
        values = jnp.concatenate(tiles, axis=1)
        out_ref[row] = jnp.where(keep(row), gelu_exact(values), 0.0)

    convolve_rows(lambda i: cells[i], cells.shape[0], 512, taps, refs, finish)


def third_body(cells, taps, out_ref, *refs):
    def finish(row, tiles):
        out_ref[row] = jnp.concatenate(tiles[1:3], axis=1)

    convolve_rows(lambda i: cells[i], cells.shape[0], 512, taps, refs, finish)


def last_body(received, third, table, out_ref):
    spectrum = load_payload(received)[:, : third.shape[0] * CP]
    high, low = split(spectrum)

    def dot(left, right):
        return lax.dot_general(left, right, (((0,), (0,)), ((), ())), preferred_element_type=F32)

    spectral = dot(high, table[0]) + dot(low, table[0]) + dot(high, table[1])
    out_ref[...] = gelu_exact(spectral.reshape(third.shape) + third[...])


def shift(values, axis, step):
    count = lax.axis_size(axis)
    pairs = [(i, i + step) for i in range(count) if 0 <= i + step < count]
    return lax.ppermute(values, axis, pairs)


def shards(field, mix_weights, kept_z, conv_kernels):
    channels = field.shape[0]
    cells_x = field.shape[1]
    cells_y = field.shape[2] // NZ
    size_x = lax.axis_size("gx")
    size_y = lax.axis_size("gy")
    full_x, full_y = cells_x * size_x, cells_y * size_y
    modes_z = mix_weights.shape[3] * size_x
    kx_local = mix_weights.shape[4] // KY
    modes_x = kx_local * size_y
    place = jnp.stack([lax.axis_index("gx"), lax.axis_index("gy")]).astype(jnp.int32)
    z_in, x_in, y_in, y_out, x_out, z_out = [
        jnp.asarray(t) for t in tables(size_x, size_y, cells_x, cells_y, modes_x, modes_z)
    ]

    grid = field.reshape(channels, cells_x, cells_y, NZ).transpose(2, 0, 1, 3)
    grid = jnp.pad(grid.reshape(cells_y, channels, cells_x * NZ), ((0, 0), (0, CP - channels), (0, 0)))

    from_left = shift(grid, "gx", 1)
    from_right = shift(grid, "gx", -1)
    sent = call(z_in_body, jax.ShapeDtypeStruct((size_x, 24, LANES), F32), grid, z_in)
    taps = call(
        taps_body, jax.ShapeDtypeStruct((3, 2 * ROW, 256), BF16), conv_kernels,
        scratch=[pltpu.VMEM((128, 384), F32)],
    )
    received = lax.all_to_all(sent, "gx", 0, 0, tiled=True)
    wide = jnp.concatenate([from_left, grid, from_right], axis=2)
    before = shift(wide[cells_y - 3 :], "gy", 1)
    after = shift(wide[:3], "gy", -1)
    sent = call(rows_body, jax.ShapeDtypeStruct((size_y, 24, LANES), F32), received, x_in)

    sizes = (cells_x, cells_y, full_x, full_y)
    wide, sent = lax.optimization_barrier((wide, sent))
    received = lax.all_to_all(sent, "gy", 0, 0, tiled=True)
    first = call(
        lambda *refs: first_body(sizes, *refs),
        jax.ShapeDtypeStruct((cells_y + 4, CP, 512), F32),
        wide, before, after, place, taps[0],
        scratch=[pltpu.VMEM((cells_y + 6, CP, 768), F32)] + conv_scratch(768),
        smem=(3,), flops=6 << 30,
    )
    first, received = lax.optimization_barrier((first, received))
    weights = mix_weights.reshape(2, channels * channels, kx_local * KY)
    sent = call(
        mix_body,
        jax.ShapeDtypeStruct((size_y, 24, LANES), F32),
        received, weights, kept_z.reshape(1, -1), place, y_in, y_out,
        scratch=[pltpu.VMEM((cells_y * size_y * kx_local * 2, LANES), F32)]
        + [pltpu.VMEM((LANES, kx_local * KY), F32)] * 2,
        smem=(3,),
    )
    first, sent = lax.optimization_barrier((first, sent))
    received = lax.all_to_all(sent, "gy", 0, 0, tiled=True)
    second = call(
        lambda *refs: second_body(sizes, *refs),
        jax.ShapeDtypeStruct((cells_y + 2, CP, 512), F32),
        first, place, taps[1], scratch=conv_scratch(512), smem=(1,), flops=4 << 30,
    )
    second, received = lax.optimization_barrier((second, received))
    sent = call(rows_body, jax.ShapeDtypeStruct((size_x, 24, LANES), F32), received, x_out)
    second, sent = lax.optimization_barrier((second, sent))
    received = lax.all_to_all(sent, "gx", 0, 0, tiled=True)
    third = call(
        third_body,
        jax.ShapeDtypeStruct((cells_y, CP, cells_x * NZ), F32),
        second, taps[2], scratch=conv_scratch(512), flops=3 << 30,
    )
    out = call(last_body, jax.ShapeDtypeStruct(third.shape, F32), received, third, z_out)
    out = out[:, :channels].reshape(cells_y, channels, cells_x, NZ).transpose(1, 2, 0, 3)
    return out.reshape(channels, cells_x, cells_y * NZ)


def solution(mesh):
    placed = (P(None, "gx", "gy"), P(None, None, None, "gx", "gy"), P("gy"), P())
    return jax.shard_map(
        shards, mesh=mesh, in_specs=placed, out_specs=P(None, "gx", "gy"), check_vma=False
    )
```

time: 477 us -> 90.7 us (0.19); the launches traced: 467 us -> 89 us
  local copies, waits for them, and re-layouts: 278 us -> 11 us
  matrix products: 71.5 us -> 0 us
  other arithmetic: 29.6 us -> 1.22 us
  starting transfers between devices: 69 us -> 42.3 us
  Pallas kernels: 0 us -> 20.1 us
    squeeze x81 -> x1, local copies, waits for them, and re-layouts: 126 us -> 1.03 us  [shards(): taps[2]]
    slice x98 -> x2, local copies, waits for them, and re-layouts: 120 us -> 0.15 us  [the longest x1 0.1 us: shards(): out[:, :channels].reshape(cells_y, channels, cells_x, NZ)]
    dot_general x33 -> x0, matrix products: 71.5 us -> none  [contract(): return jnp.einsum(form, left, right, precision=precise)]
    pallas_call x0 -> x9, Pallas kernels: none -> 20.1 us  [call(): pl.pallas_call(body, out_shape=out_shape, in_specs=space, out_specs=jax.t...]
    ppermute x12 -> x4, starting transfers between devices: 32.8 us -> 13.4 us  [shift(): return lax.ppermute(values, axis, pairs)]
    mul x5 -> x0, other arithmetic: 17.5 us -> none  [the longest x3 16.9 us: gelu_exact(): return jax.nn.gelu(values, approximate=False)]
    ppermute x12 -> x4, waiting for transfers between devices: 17.4 us -> 0.01 us  [shift(): return lax.ppermute(values, axis, pairs)]
    all_to_all x4, waiting for transfers between devices: 0.79 us -> 14.1 us  [the longest x2 14.1 us: shards(): received = lax.all_to_all(sent, 'gx', 0, 0, tiled=True)]
  transfers between devices with their start and end apart: 16 -> 8, of which waited for: 7 -> 2; matrix products, arithmetic and copies ran while one was open for 69% -> 3% of each run, Pallas kernels for 0% -> 18%
where the time goes in v1:
time: 90.7 us; the launch traced here: 89 us
  starting transfers between devices  42.3 us (47%)
  Pallas kernels  20.1 us (22%)
  waiting for transfers between devices  14.1 us (16%)
  local copies, waits for them, and re-layouts  11 us (12%)
  other arithmetic  1.22 us (1%)
    pallas_call x9, Pallas kernels, call(): pl.pallas_call(body, out_shape=out_shape, in_specs=space, out_specs=jax.t...  20.1 us
    all_to_all x2, starting transfers between devices, shards(): received = lax.all_to_all(sent, 'gx', 0, 0, tiled=True)  16.4 us
    all_to_all x2, waiting for transfers between devices, shards(): received = lax.all_to_all(sent, 'gx', 0, 0, tiled=True)  14.1 us
    ppermute x4, starting transfers between devices, shift(): return lax.ppermute(values, axis, pairs)  13.4 us
    all_to_all x2, starting transfers between devices, shards(): received = lax.all_to_all(sent, 'gy', 0, 0, tiled=True)  12.6 us
    unnamed x36, local copies, waits for them, and re-layouts  6.73 us
  transfers between devices with their start and end apart: 8, of which 2 were waited for; matrix products, arithmetic and copies ran while one was open for 3% of the time, Pallas kernels for 18%

profile of v1, /device:TPU:1, one launch (start us, length us, event | category | flops | bytes accessed | tf_op | source)
XLA Modules:
  0.0 89.0 jit_solution(1199286398239337455)
XLA Ops:
  0.0 1.2 %reshape.18 = f32[36,4,8,64]{3,2,1,0:T(8,128)S(1)} reshape(f32[36,4,512]{2,1,0:T(4,128)} %param.10) | data formatting | bytes 589824 | tf_op jit(solution)/shard_map/reshape | solution.py:330
  1.9 1.4 %collective-permute-start.1 = (f32[8,40,256]{2,1,0:T(8,128)S(1)}, f32[8,40,256]{2,1,0:T(8,128)}, u32[]{:S(2)}, u32[]{:S(2)}) collective-permute-start(f32[8,40,256]{2,1,0:T(8,128)S(1)} %pad.4.grid_ref), channel_id=1, source_target_pairs={{8,0},{16,8},{24,16},{32,24},{40,32},{48,40},{56,48},{64,56},{72,6... | collective-permute-start | bytes 983048 | tf_op jit(solution)/shard_map/ppermute | solution.py:312
  3.3 5.3 %collective-permute-start = (f32[8,40,256]{2,1,0:T(8,128)S(1)}, f32[8,40,256]{2,1,0:T(8,128)}, u32[]{:S(2)}, u32[]{:S(2)}) collective-permute-start(f32[8,40,256]{2,1,0:T(8,128)S(1)} %pad.4.grid_ref), channel_id=1, source_target_pairs={{0,8},{8,16},{16,24},{24,32},{32,40},{40,48},{48,56},{56,64},{64,7... | collective-permute-start | bytes 983048 | tf_op jit(solution)/shard_map/ppermute | solution.py:312
  8.6 1.1 %shard_map.100 = f32[32,24,128]{2,1,0:T(8,128)} custom-call(f32[8,40,256]{2,1,0:T(8,128)S(1)} %pad.4.grid_ref, bf16[2,256,256]{2,1,0:T(8,128)(2,1)S(1)} %copy-done.8), custom_call_target="tpu_custom_call" | custom-call | bytes 589824 | tf_op jit(solution)/shard_map/pallas_call | solution.py:89
  9.7 12.4 %all-to-all-start = ((f32[32,24,128]{2,1,0:T(8,128)}), f32[32,24,128]{2,1,0:T(8,128)S(1)}, u32[]{:S(2)}, u32[]{:S(2)}) async-start(f32[32,24,128]{2,1,0:T(8,128)} %shard_map.100), calls=%async_computation | async-start | bytes 786432 | tf_op jit(solution)/shard_map/all_to_all | solution.py:340
  22.9 1.1 %pad_maximum_fusion.refs_0_ = f32[8,40,768]{2,1,0:T(8,128)S(1)} fusion(f32[8,40,256]{2,1,0:T(8,128)} %collective-permute-done.1, f32[8,40,256]{2,1,0:T(8,128)S(1)} %pad.4.grid_ref, f32[8,40,256]{2,1,0:T(8,128)} %collective-permute-done), kind=kLoop, calls=%fused_computation | loop fusion | flops 491520 | bytes 1966080 | tf_op jit(solution)/shard_map/concatenate | solution.py:341
  24.1 3.6 %collective-permute-start.3 = (f32[3,40,768]{2,1,0:T(8,128)S(1)}, f32[3,40,768]{2,1,0:T(8,128)S(1)}, u32[]{:S(2)}, u32[]{:S(2)}) collective-permute-start(f32[3,40,768]{2,1,0:T(8,128)S(1)} %get-tuple-element.28), channel_id=1, source_target_pairs={{1,0},{2,1},{3,2},{4,3},{5,4},{6,5},{7,6},{9,8},{10,9},{11,10},{12... | collective-permute-start | bytes 1105928 | tf_op jit(solution)/shard_map/ppermute | solution.py:312
  27.7 3.1 %collective-permute-start.2 = (f32[3,40,768]{2,1,0:T(8,128)S(1)}, f32[3,40,768]{2,1,0:T(8,128)S(1)}, u32[]{:S(2)}, u32[]{:S(2)}) collective-permute-start(f32[3,40,768]{2,1,0:T(8,128)S(1)} %get-tuple-element.29), channel_id=1, source_target_pairs={{0,1},{1,2},{2,3},{3,4},{4,5},{5,6},{6,7},{8,9},{9,10},{10,11},{11... | collective-permute-start | bytes 1105928 | tf_op jit(solution)/shard_map/ppermute | solution.py:312
  30.9 1.0 %slice_bitcast_fusion = (bf16[736,256]{1,0:T(8,128)(2,1)}, bf16[736,256]{1,0:T(8,128)(2,1)}, bf16[736,256]{1,0:T(8,128)(2,1)}) fusion(bf16[3,736,256]{2,1,0:T(8,128)(2,1)S(1)} %shard_map.102), kind=kLoop, calls=%fused_computation.2 | loop fusion | bytes 2260992 | tf_op jit(solution)/shard_map/squeeze | solution.py:380
  31.9 3.3 %all-to-all-done.received = f32[32,24,128]{2,1,0:T(8,128)S(1)} async-done(((f32[32,24,128]{2,1,0:T(8,128)}), f32[32,24,128]{2,1,0:T(8,128)S(1)}, u32[]{:S(2)}, u32[]{:S(2)}) %all-to-all-start) | async-done | bytes 393248 | tf_op jit(solution)/shard_map/all_to_all | solution.py:340
  36.1 7.7 %all-to-all-start.1 = ((f32[8,24,128]{2,1,0:T(8,128)}), f32[8,24,128]{2,1,0:T(8,128)S(1)}, u32[]{:S(2)}, u32[]{:S(2)}) async-start(f32[8,24,128]{2,1,0:T(8,128)} %shard_map.101), calls=%async_computation.1 | async-start | bytes 196608 | tf_op jit(solution)/shard_map/all_to_all | solution.py:348
  45.4 1.0 %copy-done.6 = bf16[736,256]{1,0:T(8,128)(2,1)S(1)} copy-done((bf16[736,256]{1,0:T(8,128)(2,1)S(1)}, bf16[736,256]{1,0:T(8,128)(2,1)}, u32[]{:S(2)}) %copy-start.6) | copy-done | bytes 376856
  46.4 1.0 %copy-done.13 = f32[3,40,768]{2,1,0:T(8,128)S(1)} copy-done((f32[3,40,768]{2,1,0:T(8,128)S(1)}, f32[3,40,768]{2,1,0:T(8,128)}, u32[]{:S(2)}) %copy-start.13) | copy-done | bytes 368664
  47.3 1.0 %copy-done.15 = f32[3,40,768]{2,1,0:T(8,128)S(1)} copy-done((f32[3,40,768]{2,1,0:T(8,128)S(1)}, f32[3,40,768]{2,1,0:T(8,128)}, u32[]{:S(2)}) %copy-start.15) | copy-done | bytes 368664
  48.3 6.2 %shard_map.103.refs_0_ = f32[12,40,512]{2,1,0:T(8,128)S(1)} custom-call(f32[8,40,768]{2,1,0:T(8,128)S(1)} %pad_maximum_fusion.refs_0_, f32[3,40,768]{2,1,0:T(8,128)S(1)} %copy-done.15, f32[3,40,768]{2,1,0:T(8,128)S(1)} %copy-done.13, s32[2]{0:T(128)S(1)} %pad_add_fusion.refs_3_.place.refs_1_, bf16[736,256]{1,0:T(8,128)(2,1)S(1)} %copy-done.6), custom_call_target="tpu_custom_call" | custom-call | flops 6442450944 | bytes 2097160 | tf_op jit(solution)/shard_map/pallas_call | solution.py:89
  54.6 1.0 %copy-done.16 = f32[12,40,512]{2,1,0:T(8,128)} copy-done((f32[12,40,512]{2,1,0:T(8,128)}, f32[12,40,512]{2,1,0:T(8,128)S(1)}, u32[]{:S(2)}) %copy-start.16) | copy-done | bytes 983064
  55.6 2.5 %shard_map.104 = f32[8,24,128]{2,1,0:T(8,128)} custom-call(f32[8,24,128]{2,1,0:T(8,128)S(1)} %all-to-all-done.1.received, f32[2,1296,128]{2,1,0:T(8,128)S(1)} %bitcast.21, s32[1,128]{1,0:T(1,128)S(1)} %bitcast.23, s32[2]{0:T(128)S(1)} %pad_add_fusion.refs_3_.place.refs_1_, bf16[2,256,512]{2,1,0:T(8,128)(2,1)S(1)} %copy-done.3, bf16[2,512,256]{2,1,0:T(8,128)(2,1)S(1)} %copy-done.2), custom_call_target="tpu_custom_call" | custom-call | bytes 2474504 | tf_op jit(solution)/shard_map/pallas_call | solution.py:89
  58.1 4.8 %all-to-all-start.2 = ((f32[8,24,128]{2,1,0:T(8,128)}), f32[8,24,128]{2,1,0:T(8,128)S(1)}, u32[]{:S(2)}, u32[]{:S(2)}) async-start(f32[8,24,128]{2,1,0:T(8,128)} %shard_map.104), calls=%async_computation.2 | async-start | bytes 196608 | tf_op jit(solution)/shard_map/all_to_all | solution.py:367
  62.9 1.2 %copy-done.17 = f32[12,40,512]{2,1,0:T(8,128)S(1)} copy-done((f32[12,40,512]{2,1,0:T(8,128)S(1)}, f32[12,40,512]{2,1,0:T(8,128)}, u32[]{:S(2)}) %copy-start.17) | copy-done | bytes 983064
  64.1 4.2 %shard_map.105.cells = f32[10,40,512]{2,1,0:T(8,128)S(1)} custom-call(f32[12,40,512]{2,1,0:T(8,128)S(1)} %copy-done.17, s32[2]{0:T(128)S(1)} %pad_add_fusion.refs_3_.place.refs_1_, bf16[736,256]{1,0:T(8,128)(2,1)S(1)} %copy-done.5), custom_call_target="tpu_custom_call" | custom-call | flops 4294967296 | bytes 1359880 | tf_op jit(solution)/shard_map/pallas_call | solution.py:89
  68.3 1.1 %shard_map.106 = f32[32,24,128]{2,1,0:T(8,128)} custom-call(f32[8,24,128]{2,1,0:T(8,128)S(1)} %all-to-all-done.2.received, bf16[2,256,64]{2,1,0:T(8,128)(2,1)S(1)} %copy-done.9), custom_call_target="tpu_custom_call" | custom-call | bytes 163840 | tf_op jit(solution)/shard_map/pallas_call | solution.py:89
  69.4 4.0 %all-to-all-start.3 = ((f32[32,24,128]{2,1,0:T(8,128)}), f32[32,24,128]{2,1,0:T(8,128)S(1)}, u32[]{:S(2)}, u32[]{:S(2)}) async-start(f32[32,24,128]{2,1,0:T(8,128)} %shard_map.106), calls=%async_computation.3 | async-start | bytes 786432 | tf_op jit(solution)/shard_map/all_to_all | solution.py:376
  73.4 3.1 %shard_map.107.third = f32[8,40,256]{2,1,0:T(8,128)S(1)} custom-call(f32[10,40,512]{2,1,0:T(8,128)S(1)} %shard_map.105.cells, bf16[736,256]{1,0:T(8,128)(2,1)S(1)} %copy-done.4), custom_call_target="tpu_custom_call" | custom-call | flops 3221225472 | bytes 1196032 | tf_op jit(solution)/shard_map/pallas_call | solution.py:89
  76.4 10.8 %all-to-all-done.3.received = f32[32,24,128]{2,1,0:T(8,128)S(1)} async-done(((f32[32,24,128]{2,1,0:T(8,128)}), f32[32,24,128]{2,1,0:T(8,128)S(1)}, u32[]{:S(2)}, u32[]{:S(2)}) %all-to-all-start.3) | async-done | bytes 393248 | tf_op jit(solution)/shard_map/all_to_all | solution.py:376
  (50 shorter events, 5.6 us)
Async XLA Ops:
  1.4 7.3 %copy-start.8 = (bf16[2,256,256]{2,1,0:T(8,128)(2,1)S(1)}, bf16[2,256,256]{2,1,0:T(8,128)(2,1)}, u32[]{:S(2)}) copy-start(bf16[2,256,256]{2,1,0:T(8,128)(2,1)} %constant.24.clone.table) | copy-start | bytes 786436
  1.8 20.3 %copy-start = (f32[3,27,36,36]{3,2,1,0:T(8,128)S(1)}, f32[3,27,36,36]{3,2,1,0:T(8,128)}, u32[]{:S(2)}) copy-start(f32[3,27,36,36]{3,2,1,0:T(8,128)} %kernels.1) | copy-start | bytes 1259716
  1.9 21.0 %collective-permute-start.1 = (f32[8,40,256]{2,1,0:T(8,128)S(1)}, f32[8,40,256]{2,1,0:T(8,128)}, u32[]{:S(2)}, u32[]{:S(2)}) collective-permute-start(f32[8,40,256]{2,1,0:T(8,128)S(1)} %pad.4.grid_ref), channel_id=1, source_target_pairs={{8,0},{16,8},{24,16},{32,24},{40,32},{48,40},{56,48},{64,56},{72,6... | collective-permute-start | bytes 983048 | tf_op jit(solution)/shard_map/ppermute | solution.py:312
  3.3 19.6 %collective-permute-start = (f32[8,40,256]{2,1,0:T(8,128)S(1)}, f32[8,40,256]{2,1,0:T(8,128)}, u32[]{:S(2)}, u32[]{:S(2)}) collective-permute-start(f32[8,40,256]{2,1,0:T(8,128)S(1)} %pad.4.grid_ref), channel_id=1, source_target_pairs={{0,8},{8,16},{16,24},{24,32},{32,40},{40,48},{48,56},{56,64},{64,7... | collective-permute-start | bytes 983048 | tf_op jit(solution)/shard_map/ppermute | solution.py:312
  9.7 25.5 %all-to-all-start = ((f32[32,24,128]{2,1,0:T(8,128)}), f32[32,24,128]{2,1,0:T(8,128)S(1)}, u32[]{:S(2)}, u32[]{:S(2)}) async-start(f32[32,24,128]{2,1,0:T(8,128)} %shard_map.100), calls=%async_computation | async-start | bytes 786432 | tf_op jit(solution)/shard_map/all_to_all | solution.py:340
  24.1 11.1 %copy-start.10 = (bf16[2,64,256]{2,1,0:T(8,128)(2,1)S(1)}, bf16[2,64,256]{2,1,0:T(8,128)(2,1)}, u32[]{:S(2)}) copy-start(bf16[2,64,256]{2,1,0:T(8,128)(2,1)} %constant.25.clone.table) | copy-start | bytes 196612
  24.1 19.7 %collective-permute-start.3 = (f32[3,40,768]{2,1,0:T(8,128)S(1)}, f32[3,40,768]{2,1,0:T(8,128)S(1)}, u32[]{:S(2)}, u32[]{:S(2)}) collective-permute-start(f32[3,40,768]{2,1,0:T(8,128)S(1)} %get-tuple-element.28), channel_id=1, source_target_pairs={{1,0},{2,1},{3,2},{4,3},{5,4},{6,5},{7,6},{9,8},{10,9},{11,10},{12... | collective-permute-start | bytes 1105928 | tf_op jit(solution)/shard_map/ppermute | solution.py:312
  27.7 16.9 %collective-permute-start.2 = (f32[3,40,768]{2,1,0:T(8,128)S(1)}, f32[3,40,768]{2,1,0:T(8,128)S(1)}, u32[]{:S(2)}, u32[]{:S(2)}) collective-permute-start(f32[3,40,768]{2,1,0:T(8,128)S(1)} %get-tuple-element.29), channel_id=1, source_target_pairs={{0,1},{1,2},{2,3},{3,4},{4,5},{5,6},{6,7},{8,9},{9,10},{10,11},{11... | collective-permute-start | bytes 1105928 | tf_op jit(solution)/shard_map/ppermute | solution.py:312
  36.1 19.5 %all-to-all-start.1 = ((f32[8,24,128]{2,1,0:T(8,128)}), f32[8,24,128]{2,1,0:T(8,128)S(1)}, u32[]{:S(2)}, u32[]{:S(2)}) async-start(f32[8,24,128]{2,1,0:T(8,128)} %shard_map.101), calls=%async_computation.1 | async-start | bytes 196608 | tf_op jit(solution)/shard_map/all_to_all | solution.py:348
  45.4 1.0 %copy-start.6 = (bf16[736,256]{1,0:T(8,128)(2,1)S(1)}, bf16[736,256]{1,0:T(8,128)(2,1)}, u32[]{:S(2)}) copy-start(bf16[736,256]{1,0:T(8,128)(2,1)} %get-tuple-element.27.refs_4_) | copy-start | bytes 1130500
  46.4 1.0 %copy-start.13 = (f32[3,40,768]{2,1,0:T(8,128)S(1)}, f32[3,40,768]{2,1,0:T(8,128)}, u32[]{:S(2)}) copy-start(f32[3,40,768]{2,1,0:T(8,128)} %copy-done.12) | copy-start | bytes 1105924
  47.3 1.0 %copy-start.15 = (f32[3,40,768]{2,1,0:T(8,128)S(1)}, f32[3,40,768]{2,1,0:T(8,128)}, u32[]{:S(2)}) copy-start(f32[3,40,768]{2,1,0:T(8,128)} %copy-done.14) | copy-start | bytes 1105924
  48.3 7.3 %copy-start.1 = (f32[2,36,36,1,128]{4,3,2,1,0:T(1,128)S(1)}, f32[2,36,36,1,128]{4,3,2,1,0:T(1,128)}, u32[]{:S(2)}) copy-start(f32[2,36,36,1,128]{4,3,2,1,0:T(1,128)} %param.11) | copy-start | bytes 3981316
  48.3 7.3 %copy-start.2 = (bf16[2,512,256]{2,1,0:T(8,128)(2,1)S(1)}, bf16[2,512,256]{2,1,0:T(8,128)(2,1)}, u32[]{:S(2)}) copy-start(bf16[2,512,256]{2,1,0:T(8,128)(2,1)} %constant.27.clone.y_out) | copy-start | bytes 1572868
  48.3 7.3 %copy-start.3 = (bf16[2,256,512]{2,1,0:T(8,128)(2,1)S(1)}, bf16[2,256,512]{2,1,0:T(8,128)(2,1)}, u32[]{:S(2)}) copy-start(bf16[2,256,512]{2,1,0:T(8,128)(2,1)} %constant.26.clone.y_in) | copy-start | bytes 1572868
  48.3 7.3 %copy-start.11 = (s32[128]{0:T(128)S(1)}, s32[128]{0:T(128)}, u32[]{:S(2)}) copy-start(s32[128]{0:T(128)} %param.12) | copy-start | bytes 1540
  54.6 1.0 %copy-start.16 = (f32[12,40,512]{2,1,0:T(8,128)}, f32[12,40,512]{2,1,0:T(8,128)S(1)}, u32[]{:S(2)}) copy-start(f32[12,40,512]{2,1,0:T(8,128)S(1)} %shard_map.103.refs_0_) | copy-start | bytes 2949124
  55.6 7.3 %copy-start.5 = (bf16[736,256]{1,0:T(8,128)(2,1)S(1)}, bf16[736,256]{1,0:T(8,128)(2,1)}, u32[]{:S(2)}) copy-start(bf16[736,256]{1,0:T(8,128)(2,1)} %get-tuple-element.26.refs_2_) | copy-start | bytes 1130500
  58.1 10.2 %all-to-all-start.2 = ((f32[8,24,128]{2,1,0:T(8,128)}), f32[8,24,128]{2,1,0:T(8,128)S(1)}, u32[]{:S(2)}, u32[]{:S(2)}) async-start(f32[8,24,128]{2,1,0:T(8,128)} %shard_map.104), calls=%async_computation.2 | async-start | bytes 196608 | tf_op jit(solution)/shard_map/all_to_all | solution.py:367
  62.9 1.2 %copy-start.17 = (f32[12,40,512]{2,1,0:T(8,128)S(1)}, f32[12,40,512]{2,1,0:T(8,128)}, u32[]{:S(2)}) copy-start(f32[12,40,512]{2,1,0:T(8,128)} %copy-done.16) | copy-start | bytes 2949124
  64.1 4.2 %copy-start.9 = (bf16[2,256,64]{2,1,0:T(8,128)(2,1)S(1)}, bf16[2,256,64]{2,1,0:T(8,128)(2,1)}, u32[]{:S(2)}) copy-start(bf16[2,256,64]{2,1,0:T(8,128)(2,1)} %constant.28.clone.table) | copy-start | bytes 196612
  68.3 5.1 %copy-start.4 = (bf16[736,256]{1,0:T(8,128)(2,1)S(1)}, bf16[736,256]{1,0:T(8,128)(2,1)}, u32[]{:S(2)}) copy-start(bf16[736,256]{1,0:T(8,128)(2,1)} %get-tuple-element.25.taps) | copy-start | bytes 1130500
  69.4 17.8 %all-to-all-start.3 = ((f32[32,24,128]{2,1,0:T(8,128)}), f32[32,24,128]{2,1,0:T(8,128)S(1)}, u32[]{:S(2)}, u32[]{:S(2)}) async-start(f32[32,24,128]{2,1,0:T(8,128)} %shard_map.106), calls=%async_computation.3 | async-start | bytes 786432 | tf_op jit(solution)/shard_map/all_to_all | solution.py:376
  73.4 13.9 %copy-start.7 = (bf16[2,256,256]{2,1,0:T(8,128)(2,1)S(1)}, bf16[2,256,256]{2,1,0:T(8,128)(2,1)}, u32[]{:S(2)}) copy-start(bf16[2,256,256]{2,1,0:T(8,128)(2,1)} %constant.29.clone.table) | copy-start | bytes 786436
  (2 other events, 1.5 us)

commit v2 on v1

--- a/solution.py
+++ b/solution.py
@@ -79,22 +79,34 @@
     return [split_table(t) for t in (z_in, x_in, y_in, y_out, x_out, z_out)]
 
 
-def params(vmem=16 << 20):
-    return pltpu.CompilerParams(vmem_limit_bytes=vmem)
-
-
-def call(body, out_shape, *args, scratch=(), flops=0, smem=()):
-    space = [pl.BlockSpec(memory_space=pltpu.SMEM if i in smem else pltpu.VMEM) for i in range(len(args))]
+def call(body, out_shape, *args, scratch=(), flops=0, smem=(), hbm=(), out_hbm=(), vmem=24):
+    def spec(index, kept):
+        return pl.BlockSpec(memory_space=pl.ANY if index in kept else pltpu.VMEM)
+
+    in_specs = [pl.BlockSpec(memory_space=pltpu.SMEM) if i in smem else spec(i, hbm) for i in range(len(args))]
     size = sum(a.size * a.dtype.itemsize for a in args)
+    many = isinstance(out_shape, tuple)
     return pl.pallas_call(
         body,
         out_shape=out_shape,
-        in_specs=space,
-        out_specs=jax.tree.map(lambda _: pl.BlockSpec(memory_space=pltpu.VMEM), out_shape),
+        in_specs=in_specs,
+        out_specs=tuple(spec(i, out_hbm) for i in range(len(out_shape))) if many else spec(0, out_hbm),
         scratch_shapes=list(scratch),
-        compiler_params=params(),
+        compiler_params=pltpu.CompilerParams(vmem_limit_bytes=vmem << 20),
         cost_estimate=pl.CostEstimate(flops=flops, bytes_accessed=size, transcendentals=0),
     )(*args)
+
+
+def copies(pairs, semaphores, first=0):
+    started = [pltpu.make_async_copy(a, b, semaphores.at[first + i]) for i, (a, b) in enumerate(pairs)]
+    for copy in started:
+        copy.start()
+    return started
+
+
+def wait(started):
+    for copy in started:
+        copy.wait()
 
 
 def store_payload(ref, rows):
@@ -113,7 +125,13 @@
     return jnp.concatenate(tiles, axis=1)
 
 
-def z_in_body(grid_ref, table, out_ref):
+def z_in_body(field, table, grid_ref, out_ref):
+    channels, cells_x, width = field.shape
+    for x in range(cells_x):
+        piece = field[:, x, :]
+        piece = jnp.concatenate([piece, jnp.zeros((CP - channels, width), F32)], axis=0)
+        for y in range(width // NZ):
+            grid_ref[y, :, NZ * x : NZ * x + NZ] = piece[:, NZ * y : NZ * y + NZ]
     cells = grid_ref[...].reshape(-1, grid_ref.shape[2])
     store_payload(out_ref, product(table, cells, ((1,), (1,))))
 
@@ -125,7 +143,10 @@
         out_ref[:, 8 * tile : 8 * tile + 8, :] = block.reshape(out_ref.shape[0], 8, LANES)
 
 
-def mix_body(received, weights, kept, place, y_in, y_out, out_ref, stacked, s_re, s_im):
+def mix_body(received_hbm, weights_hbm, kept, place, y_in, y_out, out_ref, stacked, s_re, s_im, received, weights, sems):
+    arrived = copies([(received_hbm, received)], sems, 2)
+    started = copies([(weights_hbm.at[0], weights.at[0]), (weights_hbm.at[1], weights.at[1])], sems)
+    wait(arrived)
     cells_y = received.shape[0]
     rows = load_payload(received)
     block = rows.shape[0]
@@ -146,6 +167,7 @@
         middle = jnp.where(row < 4, first, second)
         return jnp.concatenate([first] * 4 + [middle] + [second] * 4, axis=0)
 
+    wait(started)
     total_re = jnp.zeros((pair, count), F32)
     total_im = jnp.zeros((pair, count), F32)
     for c in range(0, channels, 2):
@@ -173,21 +195,23 @@
 ROW = 368
 
 
-def taps_body(kernels, out_ref, scratch):
+def taps_body(kernels, *refs):
     channels = kernels.shape[2]
+    scratch = refs[3]
     for r in range(3):
+        out_ref = refs[r]
         scratch[...] = jnp.zeros(scratch.shape, F32)
         for tap in range(27):
             row, lane = CP * (tap % 3), CP * (tap // 3)
             scratch[row : row + channels, lane : lane + channels] = kernels[r, tap]
         high, low = split(scratch[...].T[:ROW])
-        out_ref[r, :ROW, :128] = high
-        out_ref[r, :ROW, 128:] = high
-        out_ref[r, ROW:, :128] = low
-        out_ref[r, ROW:, 128:] = jnp.zeros((ROW, 128), BF16)
-
-
-def convolve_rows(load_row, rows_in, width, taps, refs, finish):
+        out_ref[:ROW, :128] = high
+        out_ref[:ROW, 128:] = high
+        out_ref[ROW:, :128] = low
+        out_ref[ROW:, 128:] = jnp.zeros((ROW, 128), BF16)
+
+
+def convolve_rows(load_row, rows_in, width, taps, refs, finish, rest=()):
     stack_a, stack_b, first_sum, second_sum, whole = refs
     z_position = lax.broadcasted_iota(jnp.int32, (CP, LANES), 1) % NZ
     has_lower = z_position >= 1
@@ -244,7 +268,9 @@
         return carry
 
     prepare(0, stack_a)
-    lax.fori_loop(0, rows_in // 2, pair, 0)
+    pair(0, 0)
+    wait(rest)
+    lax.fori_loop(1, rows_in // 2, pair, 0)
     emit(rows_in - 3)
 
 
@@ -252,50 +278,87 @@
     return [pltpu.VMEM((256, width), BF16)] * 2 + [pltpu.VMEM((3 * CP, width), F32)] * 3
 
 
-def inside(place, first_x, first_y, sizes, width):
+def inside(place, first_x, sizes, width):
     cells_x, cells_y, full_x, full_y = sizes
     x = place[0] * cells_x + first_x + lax.broadcasted_iota(jnp.int32, (CP, width), 1) // NZ
     in_x = (x >= 0) & (x < full_x)
 
-    def at(row):
-        y = place[1] * cells_y + first_y + row
+    def at(local_y):
+        y = place[1] * cells_y + local_y
         return in_x & ((y >= 0) & (y < full_y))
 
     return at
 
 
-def first_body(sizes, wide, before, after, place, taps, out_ref, rows, *refs):
-    cells_y = wide.shape[0]
-    rows[0:3] = before[...]
-    rows[3 : 3 + cells_y] = wide[...]
-    rows[3 + cells_y :] = after[...]
-    keep = inside(place, -2, -2, sizes, 512)
+def gather(sources, rows, target, first):
+    width = sources[0].shape[2]
+    count = rows.stop - rows.start
+    return [
+        (s.at[rows], target.at[slice(first, first + count), :, slice(width * i, width * i + width)])
+        for i, s in enumerate(sources)
+    ]
+
+
+def inner_body(sizes, left, own, right, place, taps, out_ref, rows, staged, sems, *refs):
+    taps_ref, refs = refs[0], refs[1:]
+    count = own.shape[0]
+    sides = (left, own, right)
+    head = copies([(taps, taps_ref)] + gather(sides, slice(0, 3), rows, 0), sems)
+    rest = copies(gather(sides, slice(3, count), rows, 3), sems, 4)
+    wait(head)
+    keep = inside(place, -2, sizes, 512)
 
     def finish(row, tiles):
         values = jnp.concatenate(tiles[1:5], axis=1)
-        out_ref[row] = jnp.where(keep(row), gelu_exact(values), 0.0)
-
-    convolve_rows(lambda i: rows[i], cells_y + 6, 768, taps, refs, finish)
-
-
-def second_body(sizes, cells, place, taps, out_ref, *refs):
-    keep = inside(place, -2, -1, sizes, 512)
+        staged[row] = jnp.where(keep(row + 1), gelu_exact(values), 0.0)
+
+    convolve_rows(lambda i: rows[i], count, 768, taps_ref, refs, finish, rest)
+    wait(copies([(staged, out_ref)], sems))
+
+
+def outer_body(sizes, before, left, own, right, after, place, taps, out_ref, rows, staged, sems, *refs):
+    taps_ref, refs = refs[0], refs[1:]
+    count = own.shape[0]
+    sides = (left, own, right)
+    head = copies([(taps, taps_ref), (before, rows.at[0:3])], sems)
+    pairs = gather(sides, slice(0, 2), rows, 3) + gather(sides, slice(count - 2, count), rows, 5)
+    rest = copies(pairs + [(after, rows.at[7:10])], sems, 2)
+    wait(head)
+    keep = inside(place, -2, sizes, 512)
 
     def finish(row, tiles):
+        values = jnp.concatenate(tiles[1:5], axis=1)
+        local_y = jnp.where(row < 4, row - 2, row + count - 6)
+        staged[row] = jnp.where(keep(local_y), gelu_exact(values), 0.0)
+
+    convolve_rows(lambda i: rows[i], 10, 768, taps_ref, refs, finish, rest)
+    wait(copies([(staged, out_ref)], sems))
+
+
+def later_body(sizes, inner, outer, place, taps_1, taps_2, out_ref, rows, second, staged, sems, *refs):
+    taps_ref_1, taps_ref_2, refs = refs[0], refs[1], refs[2:]
+    count = inner.shape[0]
+    head = copies([(taps_1, taps_ref_1), (outer.at[0:3], rows.at[0:3])], sems)
+    pairs = [(inner, rows.at[3 : 3 + count]), (outer.at[5:8], rows.at[3 + count : 6 + count]), (taps_2, taps_ref_2)]
+    rest = copies(pairs, sems, 2)
+    wait(head)
+    keep = inside(place, -2, sizes, 512)
+
+    def finish_second(row, tiles):
         values = jnp.concatenate(tiles, axis=1)
-        out_ref[row] = jnp.where(keep(row), gelu_exact(values), 0.0)
-
-    convolve_rows(lambda i: cells[i], cells.shape[0], 512, taps, refs, finish)
-
-
-def third_body(cells, taps, out_ref, *refs):
-    def finish(row, tiles):
-        out_ref[row] = jnp.concatenate(tiles[1:3], axis=1)
-
-    convolve_rows(lambda i: cells[i], cells.shape[0], 512, taps, refs, finish)
-
-
-def last_body(received, third, table, out_ref):
+        second[row] = jnp.where(keep(row - 1), gelu_exact(values), 0.0)
+
+    def finish_third(row, tiles):
+        staged[row] = jnp.concatenate(tiles[1:3], axis=1)
+
+    convolve_rows(lambda i: rows[i], count + 6, 512, taps_ref_1, refs, finish_second, rest)
+    convolve_rows(lambda i: second[i], count + 4, 512, taps_ref_2, refs, finish_third)
+    wait(copies([(staged, out_ref)], sems))
+
+
+def last_body(received_hbm, third_hbm, table, out_ref, received, third, sems):
+    arrived = copies([(received_hbm, received), (third_hbm, third)], sems)
+    wait(arrived)
     spectrum = load_payload(received)[:, : third.shape[0] * CP]
     high, low = split(spectrum)
 
@@ -303,7 +366,11 @@
         return lax.dot_general(left, right, (((0,), (0,)), ((), ())), preferred_element_type=F32)
 
     spectral = dot(high, table[0]) + dot(low, table[0]) + dot(high, table[1])
-    out_ref[...] = gelu_exact(spectral.reshape(third.shape) + third[...])
+    out = gelu_exact(spectral.reshape(third.shape) + third[...])
+    channels, cells_x, width = out_ref.shape
+    for x in range(cells_x):
+        piece = [out[y, :channels, NZ * x : NZ * x + NZ] for y in range(width // NZ)]
+        out_ref[:, x, :] = jnp.concatenate(piece, axis=1)
 
 
 def shift(values, axis, step):
@@ -327,61 +394,81 @@
         jnp.asarray(t) for t in tables(size_x, size_y, cells_x, cells_y, modes_x, modes_z)
     ]
 
-    grid = field.reshape(channels, cells_x, cells_y, NZ).transpose(2, 0, 1, 3)
-    grid = jnp.pad(grid.reshape(cells_y, channels, cells_x * NZ), ((0, 0), (0, CP - channels), (0, 0)))
-
-    from_left = shift(grid, "gx", 1)
-    from_right = shift(grid, "gx", -1)
-    sent = call(z_in_body, jax.ShapeDtypeStruct((size_x, 24, LANES), F32), grid, z_in)
-    taps = call(
-        taps_body, jax.ShapeDtypeStruct((3, 2 * ROW, 256), BF16), conv_kernels,
-        scratch=[pltpu.VMEM((128, 384), F32)],
-    )
+    sizes = (cells_x, cells_y, full_x, full_y)
+    row_scratch = [pltpu.SemaphoreType.DMA((9,)), pltpu.VMEM((2 * ROW, 256), BF16)]
+    taps_shape = jax.ShapeDtypeStruct((2 * ROW, 256), BF16)
+
+    grid, sent = call(
+        z_in_body,
+        (
+            jax.ShapeDtypeStruct((cells_y, CP, cells_x * NZ), F32),
+            jax.ShapeDtypeStruct((size_x, 24, LANES), F32),
+        ),
+        field, z_in,
+    )
+    left = shift(grid, "gx", 1)
+    right = shift(grid, "gx", -1)
+    taps = call(taps_body, (taps_shape,) * 3, conv_kernels, scratch=[pltpu.VMEM((128, 384), F32)])
     received = lax.all_to_all(sent, "gx", 0, 0, tiled=True)
-    wide = jnp.concatenate([from_left, grid, from_right], axis=2)
-    before = shift(wide[cells_y - 3 :], "gy", 1)
-    after = shift(wide[:3], "gy", -1)
+
+    def edge(rows):
+        return jnp.concatenate([left[rows], grid[rows], right[rows]], axis=2)
+
+    before = shift(edge(slice(cells_y - 3, cells_y)), "gy", 1)
+    after = shift(edge(slice(0, 3)), "gy", -1)
     sent = call(rows_body, jax.ShapeDtypeStruct((size_y, 24, LANES), F32), received, x_in)
 
-    sizes = (cells_x, cells_y, full_x, full_y)
-    wide, sent = lax.optimization_barrier((wide, sent))
+    left, sent = lax.optimization_barrier((left, sent))
     received = lax.all_to_all(sent, "gy", 0, 0, tiled=True)
-    first = call(
-        lambda *refs: first_body(sizes, *refs),
-        jax.ShapeDtypeStruct((cells_y + 4, CP, 512), F32),
-        wide, before, after, place, taps[0],
-        scratch=[pltpu.VMEM((cells_y + 6, CP, 768), F32)] + conv_scratch(768),
-        smem=(3,), flops=6 << 30,
-    )
-    first, received = lax.optimization_barrier((first, received))
+    inner = call(
+        lambda *refs: inner_body(sizes, *refs),
+        jax.ShapeDtypeStruct((cells_y - 2, CP, 512), F32),
+        left, grid, right, place, taps[0],
+        scratch=[pltpu.VMEM((cells_y, CP, 768), F32), pltpu.VMEM((cells_y - 2, CP, 512), F32)]
+        + row_scratch + conv_scratch(768),
+        smem=(3,), hbm=(0, 1, 2, 4), out_hbm=(0,), vmem=60, flops=3 << 30,
+    )
+    inner, received = lax.optimization_barrier((inner, received))
     weights = mix_weights.reshape(2, channels * channels, kx_local * KY)
     sent = call(
         mix_body,
         jax.ShapeDtypeStruct((size_y, 24, LANES), F32),
         received, weights, kept_z.reshape(1, -1), place, y_in, y_out,
         scratch=[pltpu.VMEM((cells_y * size_y * kx_local * 2, LANES), F32)]
-        + [pltpu.VMEM((LANES, kx_local * KY), F32)] * 2,
-        smem=(3,),
-    )
-    first, sent = lax.optimization_barrier((first, sent))
+        + [pltpu.VMEM((LANES, kx_local * KY), F32)] * 2
+        + [pltpu.VMEM(received.shape, F32), pltpu.VMEM(weights.shape, F32), pltpu.SemaphoreType.DMA((3,))],
+        smem=(3,), hbm=(0, 1), vmem=60,
+    )
+    before, sent = lax.optimization_barrier((before, sent))
     received = lax.all_to_all(sent, "gy", 0, 0, tiled=True)
-    second = call(
-        lambda *refs: second_body(sizes, *refs),
-        jax.ShapeDtypeStruct((cells_y + 2, CP, 512), F32),
-        first, place, taps[1], scratch=conv_scratch(512), smem=(1,), flops=4 << 30,
-    )
-    second, received = lax.optimization_barrier((second, received))
+    outer = call(
+        lambda *refs: outer_body(sizes, *refs),
+        jax.ShapeDtypeStruct((8, CP, 512), F32),
+        before, left, grid, right, after, place, taps[0],
+        scratch=[pltpu.VMEM((10, CP, 768), F32), pltpu.VMEM((8, CP, 512), F32)] + row_scratch + conv_scratch(768),
+        smem=(5,), hbm=(0, 1, 2, 3, 4, 6), out_hbm=(0,), vmem=60, flops=4 << 30,
+    )
+    outer, received = lax.optimization_barrier((outer, received))
     sent = call(rows_body, jax.ShapeDtypeStruct((size_x, 24, LANES), F32), received, x_out)
-    second, sent = lax.optimization_barrier((second, sent))
+    outer, sent = lax.optimization_barrier((outer, sent))
     received = lax.all_to_all(sent, "gx", 0, 0, tiled=True)
     third = call(
-        third_body,
+        lambda *refs: later_body(sizes, *refs),
         jax.ShapeDtypeStruct((cells_y, CP, cells_x * NZ), F32),
-        second, taps[2], scratch=conv_scratch(512), flops=3 << 30,
-    )
-    out = call(last_body, jax.ShapeDtypeStruct(third.shape, F32), received, third, z_out)
-    out = out[:, :channels].reshape(cells_y, channels, cells_x, NZ).transpose(1, 2, 0, 3)
-    return out.reshape(channels, cells_x, cells_y * NZ)
+        inner, outer, place, taps[1], taps[2],
+        scratch=[
+            pltpu.VMEM((cells_y + 4, CP, 512), F32),
+            pltpu.VMEM((cells_y + 2, CP, 512), F32),
+            pltpu.VMEM((cells_y, CP, cells_x * NZ), F32),
+        ]
+        + row_scratch + [pltpu.VMEM((2 * ROW, 256), BF16)] + conv_scratch(512),
+        smem=(2,), hbm=(0, 1, 3, 4), out_hbm=(0,), vmem=60, flops=8 << 30,
+    )
+    return call(
+        last_body, jax.ShapeDtypeStruct(field.shape, F32), received, third, z_out,
+        scratch=[pltpu.VMEM(received.shape, F32), pltpu.VMEM(third.shape, F32), pltpu.SemaphoreType.DMA((2,))],
+        hbm=(0, 1), vmem=60,
+    )
 
 
 def solution(mesh):

time: 90.7 us -> 91.6 us (level)
  Pallas kernels: 20.1 us -> 33 us
  local copies, waits for them, and re-layouts: 11 us -> 4.26 us
  waiting for transfers between devices: 14.1 us -> 10.2 us
    pallas_call x9, Pallas kernels: 20.1 us -> 33 us  [call(): pl.pallas_call(body, out_shape=out_shape, in_specs=in_specs, out_specs=tu...]
    all_to_all x2, waiting for transfers between devices: 14.1 us -> 10.2 us  [shards(): received = lax.all_to_all(sent, 'gx', 0, 0, tiled=True)]
    reshape x6 -> x0, local copies, waits for them, and re-layouts: 3 us -> none  [the longest x2 1.34 us: shards(): grid = field.reshape(channels, cells_x, cells_y, NZ).transpose(2, 0, 1, 3)]
    unnamed x36 -> x30, local copies, waits for them, and re-layouts: 6.73 us -> 4.21 us
    concatenate x1 -> x2, other arithmetic: 1.14 us -> 0.05 us  [edge(): return jnp.concatenate([left[rows], grid[rows], right[rows]], axis=2)]
    squeeze x1 -> x0, local copies, waits for them, and re-layouts: 1.03 us -> none  [shards(): taps[2]]
    ppermute x4, starting transfers between devices: 13.4 us -> 12.4 us  [shift(): return lax.ppermute(values, axis, pairs)]
  transfers between devices with their start and end apart: 8 -> 8, of which waited for: 2 -> 2; matrix products, arithmetic and copies ran while one was open for 3% -> 1% of each run, Pallas kernels for 18% -> 30%
where the time goes in v2:
time: 91.6 us; the launch traced here: 90.4 us
  starting transfers between devices  42 us (46%)
  Pallas kernels  33 us (36%)
  waiting for transfers between devices  10.2 us (11%)
  local copies, waits for them, and re-layouts  4.26 us (5%)
    pallas_call x9, Pallas kernels, call(): pl.pallas_call(body, out_shape=out_shape, in_specs=in_specs, out_specs=tu...  33 us
    all_to_all x2, starting transfers between devices, shards(): received = lax.all_to_all(sent, 'gx', 0, 0, tiled=True)  17 us
    all_to_all x2, starting transfers between devices, shards(): received = lax.all_to_all(sent, 'gy', 0, 0, tiled=True)  12.6 us
    ppermute x4, starting transfers between devices, shift(): return lax.ppermute(values, axis, pairs)  12.4 us
    all_to_all x2, waiting for transfers between devices, shards(): received = lax.all_to_all(sent, 'gx', 0, 0, tiled=True)  10.2 us
    unnamed x30, local copies, waits for them, and re-layouts  4.21 us
  transfers between devices with their start and end apart: 8, of which 2 were waited for; matrix products, arithmetic and copies ran while one was open for 1% of the time, Pallas kernels for 30%

profile of v2, /device:TPU:1, one launch (start us, length us, event | category | flops | bytes accessed | tf_op | source)
XLA Modules:
  0.0 90.4 jit_solution(10840807988371121048)
XLA Ops:
  0.0 1.1 %copy-done.1 = f32[36,4,512]{2,1,0:T(4,128)S(1)} copy-done((f32[36,4,512]{2,1,0:T(4,128)S(1)}, f32[36,4,512]{2,1,0:T(4,128)}, u32[]{:S(2)}) %copy-start.1) | copy-done | bytes 294936
  1.1 0.9 %copy-done.2 = bf16[2,256,256]{2,1,0:T(8,128)(2,1)S(1)} copy-done((bf16[2,256,256]{2,1,0:T(8,128)(2,1)S(1)}, bf16[2,256,256]{2,1,0:T(8,128)(2,1)}, u32[]{:S(2)}) %copy-start.2) | copy-done | bytes 262168
  2.0 1.3 %shard_map.100 = (f32[8,40,256]{2,1,0:T(8,128)S(1)}, f32[32,24,128]{2,1,0:T(8,128)}) custom-call(f32[36,4,512]{2,1,0:T(4,128)S(1)} %copy-done.1, bf16[2,256,256]{2,1,0:T(8,128)(2,1)S(1)} %copy-done.2), custom_call_target="tpu_custom_call" | custom-call | bytes 557056 | tf_op jit(solution)/shard_map/pallas_call | solution.py:89
  3.3 1.3 %collective-permute-start.1 = (f32[8,40,256]{2,1,0:T(8,128)S(1)}, f32[8,40,256]{2,1,0:T(8,128)S(1)}, u32[]{:S(2)}, u32[]{:S(2)}) collective-permute-start(f32[8,40,256]{2,1,0:T(8,128)S(1)} %get-tuple-element.20.refs_1_.refs_2_), channel_id=1, source_target_pairs={{8,0},{16,8},{24,16},{32,24},{40,32},{48,40},{56,48},{64,56},{72,6... | collective-permute-start | bytes 983048 | tf_op jit(solution)/shard_map/ppermute | solution.py:379
  4.6 4.6 %collective-permute-start = (f32[8,40,256]{2,1,0:T(8,128)S(1)}, f32[8,40,256]{2,1,0:T(8,128)S(1)}, u32[]{:S(2)}, u32[]{:S(2)}) collective-permute-start(f32[8,40,256]{2,1,0:T(8,128)S(1)} %get-tuple-element.20.refs_1_.refs_2_), channel_id=1, source_target_pairs={{0,8},{8,16},{16,24},{24,32},{32,40},{40,48},{48,56},{56,64},{64,7... | collective-permute-start | bytes 983048 | tf_op jit(solution)/shard_map/ppermute | solution.py:379
  9.2 13.1 %all-to-all-start = ((f32[32,24,128]{2,1,0:T(8,128)}), f32[32,24,128]{2,1,0:T(8,128)S(1)}, u32[]{:S(2)}, u32[]{:S(2)}) async-start(f32[32,24,128]{2,1,0:T(8,128)} %get-tuple-element.21), calls=%async_computation | async-start | bytes 786432 | tf_op jit(solution)/shard_map/all_to_all | solution.py:412
  22.4 0.7 shard_map.102
  23.3 4.6 %collective-permute-start.2 = (f32[3,40,768]{2,1,0:T(8,128)S(1)}, f32[3,40,768]{2,1,0:T(8,128)S(1)}, u32[]{:S(2)}, u32[]{:S(2)}) collective-permute-start(f32[3,40,768]{2,1,0:T(8,128)S(1)} %pad_maximum_fusion), channel_id=1, source_target_pairs={{0,1},{1,2},{2,3},{3,4},{4,5},{5,6},{6,7},{8,9},{9,10},{10,11},{11... | collective-permute-start | bytes 1105928 | tf_op jit(solution)/shard_map/ppermute | solution.py:379
  27.9 1.9 %collective-permute-start.3 = (f32[3,40,768]{2,1,0:T(8,128)S(1)}, f32[3,40,768]{2,1,0:T(8,128)S(1)}, u32[]{:S(2)}, u32[]{:S(2)}) collective-permute-start(f32[3,40,768]{2,1,0:T(8,128)S(1)} %pad_maximum_fusion.1), channel_id=1, source_target_pairs={{1,0},{2,1},{3,2},{4,3},{5,4},{6,5},{7,6},{9,8},{10,9},{11,10},{12... | collective-permute-start | bytes 1105928 | tf_op jit(solution)/shard_map/ppermute | solution.py:379
  30.5 4.9 %all-to-all-done.received = f32[32,24,128]{2,1,0:T(8,128)S(1)} async-done(((f32[32,24,128]{2,1,0:T(8,128)}), f32[32,24,128]{2,1,0:T(8,128)S(1)}, u32[]{:S(2)}, u32[]{:S(2)}) %all-to-all-start) | async-done | bytes 393248 | tf_op jit(solution)/shard_map/all_to_all | solution.py:412
  35.4 0.9 shard_map.101
  36.3 7.7 %all-to-all-start.1 = ((f32[8,24,128]{2,1,0:T(8,128)}), f32[8,24,128]{2,1,0:T(8,128)S(1)}, u32[]{:S(2)}, u32[]{:S(2)}) async-start(f32[8,24,128]{2,1,0:T(8,128)} %shard_map.101), calls=%async_computation.1 | async-start | bytes 196608 | tf_op jit(solution)/shard_map/all_to_all | solution.py:422
  44.0 6.0 %shard_map.103.refs_0_ = f32[6,40,512]{2,1,0:T(8,128)} custom-call(f32[8,40,256]{2,1,0:T(8,128)} %copy-done.12, f32[8,40,256]{2,1,0:T(8,128)} %copy-done.3, f32[8,40,256]{2,1,0:T(8,128)} %copy-done.11, s32[2]{0:T(128)} %pad_add_fusion.refs_3_.place.refs_5_.refs_2_, bf16[736,256]{1,0:T(8,128)(2,1)} %copy-done.8), custom_call_target="tpu_custom_call" | custom-call | flops 3221225472 | bytes 1359880 | tf_op jit(solution)/shard_map/pallas_call | solution.py:89
  50.0 0.6 copy-done.10
  50.6 4.1 %shard_map.104 = f32[8,24,128]{2,1,0:T(8,128)} custom-call(f32[8,24,128]{2,1,0:T(8,128)} %copy-done.10, f32[2,1296,128]{2,1,0:T(8,128)} %bitcast.4, s32[1,128]{1,0:T(1,128)} %bitcast.5, s32[2]{0:T(128)} %pad_add_fusion.refs_3_.place.refs_5_.refs_2_, bf16[2,256,512]{2,1,0:T(8,128)(2,1)} %constant.23.clone.y_in, bf16[2,512,256]{2,1,0:T(8,128)(2,1)} %constant.24.clone.y_out), custom_call_target="tpu_custom_call" | custom-call | bytes 2474504 | tf_op jit(solution)/shard_map/pallas_call | solution.py:89
  54.7 4.8 %all-to-all-start.2 = ((f32[8,24,128]{2,1,0:T(8,128)}), f32[8,24,128]{2,1,0:T(8,128)S(1)}, u32[]{:S(2)}, u32[]{:S(2)}) async-start(f32[8,24,128]{2,1,0:T(8,128)} %shard_map.104), calls=%async_computation.2 | async-start | bytes 196608 | tf_op jit(solution)/shard_map/all_to_all | solution.py:443
  59.6 0.7 copy-done.14
  60.3 6.7 %shard_map.105.refs_1_ = f32[8,40,512]{2,1,0:T(8,128)} custom-call(f32[3,40,768]{2,1,0:T(8,128)} %copy-done.13, f32[8,40,256]{2,1,0:T(8,128)} %copy-done.12, f32[8,40,256]{2,1,0:T(8,128)} %copy-done.3, f32[8,40,256]{2,1,0:T(8,128)} %copy-done.11, f32[3,40,768]{2,1,0:T(8,128)} %copy-done.14, s32[2]{0:T(128)} %pad_add_fusion.refs_3_.place.refs_5_.refs_2_, ...), custom_call_target="tpu_custom_call" | custom-call | flops 4294967296 | bytes 2097160 | tf_op jit(solution)/shard_map/pallas_call | solution.py:89
  67.1 1.1 %shard_map.106 = f32[32,24,128]{2,1,0:T(8,128)} custom-call(f32[8,24,128]{2,1,0:T(8,128)S(1)} %all-to-all-done.2.received, bf16[2,256,64]{2,1,0:T(8,128)(2,1)S(1)} %copy-done.4), custom_call_target="tpu_custom_call" | custom-call | bytes 163840 | tf_op jit(solution)/shard_map/pallas_call | solution.py:89
  68.1 3.9 %all-to-all-start.3 = ((f32[32,24,128]{2,1,0:T(8,128)}), f32[32,24,128]{2,1,0:T(8,128)S(1)}, u32[]{:S(2)}, u32[]{:S(2)}) async-start(f32[32,24,128]{2,1,0:T(8,128)} %shard_map.106), calls=%async_computation.3 | async-start | bytes 786432 | tf_op jit(solution)/shard_map/all_to_all | solution.py:454
  72.1 9.1 %shard_map.107.third_hbm = f32[8,40,256]{2,1,0:T(8,128)} custom-call(f32[6,40,512]{2,1,0:T(8,128)} %shard_map.103.refs_0_, f32[8,40,512]{2,1,0:T(8,128)} %shard_map.105.refs_1_, s32[2]{0:T(128)} %pad_add_fusion.refs_3_.place.refs_5_.refs_2_, bf16[736,256]{1,0:T(8,128)(2,1)} %copy-done.6, bf16[736,256]{1,0:T(8,128)(2,1)} %copy-done.7), custom_call_target="tpu_custom_call" | custom-call | flops 8589934592 | bytes 1900552 | tf_op jit(solution)/shard_map/pallas_call | solution.py:89
  81.2 5.3 %all-to-all-done.3.received_hbm = f32[32,24,128]{2,1,0:T(8,128)S(1)} async-done(((f32[32,24,128]{2,1,0:T(8,128)}), f32[32,24,128]{2,1,0:T(8,128)S(1)}, u32[]{:S(2)}, u32[]{:S(2)}) %all-to-all-start.3) | async-done | bytes 393248 | tf_op jit(solution)/shard_map/all_to_all | solution.py:454
  86.5 0.8 copy-done.9
  87.2 3.2 %shard_map.108 = f32[36,4,512]{2,1,0:T(4,128)} custom-call(f32[32,24,128]{2,1,0:T(8,128)} %copy-done.9, f32[8,40,256]{2,1,0:T(8,128)} %shard_map.107.third_hbm, bf16[2,256,256]{2,1,0:T(8,128)(2,1)} %constant.26.clone.table), custom_call_target="tpu_custom_call" | custom-call | bytes 983040 | tf_op jit(solution)/shard_map/pallas_call | solution.py:89
  (37 shorter events, 0.8 us)
Async XLA Ops:
  0.0 22.4 %copy-start = (f32[3,27,36,36]{3,2,1,0:T(8,128)S(1)}, f32[3,27,36,36]{3,2,1,0:T(8,128)}, u32[]{:S(2)}) copy-start(f32[3,27,36,36]{3,2,1,0:T(8,128)} %kernels.1) | copy-start | bytes 1259716
  0.0 1.1 %copy-start.1 = (f32[36,4,512]{2,1,0:T(4,128)S(1)}, f32[36,4,512]{2,1,0:T(4,128)}, u32[]{:S(2)}) copy-start(f32[36,4,512]{2,1,0:T(4,128)} %field.1) | copy-start | bytes 884740
  1.1 0.9 %copy-start.2 = (bf16[2,256,256]{2,1,0:T(8,128)(2,1)S(1)}, bf16[2,256,256]{2,1,0:T(8,128)(2,1)}, u32[]{:S(2)}) copy-start(bf16[2,256,256]{2,1,0:T(8,128)(2,1)} %constant.21.clone.table) | copy-start | bytes 786436
  3.3 19.9 %copy-start.3 = (f32[8,40,256]{2,1,0:T(8,128)}, f32[8,40,256]{2,1,0:T(8,128)S(1)}, u32[]{:S(2)}) copy-start(f32[8,40,256]{2,1,0:T(8,128)S(1)} %get-tuple-element.20.refs_1_.refs_2_) | copy-start | bytes 983044
  3.3 19.8 %collective-permute-start.1 = (f32[8,40,256]{2,1,0:T(8,128)S(1)}, f32[8,40,256]{2,1,0:T(8,128)S(1)}, u32[]{:S(2)}, u32[]{:S(2)}) collective-permute-start(f32[8,40,256]{2,1,0:T(8,128)S(1)} %get-tuple-element.20.refs_1_.refs_2_), channel_id=1, source_target_pairs={{8,0},{16,8},{24,16},{32,24},{40,32},{48,40},{56,48},{64,56},{72,6... | collective-permute-start | bytes 983048 | tf_op jit(solution)/shard_map/ppermute | solution.py:379
  4.6 18.6 %collective-permute-start = (f32[8,40,256]{2,1,0:T(8,128)S(1)}, f32[8,40,256]{2,1,0:T(8,128)S(1)}, u32[]{:S(2)}, u32[]{:S(2)}) collective-permute-start(f32[8,40,256]{2,1,0:T(8,128)S(1)} %get-tuple-element.20.refs_1_.refs_2_), channel_id=1, source_target_pairs={{0,8},{8,16},{16,24},{24,32},{32,40},{40,48},{48,56},{56,64},{64,7... | collective-permute-start | bytes 983048 | tf_op jit(solution)/shard_map/ppermute | solution.py:379
  9.2 26.2 %all-to-all-start = ((f32[32,24,128]{2,1,0:T(8,128)}), f32[32,24,128]{2,1,0:T(8,128)S(1)}, u32[]{:S(2)}, u32[]{:S(2)}) async-start(f32[32,24,128]{2,1,0:T(8,128)} %get-tuple-element.21), calls=%async_computation | async-start | bytes 786432 | tf_op jit(solution)/shard_map/all_to_all | solution.py:412
  22.4 13.0 %copy-start.5 = (bf16[2,64,256]{2,1,0:T(8,128)(2,1)S(1)}, bf16[2,64,256]{2,1,0:T(8,128)(2,1)}, u32[]{:S(2)}) copy-start(bf16[2,64,256]{2,1,0:T(8,128)(2,1)} %constant.22.clone.table) | copy-start | bytes 196612
  23.1 6.7 %copy-start.6 = (bf16[736,256]{1,0:T(8,128)(2,1)}, bf16[736,256]{1,0:T(8,128)(2,1)S(1)}, u32[]{:S(2)}) copy-start(bf16[736,256]{1,0:T(8,128)(2,1)S(1)} %get-tuple-element.33.refs_3_) | copy-start | bytes 1130500
  23.1 6.7 %copy-start.7 = (bf16[736,256]{1,0:T(8,128)(2,1)}, bf16[736,256]{1,0:T(8,128)(2,1)S(1)}, u32[]{:S(2)}) copy-start(bf16[736,256]{1,0:T(8,128)(2,1)S(1)} %get-tuple-element.34.refs_4_) | copy-start | bytes 1130500
  23.1 6.7 %copy-start.8 = (bf16[736,256]{1,0:T(8,128)(2,1)}, bf16[736,256]{1,0:T(8,128)(2,1)S(1)}, u32[]{:S(2)}) copy-start(bf16[736,256]{1,0:T(8,128)(2,1)S(1)} %get-tuple-element.23.refs_4_.refs_6_) | copy-start | bytes 1130500
  23.1 20.9 %copy-start.11 = (f32[8,40,256]{2,1,0:T(8,128)}, f32[8,40,256]{2,1,0:T(8,128)S(1)}, u32[]{:S(2)}) copy-start(f32[8,40,256]{2,1,0:T(8,128)S(1)} %collective-permute-done.1.refs_2_.refs_3_) | copy-start | bytes 983044
  23.2 20.8 %copy-start.12 = (f32[8,40,256]{2,1,0:T(8,128)}, f32[8,40,256]{2,1,0:T(8,128)S(1)}, u32[]{:S(2)}) copy-start(f32[8,40,256]{2,1,0:T(8,128)S(1)} %collective-permute-done.refs_0_.refs_1_) | copy-start | bytes 983044
  23.3 31.4 %collective-permute-start.2 = (f32[3,40,768]{2,1,0:T(8,128)S(1)}, f32[3,40,768]{2,1,0:T(8,128)S(1)}, u32[]{:S(2)}, u32[]{:S(2)}) collective-permute-start(f32[3,40,768]{2,1,0:T(8,128)S(1)} %pad_maximum_fusion), channel_id=1, source_target_pairs={{0,1},{1,2},{2,3},{3,4},{4,5},{5,6},{6,7},{8,9},{9,10},{10,11},{11... | collective-permute-start | bytes 1105928 | tf_op jit(solution)/shard_map/ppermute | solution.py:379
  27.9 31.6 %collective-permute-start.3 = (f32[3,40,768]{2,1,0:T(8,128)S(1)}, f32[3,40,768]{2,1,0:T(8,128)S(1)}, u32[]{:S(2)}, u32[]{:S(2)}) collective-permute-start(f32[3,40,768]{2,1,0:T(8,128)S(1)} %pad_maximum_fusion.1), channel_id=1, source_target_pairs={{1,0},{2,1},{3,2},{4,3},{5,4},{6,5},{7,6},{9,8},{10,9},{11,10},{12... | collective-permute-start | bytes 1105928 | tf_op jit(solution)/shard_map/ppermute | solution.py:379
  36.3 13.7 %all-to-all-start.1 = ((f32[8,24,128]{2,1,0:T(8,128)}), f32[8,24,128]{2,1,0:T(8,128)S(1)}, u32[]{:S(2)}, u32[]{:S(2)}) async-start(f32[8,24,128]{2,1,0:T(8,128)} %shard_map.101), calls=%async_computation.1 | async-start | bytes 196608 | tf_op jit(solution)/shard_map/all_to_all | solution.py:422
  50.0 0.6 copy-start.10
  54.7 4.8 %copy-start.13 = (f32[3,40,768]{2,1,0:T(8,128)}, f32[3,40,768]{2,1,0:T(8,128)S(1)}, u32[]{:S(2)}) copy-start(f32[3,40,768]{2,1,0:T(8,128)S(1)} %collective-permute-done.2.refs_0_) | copy-start | bytes 1105924
  54.7 12.3 %all-to-all-start.2 = ((f32[8,24,128]{2,1,0:T(8,128)}), f32[8,24,128]{2,1,0:T(8,128)S(1)}, u32[]{:S(2)}, u32[]{:S(2)}) async-start(f32[8,24,128]{2,1,0:T(8,128)} %shard_map.104), calls=%async_computation.2 | async-start | bytes 196608 | tf_op jit(solution)/shard_map/all_to_all | solution.py:443
  59.5 7.5 %copy-start.4 = (bf16[2,256,64]{2,1,0:T(8,128)(2,1)S(1)}, bf16[2,256,64]{2,1,0:T(8,128)(2,1)}, u32[]{:S(2)}) copy-start(bf16[2,256,64]{2,1,0:T(8,128)(2,1)} %constant.25.clone.table) | copy-start | bytes 196612
  59.5 0.7 copy-start.14
  68.1 18.3 %all-to-all-start.3 = ((f32[32,24,128]{2,1,0:T(8,128)}), f32[32,24,128]{2,1,0:T(8,128)S(1)}, u32[]{:S(2)}, u32[]{:S(2)}) async-start(f32[32,24,128]{2,1,0:T(8,128)} %shard_map.106), calls=%async_computation.3 | async-start | bytes 786432 | tf_op jit(solution)/shard_map/all_to_all | solution.py:454
  86.5 0.8 copy-start.9

commit v3 on v2

--- a/solution.py
+++ b/solution.py
@@ -1,3 +1,4 @@
+import functools
 import math
 
 import jax
@@ -11,6 +12,8 @@
 
 NZ = 64
 KY = 32
+INNER = 1024
+FULL = 60
 CP = 40
 LANES = 128
 F32 = jnp.float32
@@ -79,12 +82,12 @@
     return [split_table(t) for t in (z_in, x_in, y_in, y_out, x_out, z_out)]
 
 
-def call(body, out_shape, *args, scratch=(), flops=0, smem=(), hbm=(), out_hbm=(), vmem=24):
+def call(body, out_shape, *args, scratch=(), flops=0, smem=(), hbm=(), out_hbm=(), vmem=24, light=False):
     def spec(index, kept):
         return pl.BlockSpec(memory_space=pl.ANY if index in kept else pltpu.VMEM)
 
     in_specs = [pl.BlockSpec(memory_space=pltpu.SMEM) if i in smem else spec(i, hbm) for i in range(len(args))]
-    size = sum(a.size * a.dtype.itemsize for a in args)
+    size = 0 if light else sum(a.size * a.dtype.itemsize for a in args)
     many = isinstance(out_shape, tuple)
     return pl.pallas_call(
         body,
@@ -125,7 +128,9 @@
     return jnp.concatenate(tiles, axis=1)
 
 
-def z_in_body(field, table, grid_ref, out_ref):
+def z_in_body(field_hbm, table_hbm, grid_ref, out_ref, field, table, sems):
+    arrived = copies([(field_hbm, field), (table_hbm, table)], sems)
+    wait(arrived[:1])
     channels, cells_x, width = field.shape
     for x in range(cells_x):
         piece = field[:, x, :]
@@ -133,6 +138,7 @@
         for y in range(width // NZ):
             grid_ref[y, :, NZ * x : NZ * x + NZ] = piece[:, NZ * y : NZ * y + NZ]
     cells = grid_ref[...].reshape(-1, grid_ref.shape[2])
+    wait(arrived[1:])
     store_payload(out_ref, product(table, cells, ((1,), (1,))))
 
 
@@ -143,10 +149,7 @@
         out_ref[:, 8 * tile : 8 * tile + 8, :] = block.reshape(out_ref.shape[0], 8, LANES)
 
 
-def mix_body(received_hbm, weights_hbm, kept, place, y_in, y_out, out_ref, stacked, s_re, s_im, received, weights, sems):
-    arrived = copies([(received_hbm, received)], sems, 2)
-    started = copies([(weights_hbm.at[0], weights.at[0]), (weights_hbm.at[1], weights.at[1])], sems)
-    wait(arrived)
+def mix_body(received, weights, kept, place, y_in, y_out, out_ref, stacked, s_re, s_im):
     cells_y = received.shape[0]
     rows = load_payload(received)
     block = rows.shape[0]
@@ -167,7 +170,6 @@
         middle = jnp.where(row < 4, first, second)
         return jnp.concatenate([first] * 4 + [middle] + [second] * 4, axis=0)
 
-    wait(started)
     total_re = jnp.zeros((pair, count), F32)
     total_im = jnp.zeros((pair, count), F32)
     for c in range(0, channels, 2):
@@ -195,15 +197,14 @@
 ROW = 368
 
 
-def taps_body(kernels, *refs):
+def taps_body(first, kernels, *refs):
     channels = kernels.shape[2]
-    scratch = refs[3]
-    for r in range(3):
-        out_ref = refs[r]
+    *outs, scratch = refs
+    for r, out_ref in enumerate(outs):
         scratch[...] = jnp.zeros(scratch.shape, F32)
         for tap in range(27):
             row, lane = CP * (tap % 3), CP * (tap // 3)
-            scratch[row : row + channels, lane : lane + channels] = kernels[r, tap]
+            scratch[row : row + channels, lane : lane + channels] = kernels[first + r, tap]
         high, low = split(scratch[...].T[:ROW])
         out_ref[:ROW, :128] = high
         out_ref[:ROW, 128:] = high
@@ -299,49 +300,47 @@
     ]
 
 
-def inner_body(sizes, left, own, right, place, taps, out_ref, rows, staged, sems, *refs):
-    taps_ref, refs = refs[0], refs[1:]
+def join(sources, rows, target, first):
+    width = sources[0].shape[2]
+    count = rows.stop - rows.start
+    for i, source in enumerate(sources):
+        target[first : first + count, :, width * i : width * i + width] = source[rows]
+
+
+def inner_body(sizes, left, own, right, place, taps, out_ref, rows, *refs):
+    count = own.shape[0]
+    join((left, own, right), slice(0, count), rows, 0)
+    keep = inside(place, -2, sizes, 512)
+
+    def finish(row, tiles):
+        values = jnp.concatenate(tiles[1:5], axis=1)
+        out_ref[row] = jnp.where(keep(row + 1), gelu_exact(values), 0.0)
+
+    convolve_rows(lambda i: rows[i], count, 768, taps, refs, finish)
+
+
+def outer_body(sizes, before, left, own, right, after, place, taps, out_ref, rows, *refs):
     count = own.shape[0]
     sides = (left, own, right)
-    head = copies([(taps, taps_ref)] + gather(sides, slice(0, 3), rows, 0), sems)
-    rest = copies(gather(sides, slice(3, count), rows, 3), sems, 4)
-    wait(head)
-    keep = inside(place, -2, sizes, 512)
-
-    def finish(row, tiles):
-        values = jnp.concatenate(tiles[1:5], axis=1)
-        staged[row] = jnp.where(keep(row + 1), gelu_exact(values), 0.0)
-
-    convolve_rows(lambda i: rows[i], count, 768, taps_ref, refs, finish, rest)
-    wait(copies([(staged, out_ref)], sems))
-
-
-def outer_body(sizes, before, left, own, right, after, place, taps, out_ref, rows, staged, sems, *refs):
-    taps_ref, refs = refs[0], refs[1:]
-    count = own.shape[0]
-    sides = (left, own, right)
-    head = copies([(taps, taps_ref), (before, rows.at[0:3])], sems)
-    pairs = gather(sides, slice(0, 2), rows, 3) + gather(sides, slice(count - 2, count), rows, 5)
-    rest = copies(pairs + [(after, rows.at[7:10])], sems, 2)
-    wait(head)
+    rows[0:3] = before[...]
+    join(sides, slice(0, 2), rows, 3)
+    join(sides, slice(count - 2, count), rows, 5)
+    rows[7:10] = after[...]
     keep = inside(place, -2, sizes, 512)
 
     def finish(row, tiles):
         values = jnp.concatenate(tiles[1:5], axis=1)
         local_y = jnp.where(row < 4, row - 2, row + count - 6)
-        staged[row] = jnp.where(keep(local_y), gelu_exact(values), 0.0)
-
-    convolve_rows(lambda i: rows[i], 10, 768, taps_ref, refs, finish, rest)
-    wait(copies([(staged, out_ref)], sems))
-
-
-def later_body(sizes, inner, outer, place, taps_1, taps_2, out_ref, rows, second, staged, sems, *refs):
-    taps_ref_1, taps_ref_2, refs = refs[0], refs[1], refs[2:]
+        out_ref[row] = jnp.where(keep(local_y), gelu_exact(values), 0.0)
+
+    convolve_rows(lambda i: rows[i], 10, 768, taps, refs, finish)
+
+
+def later_body(sizes, inner, outer, place, taps_1, taps_2, out_ref, rows, second, *refs):
     count = inner.shape[0]
-    head = copies([(taps_1, taps_ref_1), (outer.at[0:3], rows.at[0:3])], sems)
-    pairs = [(inner, rows.at[3 : 3 + count]), (outer.at[5:8], rows.at[3 + count : 6 + count]), (taps_2, taps_ref_2)]
-    rest = copies(pairs, sems, 2)
-    wait(head)
+    rows[0:3] = outer[0:3]
+    rows[3 : 3 + count] = inner[...]
+    rows[3 + count :] = outer[5:8]
     keep = inside(place, -2, sizes, 512)
 
     def finish_second(row, tiles):
@@ -349,16 +348,13 @@
         second[row] = jnp.where(keep(row - 1), gelu_exact(values), 0.0)
 
     def finish_third(row, tiles):
-        staged[row] = jnp.concatenate(tiles[1:3], axis=1)
-
-    convolve_rows(lambda i: rows[i], count + 6, 512, taps_ref_1, refs, finish_second, rest)
-    convolve_rows(lambda i: second[i], count + 4, 512, taps_ref_2, refs, finish_third)
-    wait(copies([(staged, out_ref)], sems))
-
-
-def last_body(received_hbm, third_hbm, table, out_ref, received, third, sems):
-    arrived = copies([(received_hbm, received), (third_hbm, third)], sems)
-    wait(arrived)
+        out_ref[row] = jnp.concatenate(tiles[1:3], axis=1)
+
+    convolve_rows(lambda i: rows[i], count + 6, 512, taps_1, refs, finish_second)
+    convolve_rows(lambda i: second[i], count + 4, 512, taps_2, refs, finish_third)
+
+
+def last_body(received, third, table, out_ref):
     spectrum = load_payload(received)[:, : third.shape[0] * CP]
     high, low = split(spectrum)
 
@@ -405,28 +401,38 @@
             jax.ShapeDtypeStruct((size_x, 24, LANES), F32),
         ),
         field, z_in,
-    )
+        scratch=[pltpu.VMEM(field.shape, F32), pltpu.VMEM(z_in.shape, BF16), pltpu.SemaphoreType.DMA((2,))],
+        hbm=(0, 1), vmem=FULL,
+    )
+    def make_taps(first, count, kernels):
+        body = functools.partial(taps_body, first)
+        return call(body, (taps_shape,) * count, kernels, scratch=[pltpu.VMEM((128, 384), F32)])
+
+    conv_kernels, sent = lax.optimization_barrier((conv_kernels, sent))
+    taps = make_taps(0, 1, conv_kernels)
+    grid, conv_kernels, *taps = lax.optimization_barrier((grid, conv_kernels, *taps))
     left = shift(grid, "gx", 1)
     right = shift(grid, "gx", -1)
-    taps = call(taps_body, (taps_shape,) * 3, conv_kernels, scratch=[pltpu.VMEM((128, 384), F32)])
+    taps = [*taps, *make_taps(1, 2, conv_kernels)]
     received = lax.all_to_all(sent, "gx", 0, 0, tiled=True)
+    received, *taps = lax.optimization_barrier((received, *taps))
+
+    sent = call(rows_body, jax.ShapeDtypeStruct((size_y, 24, LANES), F32), received, x_in)
+
+    left, right, _ = lax.optimization_barrier((left, right, sent))
+    received = lax.all_to_all(sent, "gy", 0, 0, tiled=True)
 
     def edge(rows):
         return jnp.concatenate([left[rows], grid[rows], right[rows]], axis=2)
 
     before = shift(edge(slice(cells_y - 3, cells_y)), "gy", 1)
     after = shift(edge(slice(0, 3)), "gy", -1)
-    sent = call(rows_body, jax.ShapeDtypeStruct((size_y, 24, LANES), F32), received, x_in)
-
-    left, sent = lax.optimization_barrier((left, sent))
-    received = lax.all_to_all(sent, "gy", 0, 0, tiled=True)
     inner = call(
         lambda *refs: inner_body(sizes, *refs),
         jax.ShapeDtypeStruct((cells_y - 2, CP, 512), F32),
         left, grid, right, place, taps[0],
-        scratch=[pltpu.VMEM((cells_y, CP, 768), F32), pltpu.VMEM((cells_y - 2, CP, 512), F32)]
-        + row_scratch + conv_scratch(768),
-        smem=(3,), hbm=(0, 1, 2, 4), out_hbm=(0,), vmem=60, flops=3 << 30,
+        scratch=[pltpu.VMEM((cells_y, CP, 768), F32)] + conv_scratch(768),
+        smem=(3,), light=False, flops=INNER << 20,
     )
     inner, received = lax.optimization_barrier((inner, received))
     weights = mix_weights.reshape(2, channels * channels, kx_local * KY)
@@ -435,18 +441,17 @@
         jax.ShapeDtypeStruct((size_y, 24, LANES), F32),
         received, weights, kept_z.reshape(1, -1), place, y_in, y_out,
         scratch=[pltpu.VMEM((cells_y * size_y * kx_local * 2, LANES), F32)]
-        + [pltpu.VMEM((LANES, kx_local * KY), F32)] * 2
-        + [pltpu.VMEM(received.shape, F32), pltpu.VMEM(weights.shape, F32), pltpu.SemaphoreType.DMA((3,))],
-        smem=(3,), hbm=(0, 1), vmem=60,
-    )
-    before, sent = lax.optimization_barrier((before, sent))
+        + [pltpu.VMEM((LANES, kx_local * KY), F32)] * 2,
+        smem=(3,), flops=30 << 30,
+    )
+    before, after, _ = lax.optimization_barrier((before, after, sent))
     received = lax.all_to_all(sent, "gy", 0, 0, tiled=True)
     outer = call(
         lambda *refs: outer_body(sizes, *refs),
         jax.ShapeDtypeStruct((8, CP, 512), F32),
         before, left, grid, right, after, place, taps[0],
-        scratch=[pltpu.VMEM((10, CP, 768), F32), pltpu.VMEM((8, CP, 512), F32)] + row_scratch + conv_scratch(768),
-        smem=(5,), hbm=(0, 1, 2, 3, 4, 6), out_hbm=(0,), vmem=60, flops=4 << 30,
+        scratch=[pltpu.VMEM((10, CP, 768), F32)] + conv_scratch(768),
+        smem=(5,), flops=4 << 30,
     )
     outer, received = lax.optimization_barrier((outer, received))
     sent = call(rows_body, jax.ShapeDtypeStruct((size_x, 24, LANES), F32), received, x_out)
@@ -459,15 +464,12 @@
         scratch=[
             pltpu.VMEM((cells_y + 4, CP, 512), F32),
             pltpu.VMEM((cells_y + 2, CP, 512), F32),
-            pltpu.VMEM((cells_y, CP, cells_x * NZ), F32),
         ]
-        + row_scratch + [pltpu.VMEM((2 * ROW, 256), BF16)] + conv_scratch(512),
-        smem=(2,), hbm=(0, 1, 3, 4), out_hbm=(0,), vmem=60, flops=8 << 30,
+        + conv_scratch(512),
+        smem=(2,), flops=8 << 30,
     )
     return call(
         last_body, jax.ShapeDtypeStruct(field.shape, F32), received, third, z_out,
-        scratch=[pltpu.VMEM(received.shape, F32), pltpu.VMEM(third.shape, F32), pltpu.SemaphoreType.DMA((2,))],
-        hbm=(0, 1), vmem=60,
     )
 
 

time: 91.6 us -> 86.6 us (0.945)
  Pallas kernels: 33 us -> 24.9 us
  local copies, waits for them, and re-layouts: 4.26 us -> 7.81 us
  other arithmetic: 0.63 us -> 1.61 us
    pallas_call x9 -> x10, Pallas kernels: 33 us -> 24.9 us  [call(): pl.pallas_call(body, out_shape=out_shape, in_specs=in_specs, out_specs=tu...]
    unnamed x30 -> x36, local copies, waits for them, and re-layouts: 4.21 us -> 7.76 us
    concatenate x2, other arithmetic: 0.05 us -> 1.54 us  [edge(): return jnp.concatenate([left[rows], grid[rows], right[rows]], axis=2)]
    ppermute x4, starting transfers between devices: 12.4 us -> 11 us  [shift(): return lax.ppermute(values, axis, pairs)]
    all_to_all x2, starting transfers between devices: 17 us -> 18.4 us  [shards(): received = lax.all_to_all(sent, 'gx', 0, 0, tiled=True)]
  transfers between devices with their start and end apart: 8 -> 8, of which waited for: 2 -> 2; matrix products, arithmetic and copies ran while one was open for 1% -> 2% of each run, Pallas kernels for 30% -> 24%
where the time goes in v3:
time: 86.6 us; the launch traced here: 85.5 us
  starting transfers between devices  41.2 us (48%)
  Pallas kernels  24.9 us (29%)
  waiting for transfers between devices  9.71 us (11%)
  local copies, waits for them, and re-layouts  7.81 us (9%)
  other arithmetic  1.61 us (2%)
    pallas_call x10, Pallas kernels, call(): pl.pallas_call(body, out_shape=out_shape, in_specs=in_specs, out_specs=tu...  24.9 us
    all_to_all x2, starting transfers between devices, shards(): received = lax.all_to_all(sent, 'gx', 0, 0, tiled=True)  18.4 us
    all_to_all x2, starting transfers between devices, shards(): received = lax.all_to_all(sent, 'gy', 0, 0, tiled=True)  11.9 us
    ppermute x4, starting transfers between devices, shift(): return lax.ppermute(values, axis, pairs)  11 us
    all_to_all x2, waiting for transfers between devices, shards(): received = lax.all_to_all(sent, 'gx', 0, 0, tiled=True)  9.7 us
    unnamed x36, local copies, waits for them, and re-layouts  7.76 us
  transfers between devices with their start and end apart: 8, of which 2 were waited for; matrix products, arithmetic and copies ran while one was open for 2% of the time, Pallas kernels for 24%

profile of v3, /device:TPU:1, one launch (start us, length us, event | category | flops | bytes accessed | tf_op | source)
XLA Modules:
  0.0 85.5 jit_solution(9519500814469245934)
XLA Ops:
  0.0 2.3 %shard_map.100 = (f32[8,40,256]{2,1,0:T(8,128)}, f32[32,24,128]{2,1,0:T(8,128)}) custom-call(f32[36,4,512]{2,1,0:T(4,128)} %field_hbm.1, bf16[2,256,256]{2,1,0:T(8,128)(2,1)} %constant.21.clone.table_hbm), custom_call_target="tpu_custom_call" | custom-call | bytes 557056 | tf_op jit(solution)/shard_map/pallas_call | solution.py:92
  2.3 12.0 %all-to-all-start = ((f32[32,24,128]{2,1,0:T(8,128)}), f32[32,24,128]{2,1,0:T(8,128)S(1)}, u32[]{:S(2)}, u32[]{:S(2)}) async-start(f32[32,24,128]{2,1,0:T(8,128)} %get-tuple-element.32), calls=%async_computation | async-start | bytes 786432 | tf_op jit(solution)/shard_map/all_to_all | solution.py:417
  14.3 1.4 %copy-done = f32[3,27,36,36]{3,2,1,0:T(8,128)S(1)} copy-done((f32[3,27,36,36]{3,2,1,0:T(8,128)S(1)}, f32[3,27,36,36]{3,2,1,0:T(8,128)}, u32[]{:S(2)}) %copy-start) | copy-done | bytes 419928
  16.1 1.4 %collective-permute-start.1 = (f32[8,40,256]{2,1,0:T(8,128)S(1)}, f32[8,40,256]{2,1,0:T(8,128)S(1)}, u32[]{:S(2)}, u32[]{:S(2)}) collective-permute-start(f32[8,40,256]{2,1,0:T(8,128)S(1)} %copy-done.3), channel_id=1, source_target_pairs={{8,0},{16,8},{24,16},{32,24},{40,32},{48,40},{56,48},{64,56},{72,6... | collective-permute-start | bytes 983048 | tf_op jit(solution)/shard_map/ppermute | solution.py:375
  17.5 4.0 %collective-permute-start = (f32[8,40,256]{2,1,0:T(8,128)S(1)}, f32[8,40,256]{2,1,0:T(8,128)S(1)}, u32[]{:S(2)}, u32[]{:S(2)}) collective-permute-start(f32[8,40,256]{2,1,0:T(8,128)S(1)} %copy-done.3), channel_id=1, source_target_pairs={{0,8},{8,16},{16,24},{24,32},{32,40},{40,48},{48,56},{56,64},{64,7... | collective-permute-start | bytes 983048 | tf_op jit(solution)/shard_map/ppermute | solution.py:375
  23.6 4.5 %all-to-all-done.received = f32[32,24,128]{2,1,0:T(8,128)S(1)} async-done(((f32[32,24,128]{2,1,0:T(8,128)}), f32[32,24,128]{2,1,0:T(8,128)S(1)}, u32[]{:S(2)}, u32[]{:S(2)}) %all-to-all-start) | async-done | bytes 393248 | tf_op jit(solution)/shard_map/all_to_all | solution.py:417
  28.1 0.9 %shard_map.103 = f32[8,24,128]{2,1,0:T(8,128)} custom-call(f32[32,24,128]{2,1,0:T(8,128)S(1)} %all-to-all-done.received, bf16[2,64,256]{2,1,0:T(8,128)(2,1)S(1)} %copy-done.5), custom_call_target="tpu_custom_call" | custom-call | bytes 458752 | tf_op jit(solution)/shard_map/pallas_call | solution.py:92
  29.0 7.0 %all-to-all-start.1 = ((f32[8,24,128]{2,1,0:T(8,128)}), f32[8,24,128]{2,1,0:T(8,128)S(1)}, u32[]{:S(2)}, u32[]{:S(2)}) async-start(f32[8,24,128]{2,1,0:T(8,128)} %shard_map.103), calls=%async_computation.1 | async-start | bytes 196608 | tf_op jit(solution)/shard_map/all_to_all | solution.py:423
  36.8 3.5 %collective-permute-start.2 = (f32[3,40,768]{2,1,0:T(8,128)}, f32[3,40,768]{2,1,0:T(8,128)}, u32[]{:S(2)}, u32[]{:S(2)}) collective-permute-start(f32[3,40,768]{2,1,0:T(8,128)} %pad_maximum_fusion), channel_id=1, source_target_pairs={{0,1},{1,2},{2,3},{3,4},{4,5},{5,6},{6,7},{8,9},{9,10},{10,11},{11... | collective-permute-start | bytes 1105928 | tf_op jit(solution)/shard_map/ppermute | solution.py:375
  41.1 2.0 %collective-permute-start.3 = (f32[3,40,768]{2,1,0:T(8,128)}, f32[3,40,768]{2,1,0:T(8,128)}, u32[]{:S(2)}, u32[]{:S(2)}) collective-permute-start(f32[3,40,768]{2,1,0:T(8,128)} %pad_maximum_fusion.1), channel_id=1, source_target_pairs={{1,0},{2,1},{3,2},{4,3},{5,4},{6,5},{7,6},{9,8},{10,9},{11,10},{12... | collective-permute-start | bytes 1105928 | tf_op jit(solution)/shard_map/ppermute | solution.py:375
  43.2 3.9 %shard_map.104.refs_0_ = f32[6,40,512]{2,1,0:T(8,128)S(1)} custom-call(f32[8,40,256]{2,1,0:T(8,128)S(1)} %collective-permute-done.refs_0_.refs_1_, f32[8,40,256]{2,1,0:T(8,128)S(1)} %copy-done.3, f32[8,40,256]{2,1,0:T(8,128)S(1)} %collective-permute-done.1.refs_2_.refs_3_, s32[2]{0:T(128)S(1)} %pad_add_fusion.refs_3_.place.refs_5_.refs_2_, ...), custom_call_target="tpu_custom_call" | custom-call | flops 1073741824 | bytes 1359880 | tf_op jit(solution)/shard_map/pallas_call | solution.py:92
  47.0 0.8 copy-done.14
  47.9 1.0 %copy-done.13 = bf16[2,256,512]{2,1,0:T(8,128)(2,1)S(1)} copy-done((bf16[2,256,512]{2,1,0:T(8,128)(2,1)S(1)}, bf16[2,256,512]{2,1,0:T(8,128)(2,1)}, u32[]{:S(2)}) %copy-start.13) | copy-done | bytes 524312
  48.9 2.5 %shard_map.105 = f32[8,24,128]{2,1,0:T(8,128)} custom-call(f32[8,24,128]{2,1,0:T(8,128)S(1)} %all-to-all-done.1.received, f32[2,1296,128]{2,1,0:T(8,128)S(1)} %bitcast.4, s32[1,128]{1,0:T(1,128)S(1)} %bitcast.5, s32[2]{0:T(128)S(1)} %pad_add_fusion.refs_3_.place.refs_5_.refs_2_, bf16[2,256,512]{2,1,0:T(8,128)(2,1)S(1)} %copy-done.13, ...), custom_call_target="tpu_custom_call" | custom-call | flops 32212254720 | bytes 2474504 | tf_op jit(solution)/shard_map/pallas_call | solution.py:92
  51.4 4.9 %all-to-all-start.2 = ((f32[8,24,128]{2,1,0:T(8,128)}), f32[8,24,128]{2,1,0:T(8,128)S(1)}, u32[]{:S(2)}, u32[]{:S(2)}) async-start(f32[8,24,128]{2,1,0:T(8,128)} %shard_map.105), calls=%async_computation.2 | async-start | bytes 196608 | tf_op jit(solution)/shard_map/all_to_all | solution.py:448
  56.3 5.3 %shard_map.106.refs_1_ = f32[8,40,512]{2,1,0:T(8,128)S(1)} custom-call(f32[3,40,768]{2,1,0:T(8,128)} %collective-permute-done.2.refs_0_, f32[8,40,256]{2,1,0:T(8,128)S(1)} %collective-permute-done.refs_0_.refs_1_, f32[8,40,256]{2,1,0:T(8,128)S(1)} %copy-done.3, f32[8,40,256]{2,1,0:T(8,128)S(1)} %collective-permute-done.1.refs_2_.refs_3_, ...), custom_call_target="tpu_custom_call" | custom-call | flops 4294967296 | bytes 2097160 | tf_op jit(solution)/shard_map/pallas_call | solution.py:92
  61.6 0.8 copy-done.16
  62.5 1.0 %shard_map.107 = f32[32,24,128]{2,1,0:T(8,128)} custom-call(f32[8,24,128]{2,1,0:T(8,128)S(1)} %all-to-all-done.2.received, bf16[2,256,64]{2,1,0:T(8,128)(2,1)S(1)} %copy-done.4), custom_call_target="tpu_custom_call" | custom-call | bytes 163840 | tf_op jit(solution)/shard_map/pallas_call | solution.py:92
  63.5 6.4 %all-to-all-start.3 = ((f32[32,24,128]{2,1,0:T(8,128)}), f32[32,24,128]{2,1,0:T(8,128)S(1)}, u32[]{:S(2)}, u32[]{:S(2)}) async-start(f32[32,24,128]{2,1,0:T(8,128)} %shard_map.107), calls=%async_computation.3 | async-start | bytes 786432 | tf_op jit(solution)/shard_map/all_to_all | solution.py:459
  69.9 1.0 %copy-done.15 = f32[6,40,512]{2,1,0:T(8,128)S(1)} copy-done((f32[6,40,512]{2,1,0:T(8,128)S(1)}, f32[6,40,512]{2,1,0:T(8,128)}, u32[]{:S(2)}) %copy-start.15) | copy-done | bytes 491544
  70.9 1.1 %copy-done.17 = f32[8,40,512]{2,1,0:T(8,128)S(1)} copy-done((f32[8,40,512]{2,1,0:T(8,128)S(1)}, f32[8,40,512]{2,1,0:T(8,128)}, u32[]{:S(2)}) %copy-start.17) | copy-done | bytes 655384
  72.0 7.1 %shard_map.108.third = f32[8,40,256]{2,1,0:T(8,128)S(1)} custom-call(f32[6,40,512]{2,1,0:T(8,128)S(1)} %copy-done.15, f32[8,40,512]{2,1,0:T(8,128)S(1)} %copy-done.17, s32[2]{0:T(128)S(1)} %pad_add_fusion.refs_3_.place.refs_5_.refs_2_, bf16[736,256]{1,0:T(8,128)(2,1)S(1)} %copy-done.8, bf16[736,256]{1,0:T(8,128)(2,1)S(1)} %copy-done.10), custom_call_target="tpu_custom_call" | custom-call | flops 8589934592 | bytes 1900552 | tf_op jit(solution)/shard_map/pallas_call | solution.py:92
  79.2 5.2 %all-to-all-done.3.received = f32[32,24,128]{2,1,0:T(8,128)S(1)} async-done(((f32[32,24,128]{2,1,0:T(8,128)}), f32[32,24,128]{2,1,0:T(8,128)S(1)}, u32[]{:S(2)}, u32[]{:S(2)}) %all-to-all-start.3) | async-done | bytes 393248 | tf_op jit(solution)/shard_map/all_to_all | solution.py:459
  84.4 1.2 %shard_map.109 = f32[36,4,512]{2,1,0:T(4,128)} custom-call(f32[32,24,128]{2,1,0:T(8,128)S(1)} %all-to-all-done.3.received, f32[8,40,256]{2,1,0:T(8,128)S(1)} %shard_map.108.third, bf16[2,256,256]{2,1,0:T(8,128)(2,1)S(1)} %copy-done.2), custom_call_target="tpu_custom_call" | custom-call | bytes 983040 | tf_op jit(solution)/shard_map/pallas_call | solution.py:92
  (43 shorter events, 4.0 us)
Async XLA Ops:
  2.3 13.8 %copy-start.3 = (f32[8,40,256]{2,1,0:T(8,128)S(1)}, f32[8,40,256]{2,1,0:T(8,128)}, u32[]{:S(2)}) copy-start(f32[8,40,256]{2,1,0:T(8,128)} %get-tuple-element.31.refs_1_.refs_2_) | copy-start | bytes 983044
  2.3 25.8 %all-to-all-start = ((f32[32,24,128]{2,1,0:T(8,128)}), f32[32,24,128]{2,1,0:T(8,128)S(1)}, u32[]{:S(2)}, u32[]{:S(2)}) async-start(f32[32,24,128]{2,1,0:T(8,128)} %get-tuple-element.32), calls=%async_computation | async-start | bytes 786432 | tf_op jit(solution)/shard_map/all_to_all | solution.py:417
  14.3 1.4 %copy-start = (f32[3,27,36,36]{3,2,1,0:T(8,128)S(1)}, f32[3,27,36,36]{3,2,1,0:T(8,128)}, u32[]{:S(2)}) copy-start(f32[3,27,36,36]{3,2,1,0:T(8,128)} %kernels.1) | copy-start | bytes 1259716
  15.8 5.8 %copy-start.1 = (f32[3,27,36,36]{3,2,1,0:T(8,128)S(1)}, f32[3,27,36,36]{3,2,1,0:T(8,128)}, u32[]{:S(2)}) copy-start(f32[3,27,36,36]{3,2,1,0:T(8,128)} %kernels.1) | copy-start | bytes 1259716
  15.8 12.4 %copy-start.5 = (bf16[2,64,256]{2,1,0:T(8,128)(2,1)S(1)}, bf16[2,64,256]{2,1,0:T(8,128)(2,1)}, u32[]{:S(2)}) copy-start(bf16[2,64,256]{2,1,0:T(8,128)(2,1)} %constant.22.clone.table) | copy-start | bytes 196612
  16.1 19.9 %collective-permute-start.1 = (f32[8,40,256]{2,1,0:T(8,128)S(1)}, f32[8,40,256]{2,1,0:T(8,128)S(1)}, u32[]{:S(2)}, u32[]{:S(2)}) collective-permute-start(f32[8,40,256]{2,1,0:T(8,128)S(1)} %copy-done.3), channel_id=1, source_target_pairs={{8,0},{16,8},{24,16},{32,24},{40,32},{48,40},{56,48},{64,56},{72,6... | collective-permute-start | bytes 983048 | tf_op jit(solution)/shard_map/ppermute | solution.py:375
  17.5 18.5 %collective-permute-start = (f32[8,40,256]{2,1,0:T(8,128)S(1)}, f32[8,40,256]{2,1,0:T(8,128)S(1)}, u32[]{:S(2)}, u32[]{:S(2)}) collective-permute-start(f32[8,40,256]{2,1,0:T(8,128)S(1)} %copy-done.3), channel_id=1, source_target_pairs={{0,8},{8,16},{16,24},{24,32},{32,40},{40,48},{48,56},{56,64},{64,7... | collective-permute-start | bytes 983048 | tf_op jit(solution)/shard_map/ppermute | solution.py:375
  29.0 18.8 %all-to-all-start.1 = ((f32[8,24,128]{2,1,0:T(8,128)}), f32[8,24,128]{2,1,0:T(8,128)S(1)}, u32[]{:S(2)}, u32[]{:S(2)}) async-start(f32[8,24,128]{2,1,0:T(8,128)} %shard_map.103), calls=%async_computation.1 | async-start | bytes 196608 | tf_op jit(solution)/shard_map/all_to_all | solution.py:423
  36.8 19.5 %collective-permute-start.2 = (f32[3,40,768]{2,1,0:T(8,128)}, f32[3,40,768]{2,1,0:T(8,128)}, u32[]{:S(2)}, u32[]{:S(2)}) collective-permute-start(f32[3,40,768]{2,1,0:T(8,128)} %pad_maximum_fusion), channel_id=1, source_target_pairs={{0,1},{1,2},{2,3},{3,4},{4,5},{5,6},{6,7},{8,9},{9,10},{10,11},{11... | collective-permute-start | bytes 1105928 | tf_op jit(solution)/shard_map/ppermute | solution.py:375
  41.1 6.8 %copy-start.6 = (f32[2,36,36,1,128]{4,3,2,1,0:T(1,128)S(1)}, f32[2,36,36,1,128]{4,3,2,1,0:T(1,128)}, u32[]{:S(2)}) copy-start(f32[2,36,36,1,128]{4,3,2,1,0:T(1,128)} %param.11) | copy-start | bytes 3981316
  41.1 6.8 %copy-start.11 = (s32[128]{0:T(128)S(1)}, s32[128]{0:T(128)}, u32[]{:S(2)}) copy-start(s32[128]{0:T(128)} %param.12) | copy-start | bytes 1540
  41.1 6.8 %copy-start.12 = (bf16[2,512,256]{2,1,0:T(8,128)(2,1)S(1)}, bf16[2,512,256]{2,1,0:T(8,128)(2,1)}, u32[]{:S(2)}) copy-start(bf16[2,512,256]{2,1,0:T(8,128)(2,1)} %constant.24.clone.y_out) | copy-start | bytes 1572868
  41.1 15.2 %collective-permute-start.3 = (f32[3,40,768]{2,1,0:T(8,128)}, f32[3,40,768]{2,1,0:T(8,128)}, u32[]{:S(2)}, u32[]{:S(2)}) collective-permute-start(f32[3,40,768]{2,1,0:T(8,128)} %pad_maximum_fusion.1), channel_id=1, source_target_pairs={{1,0},{2,1},{3,2},{4,3},{5,4},{6,5},{7,6},{9,8},{10,9},{11,10},{12... | collective-permute-start | bytes 1105928 | tf_op jit(solution)/shard_map/ppermute | solution.py:375
  47.0 0.8 copy-start.14
  47.9 1.0 %copy-start.13 = (bf16[2,256,512]{2,1,0:T(8,128)(2,1)S(1)}, bf16[2,256,512]{2,1,0:T(8,128)(2,1)}, u32[]{:S(2)}) copy-start(bf16[2,256,512]{2,1,0:T(8,128)(2,1)} %constant.23.clone.y_in) | copy-start | bytes 1572868
  51.4 11.1 %all-to-all-start.2 = ((f32[8,24,128]{2,1,0:T(8,128)}), f32[8,24,128]{2,1,0:T(8,128)S(1)}, u32[]{:S(2)}, u32[]{:S(2)}) async-start(f32[8,24,128]{2,1,0:T(8,128)} %shard_map.105), calls=%async_computation.2 | async-start | bytes 196608 | tf_op jit(solution)/shard_map/all_to_all | solution.py:448
  56.3 6.2 %copy-start.4 = (bf16[2,256,64]{2,1,0:T(8,128)(2,1)S(1)}, bf16[2,256,64]{2,1,0:T(8,128)(2,1)}, u32[]{:S(2)}) copy-start(bf16[2,256,64]{2,1,0:T(8,128)(2,1)} %constant.25.clone.table) | copy-start | bytes 196612
  56.3 13.6 %copy-start.8 = (bf16[736,256]{1,0:T(8,128)(2,1)S(1)}, bf16[736,256]{1,0:T(8,128)(2,1)}, u32[]{:S(2)}) copy-start(bf16[736,256]{1,0:T(8,128)(2,1)} %copy-done.7) | copy-start | bytes 1130500
  56.3 13.6 %copy-start.10 = (bf16[736,256]{1,0:T(8,128)(2,1)S(1)}, bf16[736,256]{1,0:T(8,128)(2,1)}, u32[]{:S(2)}) copy-start(bf16[736,256]{1,0:T(8,128)(2,1)} %copy-done.9) | copy-start | bytes 1130500
  61.6 0.9 %copy-start.16 = (f32[8,40,512]{2,1,0:T(8,128)}, f32[8,40,512]{2,1,0:T(8,128)S(1)}, u32[]{:S(2)}) copy-start(f32[8,40,512]{2,1,0:T(8,128)S(1)} %shard_map.106.refs_1_) | copy-start | bytes 1966084
  63.5 20.8 %all-to-all-start.3 = ((f32[32,24,128]{2,1,0:T(8,128)}), f32[32,24,128]{2,1,0:T(8,128)S(1)}, u32[]{:S(2)}, u32[]{:S(2)}) async-start(f32[32,24,128]{2,1,0:T(8,128)} %shard_map.107), calls=%async_computation.3 | async-start | bytes 786432 | tf_op jit(solution)/shard_map/all_to_all | solution.py:459
  69.9 1.0 %copy-start.15 = (f32[6,40,512]{2,1,0:T(8,128)S(1)}, f32[6,40,512]{2,1,0:T(8,128)}, u32[]{:S(2)}) copy-start(f32[6,40,512]{2,1,0:T(8,128)} %copy-done.14) | copy-start | bytes 1474564
  70.9 1.1 %copy-start.17 = (f32[8,40,512]{2,1,0:T(8,128)S(1)}, f32[8,40,512]{2,1,0:T(8,128)}, u32[]{:S(2)}) copy-start(f32[8,40,512]{2,1,0:T(8,128)} %copy-done.16) | copy-start | bytes 1966084
  72.0 12.3 %copy-start.2 = (bf16[2,256,256]{2,1,0:T(8,128)(2,1)S(1)}, bf16[2,256,256]{2,1,0:T(8,128)(2,1)}, u32[]{:S(2)}) copy-start(bf16[2,256,256]{2,1,0:T(8,128)(2,1)} %constant.26.clone.table) | copy-start | bytes 786436
  (2 other events, 1.5 us)

commit v4 on v3

--- a/solution.py
+++ b/solution.py
@@ -1,4 +1,3 @@
-import functools
 import math
 
 import jax
@@ -13,6 +12,7 @@
 NZ = 64
 KY = 32
 INNER = 1024
+OUTER = 1024
 FULL = 60
 CP = 40
 LANES = 128
@@ -79,7 +79,13 @@
     y_in = y_in.reshape(2 * kx_local * KY, -1)
     y_out = np.einsum("pqlsy,jk->ysjpqkl", plus_y.reshape(shape), eye_j)
     y_out = y_out.reshape(cells_y * size_y * kx_local * 2, -1)
-    return [split_table(t) for t in (z_in, x_in, y_in, y_out, x_out, z_out)]
+    z_in_4 = parts.reshape(modes_z * 2, -1) * scale_in
+    z_out_4 = (parts * weight).reshape(modes_z * 2, -1)
+    x_in_4 = minus_x.reshape(2, 2, modes_x, size_x, cells_x).transpose(4, 2, 0, 3, 1)
+    x_in_4 = x_in_4.reshape(cells_x * modes_x * 2, -1)
+    x_out_4 = plus_x.reshape(2, 2, modes_x, size_x, cells_x).transpose(4, 3, 0, 2, 1)
+    x_out_4 = x_out_4.reshape(cells_x * size_x * 2, -1)
+    return [split_table(t) for t in (z_in, x_in, y_in, y_out, x_out, z_out, z_in_4, x_in_4, x_out_4, z_out_4)]
 
 
 def call(body, out_shape, *args, scratch=(), flops=0, smem=(), hbm=(), out_hbm=(), vmem=24, light=False):
@@ -112,6 +118,25 @@
         copy.wait()
 
 
+MAIN = 32
+
+
+def store_packed(ref, main, last):
+    count = ref.shape[0]
+    for tile in range(2):
+        block = main[:, LANES * tile : LANES * tile + LANES]
+        ref[:, 8 * tile : 8 * tile + 8, :] = block.reshape(count, 8, LANES)
+    for dest in range(count):
+        ref[dest, 16:18, :] = last[2 * dest : 2 * dest + 2]
+
+
+def load_packed(ref, last):
+    count = ref.shape[0]
+    for source in range(count):
+        last[2 * source : 2 * source + 2, :] = ref[source, 16:18, :]
+    return jnp.concatenate([ref[:, 8 * t : 8 * t + 8, :].reshape(count * 8, LANES) for t in range(2)], axis=1)
+
+
 def store_payload(ref, rows):
     count = ref.shape[0]
     for tile in range(3):
@@ -128,7 +153,7 @@
     return jnp.concatenate(tiles, axis=1)
 
 
-def z_in_body(field_hbm, table_hbm, grid_ref, out_ref, field, table, sems):
+def z_in_body(field_hbm, table_hbm, table_4, grid_ref, out_ref, field, table, sems, last):
     arrived = copies([(field_hbm, field), (table_hbm, table)], sems)
     wait(arrived[:1])
     channels, cells_x, width = field.shape
@@ -137,16 +162,31 @@
         piece = jnp.concatenate([piece, jnp.zeros((CP - channels, width), F32)], axis=0)
         for y in range(width // NZ):
             grid_ref[y, :, NZ * x : NZ * x + NZ] = piece[:, NZ * y : NZ * y + NZ]
-    cells = grid_ref[...].reshape(-1, grid_ref.shape[2])
+            spot = 4 * ((width // NZ) * x + y)
+            last[spot : spot + 4, :] = piece[MAIN:channels, NZ * y : NZ * y + NZ]
+    cells = grid_ref[:, :MAIN, :].reshape(-1, grid_ref.shape[2])
     wait(arrived[1:])
-    store_payload(out_ref, product(table, cells, ((1,), (1,))))
-
-
-def rows_body(received, table, out_ref):
-    rows = product(table, load_payload(received), ((1,), (0,)))
-    for tile in range(3):
-        block = rows[:, LANES * tile : LANES * tile + LANES]
-        out_ref[:, 8 * tile : 8 * tile + 8, :] = block.reshape(out_ref.shape[0], 8, LANES)
+    main = product(table, cells, ((1,), (1,)))
+    store_packed(out_ref, main, product(table_4, last[...], ((1,), (1,))))
+
+
+def x_in_body(received, table, table_4, out_ref, last):
+    main = product(table, load_packed(received, last), ((1,), (0,)))
+    turned = product(table_4, last[...], ((1,), (0,)))
+    rows = main.shape[0]
+    rest = turned[:rows, :32]
+    for x in range(1, 4):
+        rest = rest + turned[rows * x : rows * x + rows, 32 * x : 32 * x + 32]
+    store_payload(out_ref, jnp.concatenate([main, rest], axis=1))
+
+
+def x_out_body(received, table, table_4, out_ref):
+    rows = load_payload(received)
+    main = product(table, rows[:, :256], ((1,), (0,)))
+    turned = product(table_4, rows[:, 256:], ((1,), (0,)))
+    count = turned.shape[0] // 4
+    last = jnp.concatenate([turned[count * x : count * x + count, :32] for x in range(4)], axis=1)
+    store_packed(out_ref, main, last)
 
 
 def mix_body(received, weights, kept, place, y_in, y_out, out_ref, stacked, s_re, s_im):
@@ -154,8 +194,10 @@
     rows = load_payload(received)
     block = rows.shape[0]
     for y in range(cells_y):
-        stacked[y * block : (y + 1) * block, :CP] = rows[:, CP * y : CP * y + CP]
-        stacked[y * block : (y + 1) * block, CP:] = jnp.zeros((block, LANES - CP), F32)
+        own = slice(y * block, (y + 1) * block)
+        stacked[own, :MAIN] = rows[:, MAIN * y : MAIN * y + MAIN]
+        stacked[own, MAIN : MAIN + 4] = rows[:, MAIN * cells_y + 4 * y : MAIN * cells_y + 4 * y + 4]
+        stacked[own, MAIN + 4 :] = jnp.zeros((block, LANES - MAIN - 4), F32)
     modes = product(y_in, stacked[...], ((1,), (0,)))
     count = modes.shape[0] // 2
     s_re[...] = modes[:count].T
@@ -186,7 +228,9 @@
 
     mixed = jnp.concatenate([fold(total_re), fold(total_im)], axis=1)
     back = product(y_out, mixed, ((1,), (1,)))
-    lanes = jnp.concatenate([back[y * block : (y + 1) * block] for y in range(cells_y)], axis=1)
+    pieces = [back[y * block : (y + 1) * block] for y in range(cells_y)]
+    lanes = [piece[:, :MAIN] for piece in pieces] + [piece[:, MAIN : MAIN + 4] for piece in pieces]
+    lanes = jnp.concatenate(lanes, axis=1)
     store_payload(out_ref, lanes)
 
 
@@ -197,14 +241,14 @@
 ROW = 368
 
 
-def taps_body(first, kernels, *refs):
+def taps_body(kernels, after, *refs):
     channels = kernels.shape[2]
     *outs, scratch = refs
     for r, out_ref in enumerate(outs):
         scratch[...] = jnp.zeros(scratch.shape, F32)
         for tap in range(27):
             row, lane = CP * (tap % 3), CP * (tap // 3)
-            scratch[row : row + channels, lane : lane + channels] = kernels[first + r, tap]
+            scratch[row : row + channels, lane : lane + channels] = kernels[r, tap]
         high, low = split(scratch[...].T[:ROW])
         out_ref[:ROW, :128] = high
         out_ref[:ROW, 128:] = high
@@ -354,15 +398,26 @@
     convolve_rows(lambda i: second[i], count + 4, 512, taps_2, refs, finish_third)
 
 
-def last_body(received, third, table, out_ref):
-    spectrum = load_payload(received)[:, : third.shape[0] * CP]
-    high, low = split(spectrum)
-
-    def dot(left, right):
-        return lax.dot_general(left, right, (((0,), (0,)), ((), ())), preferred_element_type=F32)
-
-    spectral = dot(high, table[0]) + dot(low, table[0]) + dot(high, table[1])
-    out = gelu_exact(spectral.reshape(third.shape) + third[...])
+def last_body(received, third, table, table_4, out_ref, last, spectral):
+    spectrum = load_packed(received, last)
+    cells_y = third.shape[0]
+
+    def turn(values, factors):
+        high, low = split(values)
+
+        def dot(left, right):
+            return lax.dot_general(left, right, (((0,), (0,)), ((), ())), preferred_element_type=F32)
+
+        return dot(high, factors[0]) + dot(low, factors[0]) + dot(high, factors[1])
+
+    spectral[:, :MAIN, :] = turn(spectrum, table).reshape(cells_y, MAIN, -1)
+    spectral[:, MAIN:, :] = jnp.zeros((cells_y, CP - MAIN, spectral.shape[2]), F32)
+    rest = turn(last[...], table_4)
+    for x in range(4):
+        for y in range(cells_y):
+            spot = 4 * (cells_y * x + y)
+            spectral[y, MAIN : MAIN + 4, NZ * x : NZ * x + NZ] = rest[spot : spot + 4]
+    out = gelu_exact(spectral[...] + third[...])
     channels, cells_x, width = out_ref.shape
     for x in range(cells_x):
         piece = [out[y, :channels, NZ * x : NZ * x + NZ] for y in range(width // NZ)]
@@ -386,38 +441,37 @@
     kx_local = mix_weights.shape[4] // KY
     modes_x = kx_local * size_y
     place = jnp.stack([lax.axis_index("gx"), lax.axis_index("gy")]).astype(jnp.int32)
-    z_in, x_in, y_in, y_out, x_out, z_out = [
+    z_in, x_in, y_in, y_out, x_out, z_out, z_in_4, x_in_4, x_out_4, z_out_4 = [
         jnp.asarray(t) for t in tables(size_x, size_y, cells_x, cells_y, modes_x, modes_z)
     ]
 
     sizes = (cells_x, cells_y, full_x, full_y)
-    row_scratch = [pltpu.SemaphoreType.DMA((9,)), pltpu.VMEM((2 * ROW, 256), BF16)]
     taps_shape = jax.ShapeDtypeStruct((2 * ROW, 256), BF16)
 
     grid, sent = call(
         z_in_body,
         (
             jax.ShapeDtypeStruct((cells_y, CP, cells_x * NZ), F32),
-            jax.ShapeDtypeStruct((size_x, 24, LANES), F32),
+            jax.ShapeDtypeStruct((size_x, 18, LANES), F32),
         ),
-        field, z_in,
-        scratch=[pltpu.VMEM(field.shape, F32), pltpu.VMEM(z_in.shape, BF16), pltpu.SemaphoreType.DMA((2,))],
+        field, z_in, z_in_4,
+        scratch=[pltpu.VMEM(field.shape, F32), pltpu.VMEM(z_in.shape, BF16), pltpu.SemaphoreType.DMA((2,)),
+                 pltpu.VMEM((LANES, NZ), F32)],
         hbm=(0, 1), vmem=FULL,
     )
-    def make_taps(first, count, kernels):
-        body = functools.partial(taps_body, first)
-        return call(body, (taps_shape,) * count, kernels, scratch=[pltpu.VMEM((128, 384), F32)])
-
-    conv_kernels, sent = lax.optimization_barrier((conv_kernels, sent))
-    taps = make_taps(0, 1, conv_kernels)
-    grid, conv_kernels, *taps = lax.optimization_barrier((grid, conv_kernels, *taps))
     left = shift(grid, "gx", 1)
     right = shift(grid, "gx", -1)
-    taps = [*taps, *make_taps(1, 2, conv_kernels)]
+    after, _ = lax.optimization_barrier((place, sent))
+    taps = call(
+        taps_body, (taps_shape,) * 3, conv_kernels, after, scratch=[pltpu.VMEM((128, 384), F32)], smem=(1,)
+    )
     received = lax.all_to_all(sent, "gx", 0, 0, tiled=True)
     received, *taps = lax.optimization_barrier((received, *taps))
 
-    sent = call(rows_body, jax.ShapeDtypeStruct((size_y, 24, LANES), F32), received, x_in)
+    sent = call(
+        x_in_body, jax.ShapeDtypeStruct((size_y, 24, LANES), F32), received, x_in, x_in_4,
+        scratch=[pltpu.VMEM((2 * size_x, LANES), F32)],
+    )
 
     left, right, _ = lax.optimization_barrier((left, right, sent))
     received = lax.all_to_all(sent, "gy", 0, 0, tiled=True)
@@ -442,7 +496,7 @@
         received, weights, kept_z.reshape(1, -1), place, y_in, y_out,
         scratch=[pltpu.VMEM((cells_y * size_y * kx_local * 2, LANES), F32)]
         + [pltpu.VMEM((LANES, kx_local * KY), F32)] * 2,
-        smem=(3,), flops=30 << 30,
+        smem=(3,), flops=8 << 30,
     )
     before, after, _ = lax.optimization_barrier((before, after, sent))
     received = lax.all_to_all(sent, "gy", 0, 0, tiled=True)
@@ -451,10 +505,10 @@
         jax.ShapeDtypeStruct((8, CP, 512), F32),
         before, left, grid, right, after, place, taps[0],
         scratch=[pltpu.VMEM((10, CP, 768), F32)] + conv_scratch(768),
-        smem=(5,), flops=4 << 30,
+        smem=(5,), flops=OUTER << 20,
     )
     outer, received = lax.optimization_barrier((outer, received))
-    sent = call(rows_body, jax.ShapeDtypeStruct((size_x, 24, LANES), F32), received, x_out)
+    sent = call(x_out_body, jax.ShapeDtypeStruct((size_x, 18, LANES), F32), received, x_out, x_out_4)
     outer, sent = lax.optimization_barrier((outer, sent))
     received = lax.all_to_all(sent, "gx", 0, 0, tiled=True)
     third = call(
@@ -469,7 +523,8 @@
         smem=(2,), flops=8 << 30,
     )
     return call(
-        last_body, jax.ShapeDtypeStruct(field.shape, F32), received, third, z_out,
+        last_body, jax.ShapeDtypeStruct(field.shape, F32), received, third, z_out, z_out_4,
+        scratch=[pltpu.VMEM((2 * size_x, LANES), F32), pltpu.VMEM(third.shape, F32)],
     )
 
 

time: 86.6 us -> 88.2 us (1.018)
  waiting for transfers between devices: 9.71 us -> 11.8 us
  starting transfers between devices: 41.2 us -> 39.4 us
  Pallas kernels: 24.9 us -> 26.3 us
    all_to_all x2, waiting for transfers between devices: 9.7 us -> 11.8 us  [shards(): received = lax.all_to_all(sent, 'gx', 0, 0, tiled=True)]
    all_to_all x2, starting transfers between devices: 18.4 us -> 16.7 us  [shards(): received = lax.all_to_all(sent, 'gx', 0, 0, tiled=True)]
    pallas_call x10 -> x9, Pallas kernels: 24.9 us -> 26.3 us  [call(): pl.pallas_call(body, out_shape=out_shape, in_specs=in_specs, out_specs=tu...]
    unnamed x36 -> x42, local copies, waits for them, and re-layouts: 7.76 us -> 8.31 us
  transfers between devices with their start and end apart: 8 -> 8, of which waited for: 2 -> 2; matrix products, arithmetic and copies ran while one was open for 2% -> 1% of each run, Pallas kernels for 24% -> 24%
where the time goes in v4:
time: 88.2 us; the launch traced here: 87 us
  starting transfers between devices  39.4 us (45%)
  Pallas kernels  26.3 us (30%)
  waiting for transfers between devices  11.8 us (13%)
  local copies, waits for them, and re-layouts  8.36 us (9%)
    pallas_call x9, Pallas kernels, call(): pl.pallas_call(body, out_shape=out_shape, in_specs=in_specs, out_specs=tu...  26.3 us
    all_to_all x2, starting transfers between devices, shards(): received = lax.all_to_all(sent, 'gx', 0, 0, tiled=True)  16.7 us
    all_to_all x2, starting transfers between devices, shards(): received = lax.all_to_all(sent, 'gy', 0, 0, tiled=True)  11.9 us
    all_to_all x2, waiting for transfers between devices, shards(): received = lax.all_to_all(sent, 'gx', 0, 0, tiled=True)  11.8 us
    ppermute x4, starting transfers between devices, shift(): return lax.ppermute(values, axis, pairs)  10.9 us
    unnamed x42, local copies, waits for them, and re-layouts  8.31 us
  transfers between devices with their start and end apart: 8, of which 2 were waited for; matrix products, arithmetic and copies ran while one was open for 1% of the time, Pallas kernels for 24%

profile of v4, /device:TPU:1, one launch (start us, length us, event | category | flops | bytes accessed | tf_op | source)
XLA Modules:
  0.0 87.0 jit_solution(5429238505160262429)
XLA Ops:
  0.0 3.1 %shard_map.136 = (f32[8,40,256]{2,1,0:T(8,128)}, f32[32,18,128]{2,1,0:T(8,128)}) custom-call(f32[36,4,512]{2,1,0:T(4,128)} %field_hbm.1, bf16[2,256,256]{2,1,0:T(8,128)(2,1)} %constant.29.clone.table_hbm, bf16[2,64,64]{2,1,0:T(8,128)(2,1)} %constant.35.clone.table_4), custom_call_target="tpu_custom_call" | custom-call | bytes 573440 | tf_op jit(solution)/shard_map/pallas_call | solution.py:98
  3.1 12.0 %all-to-all-start = ((f32[32,18,128]{2,1,0:T(8,128)}), f32[32,18,128]{2,1,0:T(8,128)S(1)}, u32[]{:S(2)}, u32[]{:S(2)}) async-start(f32[32,18,128]{2,1,0:T(8,128)} %get-tuple-element.26), calls=%async_computation | async-start | bytes 786432 | tf_op jit(solution)/shard_map/all_to_all | solution.py:468
  15.1 1.3 %collective-permute-start.1 = (f32[8,40,256]{2,1,0:T(8,128)}, f32[8,40,256]{2,1,0:T(8,128)S(1)}, u32[]{:S(2)}, u32[]{:S(2)}) collective-permute-start(f32[8,40,256]{2,1,0:T(8,128)} %get-tuple-element.25.refs_1_.refs_2_), channel_id=1, source_target_pairs={{8,0},{16,8},{24,16},{32,24},{40,32},{48,40},{56,48},{64,56},{72,6... | collective-permute-start | bytes 983048 | tf_op jit(solution)/shard_map/ppermute | solution.py:430
  16.4 4.0 %collective-permute-start = (f32[8,40,256]{2,1,0:T(8,128)}, f32[8,40,256]{2,1,0:T(8,128)S(1)}, u32[]{:S(2)}, u32[]{:S(2)}) collective-permute-start(f32[8,40,256]{2,1,0:T(8,128)} %get-tuple-element.25.refs_1_.refs_2_), channel_id=1, source_target_pairs={{0,8},{8,16},{16,24},{24,32},{32,40},{40,48},{48,56},{56,64},{64,7... | collective-permute-start | bytes 983048 | tf_op jit(solution)/shard_map/ppermute | solution.py:430
  20.5 1.4 %copy-done = f32[3,27,36,36]{3,2,1,0:T(8,128)S(1)} copy-done((f32[3,27,36,36]{3,2,1,0:T(8,128)S(1)}, f32[3,27,36,36]{3,2,1,0:T(8,128)}, u32[]{:S(2)}) %copy-start) | copy-done | bytes 419928
  21.9 1.2 %shard_map.137 = (bf16[736,256]{1,0:T(8,128)(2,1)S(1)}, bf16[736,256]{1,0:T(8,128)(2,1)S(1)}, bf16[736,256]{1,0:T(8,128)(2,1)S(1)}) custom-call(f32[3,27,36,36]{3,2,1,0:T(8,128)S(1)} %copy-done, s32[2]{0:T(128)S(1)} %pad_add_fusion.after.refs_3_.place.refs_5_.refs_2_), custom_call_target="tpu_custom_call" | custom-call | bytes 419912 | tf_op jit(solution)/shard_map/pallas_call | solution.py:98
  23.2 5.7 %all-to-all-done.received = f32[32,18,128]{2,1,0:T(8,128)S(1)} async-done(((f32[32,18,128]{2,1,0:T(8,128)}), f32[32,18,128]{2,1,0:T(8,128)S(1)}, u32[]{:S(2)}, u32[]{:S(2)}) %all-to-all-start) | async-done | bytes 294944 | tf_op jit(solution)/shard_map/all_to_all | solution.py:468
  29.9 7.0 %all-to-all-start.1 = ((f32[8,24,128]{2,1,0:T(8,128)}), f32[8,24,128]{2,1,0:T(8,128)S(1)}, u32[]{:S(2)}, u32[]{:S(2)}) async-start(f32[8,24,128]{2,1,0:T(8,128)} %shard_map.138), calls=%async_computation.1 | async-start | bytes 196608 | tf_op jit(solution)/shard_map/all_to_all | solution.py:477
  36.9 3.5 %collective-permute-start.2 = (f32[3,40,768]{2,1,0:T(8,128)S(1)}, f32[3,40,768]{2,1,0:T(8,128)}, u32[]{:S(2)}, u32[]{:S(2)}) collective-permute-start(f32[3,40,768]{2,1,0:T(8,128)S(1)} %pad_maximum_fusion), channel_id=1, source_target_pairs={{0,1},{1,2},{2,3},{3,4},{4,5},{5,6},{6,7},{8,9},{9,10},{10,11},{11... | collective-permute-start | bytes 1105928 | tf_op jit(solution)/shard_map/ppermute | solution.py:430
  41.3 2.0 %collective-permute-start.3 = (f32[3,40,768]{2,1,0:T(8,128)}, f32[3,40,768]{2,1,0:T(8,128)}, u32[]{:S(2)}, u32[]{:S(2)}) collective-permute-start(f32[3,40,768]{2,1,0:T(8,128)} %pad_maximum_fusion.1), channel_id=1, source_target_pairs={{1,0},{2,1},{3,2},{4,3},{5,4},{6,5},{7,6},{9,8},{10,9},{11,10},{12... | collective-permute-start | bytes 1105928 | tf_op jit(solution)/shard_map/ppermute | solution.py:430
  43.3 1.0 %copy-done.12 = bf16[736,256]{1,0:T(8,128)(2,1)S(1)} copy-done((bf16[736,256]{1,0:T(8,128)(2,1)S(1)}, bf16[736,256]{1,0:T(8,128)(2,1)}, u32[]{:S(2)}) %copy-start.12) | copy-done | bytes 376856
  44.3 3.8 %shard_map.139.refs_0_ = f32[6,40,512]{2,1,0:T(8,128)S(1)} custom-call(f32[8,40,256]{2,1,0:T(8,128)S(1)} %collective-permute-done.refs_0_.refs_1_, f32[8,40,256]{2,1,0:T(8,128)S(1)} %copy-done.2, f32[8,40,256]{2,1,0:T(8,128)S(1)} %collective-permute-done.1.refs_2_.refs_3_, s32[2]{0:T(128)S(1)} %pad_add_fusion.after.refs_3_.place.refs_5_.refs_2_, ...), custom_call_target="tpu_custom_call" | custom-call | flops 1073741824 | bytes 1359880 | tf_op jit(solution)/shard_map/pallas_call | solution.py:98
  48.9 1.0 %copy-done.15 = bf16[2,512,256]{2,1,0:T(8,128)(2,1)S(1)} copy-done((bf16[2,512,256]{2,1,0:T(8,128)(2,1)S(1)}, bf16[2,512,256]{2,1,0:T(8,128)(2,1)}, u32[]{:S(2)}) %copy-start.15) | copy-done | bytes 524312
  50.0 1.0 %copy-done.16 = bf16[2,256,512]{2,1,0:T(8,128)(2,1)S(1)} copy-done((bf16[2,256,512]{2,1,0:T(8,128)(2,1)S(1)}, bf16[2,256,512]{2,1,0:T(8,128)(2,1)}, u32[]{:S(2)}) %copy-start.16) | copy-done | bytes 524312
  51.0 2.5 %shard_map.140 = f32[8,24,128]{2,1,0:T(8,128)} custom-call(f32[8,24,128]{2,1,0:T(8,128)S(1)} %all-to-all-done.1.received, f32[2,1296,128]{2,1,0:T(8,128)S(1)} %bitcast.4, s32[1,128]{1,0:T(1,128)S(1)} %bitcast.5, s32[2]{0:T(128)S(1)} %pad_add_fusion.after.refs_3_.place.refs_5_.refs_2_, bf16[2,256,512]{2,1,0:T(8,128)(2,1)S(1)} %copy-done.16, ...), custom_call_target="tpu_custom_call" | custom-call | flops 8589934592 | bytes 2474504 | tf_op jit(solution)/shard_map/pallas_call | solution.py:98
  53.5 4.9 %all-to-all-start.2 = ((f32[8,24,128]{2,1,0:T(8,128)}), f32[8,24,128]{2,1,0:T(8,128)S(1)}, u32[]{:S(2)}, u32[]{:S(2)}) async-start(f32[8,24,128]{2,1,0:T(8,128)} %shard_map.140), calls=%async_computation.2 | async-start | bytes 196608 | tf_op jit(solution)/shard_map/all_to_all | solution.py:502
  58.5 1.0 %copy-done.13 = bf16[736,256]{1,0:T(8,128)(2,1)S(1)} copy-done((bf16[736,256]{1,0:T(8,128)(2,1)S(1)}, bf16[736,256]{1,0:T(8,128)(2,1)}, u32[]{:S(2)}) %copy-start.13) | copy-done | bytes 376856
  59.5 5.2 %shard_map.141.refs_1_ = f32[8,40,512]{2,1,0:T(8,128)S(1)} custom-call(f32[3,40,768]{2,1,0:T(8,128)} %collective-permute-done.2.refs_0_, f32[8,40,256]{2,1,0:T(8,128)S(1)} %collective-permute-done.refs_0_.refs_1_, f32[8,40,256]{2,1,0:T(8,128)S(1)} %copy-done.2, f32[8,40,256]{2,1,0:T(8,128)S(1)} %collective-permute-done.1.refs_2_.refs_3_, ...), custom_call_target="tpu_custom_call" | custom-call | flops 1073741824 | bytes 2097160 | tf_op jit(solution)/shard_map/pallas_call | solution.py:98
  65.6 1.1 %shard_map.142 = f32[32,18,128]{2,1,0:T(8,128)} custom-call(f32[8,24,128]{2,1,0:T(8,128)S(1)} %all-to-all-done.2.received, bf16[2,256,64]{2,1,0:T(8,128)(2,1)S(1)} %copy-done.4, bf16[2,256,64]{2,1,0:T(8,128)(2,1)S(1)} %copy-done.3), custom_call_target="tpu_custom_call" | custom-call | bytes 229376 | tf_op jit(solution)/shard_map/pallas_call | solution.py:98
  66.7 4.7 %all-to-all-start.3 = ((f32[32,18,128]{2,1,0:T(8,128)}), f32[32,18,128]{2,1,0:T(8,128)S(1)}, u32[]{:S(2)}, u32[]{:S(2)}) async-start(f32[32,18,128]{2,1,0:T(8,128)} %shard_map.142), calls=%async_computation.3 | async-start | bytes 786432 | tf_op jit(solution)/shard_map/all_to_all | solution.py:513
  71.4 1.1 %copy-done.18 = f32[8,40,512]{2,1,0:T(8,128)S(1)} copy-done((f32[8,40,512]{2,1,0:T(8,128)S(1)}, f32[8,40,512]{2,1,0:T(8,128)}, u32[]{:S(2)}) %copy-start.18) | copy-done | bytes 655384
  72.5 7.2 %shard_map.143.third = f32[8,40,256]{2,1,0:T(8,128)S(1)} custom-call(f32[6,40,512]{2,1,0:T(8,128)S(1)} %copy-done.20, f32[8,40,512]{2,1,0:T(8,128)S(1)} %copy-done.18, s32[2]{0:T(128)S(1)} %pad_add_fusion.after.refs_3_.place.refs_5_.refs_2_, bf16[736,256]{1,0:T(8,128)(2,1)S(1)} %get-tuple-element.43.refs_3_, bf16[736,256]{1,0:T(8,128)(2,1)S(1)} %copy-done.10), custom_call_target="tpu_custom_call" | custom-call | flops 8589934592 | bytes 1900552 | tf_op jit(solution)/shard_map/pallas_call | solution.py:98
  79.7 6.1 %all-to-all-done.3.received = f32[32,18,128]{2,1,0:T(8,128)S(1)} async-done(((f32[32,18,128]{2,1,0:T(8,128)}), f32[32,18,128]{2,1,0:T(8,128)S(1)}, u32[]{:S(2)}, u32[]{:S(2)}) %all-to-all-start.3) | async-done | bytes 294944 | tf_op jit(solution)/shard_map/all_to_all | solution.py:513
  85.8 1.2 %shard_map.144 = f32[36,4,512]{2,1,0:T(4,128)} custom-call(f32[32,18,128]{2,1,0:T(8,128)S(1)} %all-to-all-done.3.received, f32[8,40,256]{2,1,0:T(8,128)S(1)} %shard_map.143.third, bf16[2,256,256]{2,1,0:T(8,128)(2,1)S(1)} %copy-done.1, bf16[2,64,64]{2,1,0:T(8,128)(2,1)S(1)} %copy-done.7), custom_call_target="tpu_custom_call" | custom-call | bytes 901120 | tf_op jit(solution)/shard_map/pallas_call | solution.py:98
  (48 shorter events, 3.6 us)
Async XLA Ops:
  0.0 28.9 %copy-start.5 = (bf16[2,256,64]{2,1,0:T(8,128)(2,1)S(1)}, bf16[2,256,64]{2,1,0:T(8,128)(2,1)}, u32[]{:S(2)}) copy-start(bf16[2,256,64]{2,1,0:T(8,128)(2,1)} %constant.36.clone.table_4) | copy-start | bytes 196612
  0.0 28.9 %copy-start.6 = (bf16[2,64,256]{2,1,0:T(8,128)(2,1)S(1)}, bf16[2,64,256]{2,1,0:T(8,128)(2,1)}, u32[]{:S(2)}) copy-start(bf16[2,64,256]{2,1,0:T(8,128)(2,1)} %constant.30.clone.table) | copy-start | bytes 196612
  3.1 20.1 %copy-start.2 = (f32[8,40,256]{2,1,0:T(8,128)S(1)}, f32[8,40,256]{2,1,0:T(8,128)}, u32[]{:S(2)}) copy-start(f32[8,40,256]{2,1,0:T(8,128)} %get-tuple-element.25.refs_1_.refs_2_) | copy-start | bytes 983044
  3.1 25.8 %all-to-all-start = ((f32[32,18,128]{2,1,0:T(8,128)}), f32[32,18,128]{2,1,0:T(8,128)S(1)}, u32[]{:S(2)}, u32[]{:S(2)}) async-start(f32[32,18,128]{2,1,0:T(8,128)} %get-tuple-element.26), calls=%async_computation | async-start | bytes 786432 | tf_op jit(solution)/shard_map/all_to_all | solution.py:468
  15.1 21.8 %collective-permute-start.1 = (f32[8,40,256]{2,1,0:T(8,128)}, f32[8,40,256]{2,1,0:T(8,128)S(1)}, u32[]{:S(2)}, u32[]{:S(2)}) collective-permute-start(f32[8,40,256]{2,1,0:T(8,128)} %get-tuple-element.25.refs_1_.refs_2_), channel_id=1, source_target_pairs={{8,0},{16,8},{24,16},{32,24},{40,32},{48,40},{56,48},{64,56},{72,6... | collective-permute-start | bytes 983048 | tf_op jit(solution)/shard_map/ppermute | solution.py:430
  16.4 20.5 %collective-permute-start = (f32[8,40,256]{2,1,0:T(8,128)}, f32[8,40,256]{2,1,0:T(8,128)S(1)}, u32[]{:S(2)}, u32[]{:S(2)}) collective-permute-start(f32[8,40,256]{2,1,0:T(8,128)} %get-tuple-element.25.refs_1_.refs_2_), channel_id=1, source_target_pairs={{0,8},{8,16},{16,24},{24,32},{32,40},{40,48},{48,56},{56,64},{64,7... | collective-permute-start | bytes 983048 | tf_op jit(solution)/shard_map/ppermute | solution.py:430
  20.5 1.4 %copy-start = (f32[3,27,36,36]{3,2,1,0:T(8,128)S(1)}, f32[3,27,36,36]{3,2,1,0:T(8,128)}, u32[]{:S(2)}) copy-start(f32[3,27,36,36]{3,2,1,0:T(8,128)} %kernels.1) | copy-start | bytes 1259716
  23.2 17.3 %copy-start.9 = (bf16[736,256]{1,0:T(8,128)(2,1)}, bf16[736,256]{1,0:T(8,128)(2,1)S(1)}, u32[]{:S(2)}) copy-start(bf16[736,256]{1,0:T(8,128)(2,1)S(1)} %get-tuple-element.44.refs_4_) | copy-start | bytes 1130500
  23.2 17.3 %copy-start.11 = (bf16[736,256]{1,0:T(8,128)(2,1)}, bf16[736,256]{1,0:T(8,128)(2,1)S(1)}, u32[]{:S(2)}) copy-start(bf16[736,256]{1,0:T(8,128)(2,1)S(1)} %get-tuple-element.34.refs_4_.refs_6_) | copy-start | bytes 1130500
  29.9 19.0 %all-to-all-start.1 = ((f32[8,24,128]{2,1,0:T(8,128)}), f32[8,24,128]{2,1,0:T(8,128)S(1)}, u32[]{:S(2)}, u32[]{:S(2)}) async-start(f32[8,24,128]{2,1,0:T(8,128)} %shard_map.138), calls=%async_computation.1 | async-start | bytes 196608 | tf_op jit(solution)/shard_map/all_to_all | solution.py:477
  36.9 21.5 %collective-permute-start.2 = (f32[3,40,768]{2,1,0:T(8,128)S(1)}, f32[3,40,768]{2,1,0:T(8,128)}, u32[]{:S(2)}, u32[]{:S(2)}) collective-permute-start(f32[3,40,768]{2,1,0:T(8,128)S(1)} %pad_maximum_fusion), channel_id=1, source_target_pairs={{0,1},{1,2},{2,3},{3,4},{4,5},{5,6},{6,7},{8,9},{9,10},{10,11},{11... | collective-permute-start | bytes 1105928 | tf_op jit(solution)/shard_map/ppermute | solution.py:430
  41.3 7.7 %copy-start.8 = (f32[2,36,36,1,128]{4,3,2,1,0:T(1,128)S(1)}, f32[2,36,36,1,128]{4,3,2,1,0:T(1,128)}, u32[]{:S(2)}) copy-start(f32[2,36,36,1,128]{4,3,2,1,0:T(1,128)} %param.15) | copy-start | bytes 3981316
  41.3 17.2 %collective-permute-start.3 = (f32[3,40,768]{2,1,0:T(8,128)}, f32[3,40,768]{2,1,0:T(8,128)}, u32[]{:S(2)}, u32[]{:S(2)}) collective-permute-start(f32[3,40,768]{2,1,0:T(8,128)} %pad_maximum_fusion.1), channel_id=1, source_target_pairs={{1,0},{2,1},{3,2},{4,3},{5,4},{6,5},{7,6},{9,8},{10,9},{11,10},{12... | collective-permute-start | bytes 1105928 | tf_op jit(solution)/shard_map/ppermute | solution.py:430
  44.3 4.6 %copy-start.14 = (s32[128]{0:T(128)S(1)}, s32[128]{0:T(128)}, u32[]{:S(2)}) copy-start(s32[128]{0:T(128)} %param.16) | copy-start | bytes 1540
  53.5 12.1 %all-to-all-start.2 = ((f32[8,24,128]{2,1,0:T(8,128)}), f32[8,24,128]{2,1,0:T(8,128)S(1)}, u32[]{:S(2)}, u32[]{:S(2)}) async-start(f32[8,24,128]{2,1,0:T(8,128)} %shard_map.140), calls=%async_computation.2 | async-start | bytes 196608 | tf_op jit(solution)/shard_map/all_to_all | solution.py:502
  58.4 7.2 %copy-start.3 = (bf16[2,256,64]{2,1,0:T(8,128)(2,1)S(1)}, bf16[2,256,64]{2,1,0:T(8,128)(2,1)}, u32[]{:S(2)}) copy-start(bf16[2,256,64]{2,1,0:T(8,128)(2,1)} %constant.37.clone.table_4) | copy-start | bytes 196612
  58.4 7.2 %copy-start.4 = (bf16[2,256,64]{2,1,0:T(8,128)(2,1)S(1)}, bf16[2,256,64]{2,1,0:T(8,128)(2,1)}, u32[]{:S(2)}) copy-start(bf16[2,256,64]{2,1,0:T(8,128)(2,1)} %constant.33.clone.table) | copy-start | bytes 196612
  58.4 12.9 %copy-start.10 = (bf16[736,256]{1,0:T(8,128)(2,1)S(1)}, bf16[736,256]{1,0:T(8,128)(2,1)}, u32[]{:S(2)}) copy-start(bf16[736,256]{1,0:T(8,128)(2,1)} %copy-done.9) | copy-start | bytes 1130500
  58.4 1.1 %copy-start.13 = (bf16[736,256]{1,0:T(8,128)(2,1)S(1)}, bf16[736,256]{1,0:T(8,128)(2,1)}, u32[]{:S(2)}) copy-start(bf16[736,256]{1,0:T(8,128)(2,1)} %copy-done.11) | copy-start | bytes 1130500
  59.5 11.9 %copy-start.20 = (f32[6,40,512]{2,1,0:T(8,128)S(1)}, f32[6,40,512]{2,1,0:T(8,128)}, u32[]{:S(2)}) copy-start(f32[6,40,512]{2,1,0:T(8,128)} %copy-done.19) | copy-start | bytes 1474564
  66.7 19.1 %all-to-all-start.3 = ((f32[32,18,128]{2,1,0:T(8,128)}), f32[32,18,128]{2,1,0:T(8,128)S(1)}, u32[]{:S(2)}, u32[]{:S(2)}) async-start(f32[32,18,128]{2,1,0:T(8,128)} %shard_map.142), calls=%async_computation.3 | async-start | bytes 786432 | tf_op jit(solution)/shard_map/all_to_all | solution.py:513
  71.4 1.1 %copy-start.18 = (f32[8,40,512]{2,1,0:T(8,128)S(1)}, f32[8,40,512]{2,1,0:T(8,128)}, u32[]{:S(2)}) copy-start(f32[8,40,512]{2,1,0:T(8,128)} %copy-done.17) | copy-start | bytes 1966084
  72.5 13.3 %copy-start.1 = (bf16[2,256,256]{2,1,0:T(8,128)(2,1)S(1)}, bf16[2,256,256]{2,1,0:T(8,128)(2,1)}, u32[]{:S(2)}) copy-start(bf16[2,256,256]{2,1,0:T(8,128)(2,1)} %constant.34.clone.table) | copy-start | bytes 786436
  72.5 13.3 %copy-start.7 = (bf16[2,64,64]{2,1,0:T(8,128)(2,1)S(1)}, bf16[2,64,64]{2,1,0:T(8,128)(2,1)}, u32[]{:S(2)}) copy-start(bf16[2,64,64]{2,1,0:T(8,128)(2,1)} %constant.38.clone.table_4) | copy-start | bytes 49156
  (5 other events, 4.7 us)

commit v5 on v3

--- a/solution.py
+++ b/solution.py
@@ -1,4 +1,3 @@
-import functools
 import math
 
 import jax
@@ -12,7 +11,8 @@
 
 NZ = 64
 KY = 32
-INNER = 1024
+MIX = 8192
+CONV = 12288
 FULL = 60
 CP = 40
 LANES = 128
@@ -197,22 +197,20 @@
 ROW = 368
 
 
-def taps_body(first, kernels, *refs):
+def make_taps(kernels, which, out_ref, scratch):
     channels = kernels.shape[2]
-    *outs, scratch = refs
-    for r, out_ref in enumerate(outs):
-        scratch[...] = jnp.zeros(scratch.shape, F32)
-        for tap in range(27):
-            row, lane = CP * (tap % 3), CP * (tap // 3)
-            scratch[row : row + channels, lane : lane + channels] = kernels[first + r, tap]
-        high, low = split(scratch[...].T[:ROW])
-        out_ref[:ROW, :128] = high
-        out_ref[:ROW, 128:] = high
-        out_ref[ROW:, :128] = low
-        out_ref[ROW:, 128:] = jnp.zeros((ROW, 128), BF16)
-
-
-def convolve_rows(load_row, rows_in, width, taps, refs, finish, rest=()):
+    scratch[...] = jnp.zeros(scratch.shape, F32)
+    for tap in range(27):
+        row, lane = CP * (tap % 3), CP * (tap // 3)
+        scratch[row : row + channels, lane : lane + channels] = kernels[which, tap]
+    high, low = split(scratch[...].T[:ROW])
+    out_ref[:ROW, :128] = high
+    out_ref[:ROW, 128:] = high
+    out_ref[ROW:, :128] = low
+    out_ref[ROW:, 128:] = jnp.zeros((ROW, 128), BF16)
+
+
+def convolve_rows(load_row, rows_in, width, taps, refs, finish):
     stack_a, stack_b, first_sum, second_sum, whole = refs
     z_position = lax.broadcasted_iota(jnp.int32, (CP, LANES), 1) % NZ
     has_lower = z_position >= 1
@@ -269,9 +267,7 @@
         return carry
 
     prepare(0, stack_a)
-    pair(0, 0)
-    wait(rest)
-    lax.fori_loop(1, rows_in // 2, pair, 0)
+    lax.fori_loop(0, rows_in // 2, pair, 0)
     emit(rows_in - 3)
 
 
@@ -307,41 +303,19 @@
         target[first : first + count, :, width * i : width * i + width] = source[rows]
 
 
-def inner_body(sizes, left, own, right, place, taps, out_ref, rows, *refs):
+def convolutions_body(sizes, before, left, own, right, after, place, kernels, out_ref, *refs):
+    rows, first, second, table, taps = refs[:5]
+    wide, narrow = refs[5:10], refs[10:]
+    make_taps(kernels, 0, taps, table)
     count = own.shape[0]
-    join((left, own, right), slice(0, count), rows, 0)
+    rows[0:3] = before[...]
+    join((left, own, right), slice(0, count), rows, 3)
+    rows[3 + count :] = after[...]
     keep = inside(place, -2, sizes, 512)
 
-    def finish(row, tiles):
+    def finish_first(row, tiles):
         values = jnp.concatenate(tiles[1:5], axis=1)
-        out_ref[row] = jnp.where(keep(row + 1), gelu_exact(values), 0.0)
-
-    convolve_rows(lambda i: rows[i], count, 768, taps, refs, finish)
-
-
-def outer_body(sizes, before, left, own, right, after, place, taps, out_ref, rows, *refs):
-    count = own.shape[0]
-    sides = (left, own, right)
-    rows[0:3] = before[...]
-    join(sides, slice(0, 2), rows, 3)
-    join(sides, slice(count - 2, count), rows, 5)
-    rows[7:10] = after[...]
-    keep = inside(place, -2, sizes, 512)
-
-    def finish(row, tiles):
-        values = jnp.concatenate(tiles[1:5], axis=1)
-        local_y = jnp.where(row < 4, row - 2, row + count - 6)
-        out_ref[row] = jnp.where(keep(local_y), gelu_exact(values), 0.0)
-
-    convolve_rows(lambda i: rows[i], 10, 768, taps, refs, finish)
-
-
-def later_body(sizes, inner, outer, place, taps_1, taps_2, out_ref, rows, second, *refs):
-    count = inner.shape[0]
-    rows[0:3] = outer[0:3]
-    rows[3 : 3 + count] = inner[...]
-    rows[3 + count :] = outer[5:8]
-    keep = inside(place, -2, sizes, 512)
+        first[row] = jnp.where(keep(row - 2), gelu_exact(values), 0.0)
 
     def finish_second(row, tiles):
         values = jnp.concatenate(tiles, axis=1)
@@ -350,8 +324,11 @@
     def finish_third(row, tiles):
         out_ref[row] = jnp.concatenate(tiles[1:3], axis=1)
 
-    convolve_rows(lambda i: rows[i], count + 6, 512, taps_1, refs, finish_second)
-    convolve_rows(lambda i: second[i], count + 4, 512, taps_2, refs, finish_third)
+    convolve_rows(lambda i: rows[i], count + 6, 768, taps, wide, finish_first)
+    make_taps(kernels, 1, taps, table)
+    convolve_rows(lambda i: first[i], count + 4, 512, taps, narrow, finish_second)
+    make_taps(kernels, 2, taps, table)
+    convolve_rows(lambda i: second[i], count + 2, 512, taps, narrow, finish_third)
 
 
 def last_body(received, third, table, out_ref):
@@ -391,9 +368,6 @@
     ]
 
     sizes = (cells_x, cells_y, full_x, full_y)
-    row_scratch = [pltpu.SemaphoreType.DMA((9,)), pltpu.VMEM((2 * ROW, 256), BF16)]
-    taps_shape = jax.ShapeDtypeStruct((2 * ROW, 256), BF16)
-
     grid, sent = call(
         z_in_body,
         (
@@ -404,18 +378,9 @@
         scratch=[pltpu.VMEM(field.shape, F32), pltpu.VMEM(z_in.shape, BF16), pltpu.SemaphoreType.DMA((2,))],
         hbm=(0, 1), vmem=FULL,
     )
-    def make_taps(first, count, kernels):
-        body = functools.partial(taps_body, first)
-        return call(body, (taps_shape,) * count, kernels, scratch=[pltpu.VMEM((128, 384), F32)])
-
-    conv_kernels, sent = lax.optimization_barrier((conv_kernels, sent))
-    taps = make_taps(0, 1, conv_kernels)
-    grid, conv_kernels, *taps = lax.optimization_barrier((grid, conv_kernels, *taps))
     left = shift(grid, "gx", 1)
     right = shift(grid, "gx", -1)
-    taps = [*taps, *make_taps(1, 2, conv_kernels)]
     received = lax.all_to_all(sent, "gx", 0, 0, tiled=True)
-    received, *taps = lax.optimization_barrier((received, *taps))
 
     sent = call(rows_body, jax.ShapeDtypeStruct((size_y, 24, LANES), F32), received, x_in)
 
@@ -427,14 +392,6 @@
 
     before = shift(edge(slice(cells_y - 3, cells_y)), "gy", 1)
     after = shift(edge(slice(0, 3)), "gy", -1)
-    inner = call(
-        lambda *refs: inner_body(sizes, *refs),
-        jax.ShapeDtypeStruct((cells_y - 2, CP, 512), F32),
-        left, grid, right, place, taps[0],
-        scratch=[pltpu.VMEM((cells_y, CP, 768), F32)] + conv_scratch(768),
-        smem=(3,), light=False, flops=INNER << 20,
-    )
-    inner, received = lax.optimization_barrier((inner, received))
     weights = mix_weights.reshape(2, channels * channels, kx_local * KY)
     sent = call(
         mix_body,
@@ -442,31 +399,25 @@
         received, weights, kept_z.reshape(1, -1), place, y_in, y_out,
         scratch=[pltpu.VMEM((cells_y * size_y * kx_local * 2, LANES), F32)]
         + [pltpu.VMEM((LANES, kx_local * KY), F32)] * 2,
-        smem=(3,), flops=30 << 30,
+        smem=(3,), flops=MIX << 20,
     )
+    received = lax.all_to_all(sent, "gy", 0, 0, tiled=True)
+    sent = call(rows_body, jax.ShapeDtypeStruct((size_x, 24, LANES), F32), received, x_out)
     before, after, _ = lax.optimization_barrier((before, after, sent))
-    received = lax.all_to_all(sent, "gy", 0, 0, tiled=True)
-    outer = call(
-        lambda *refs: outer_body(sizes, *refs),
-        jax.ShapeDtypeStruct((8, CP, 512), F32),
-        before, left, grid, right, after, place, taps[0],
-        scratch=[pltpu.VMEM((10, CP, 768), F32)] + conv_scratch(768),
-        smem=(5,), flops=4 << 30,
-    )
-    outer, received = lax.optimization_barrier((outer, received))
-    sent = call(rows_body, jax.ShapeDtypeStruct((size_x, 24, LANES), F32), received, x_out)
-    outer, sent = lax.optimization_barrier((outer, sent))
     received = lax.all_to_all(sent, "gx", 0, 0, tiled=True)
     third = call(
-        lambda *refs: later_body(sizes, *refs),
+        lambda *refs: convolutions_body(sizes, *refs),
         jax.ShapeDtypeStruct((cells_y, CP, cells_x * NZ), F32),
-        inner, outer, place, taps[1], taps[2],
+        before, left, grid, right, after, place, conv_kernels,
         scratch=[
+            pltpu.VMEM((cells_y + 6, CP, 768), F32),
             pltpu.VMEM((cells_y + 4, CP, 512), F32),
             pltpu.VMEM((cells_y + 2, CP, 512), F32),
+            pltpu.VMEM((128, 384), F32),
+            pltpu.VMEM((2 * ROW, 256), BF16),
         ]
-        + conv_scratch(512),
-        smem=(2,), flops=8 << 30,
+        + conv_scratch(768) + conv_scratch(512),
+        smem=(5,), flops=CONV << 20,
     )
     return call(
         last_body, jax.ShapeDtypeStruct(field.shape, F32), received, third, z_out,

time: 86.6 us -> 78.2 us (0.903)
  blocking collectives: 0 us -> 9.34 us
  starting transfers between devices: 41.2 us -> 33.9 us
  Pallas kernels: 24.9 us -> 21.5 us
  local copies, waits for them, and re-layouts: 7.81 us -> 4.59 us
  waiting for transfers between devices: 9.71 us -> 7.83 us
  other arithmetic: 1.61 us -> 0.13 us
    all_to_all x0 -> x1, blocking collectives: none -> 9.34 us  [shards(): received = lax.all_to_all(sent, 'gy', 0, 0, tiled=True)]
    unnamed x36 -> x18, local copies, waits for them, and re-layouts: 7.76 us -> 3.58 us
    all_to_all x2 -> x1, starting transfers between devices: 11.9 us -> 8.17 us  [shards(): received = lax.all_to_all(sent, 'gy', 0, 0, tiled=True)]
    pallas_call x10 -> x6, Pallas kernels: 24.9 us -> 21.5 us  [call(): pl.pallas_call(body, out_shape=out_shape, in_specs=in_specs, out_specs=tu...]
    all_to_all x2, starting transfers between devices: 18.4 us -> 15.8 us  [shards(): received = lax.all_to_all(sent, 'gx', 0, 0, tiled=True)]
    all_to_all x2, waiting for transfers between devices: 9.7 us -> 7.82 us  [shards(): received = lax.all_to_all(sent, 'gx', 0, 0, tiled=True)]
    concatenate x2, other arithmetic: 1.54 us -> 0.05 us  [edge(): return jnp.concatenate([left[rows], grid[rows], right[rows]], axis=2)]
    ppermute x4, starting transfers between devices: 11 us -> 10 us  [shift(): return lax.ppermute(values, axis, pairs)]
  transfers between devices with their start and end apart: 8 -> 7, of which waited for: 2 -> 1; matrix products, arithmetic and copies ran while one was open for 2% -> 1% of each run, Pallas kernels for 24% -> 23%
where the time goes in v5:
time: 78.2 us; the launch traced here: 77.6 us
  starting transfers between devices  33.9 us (43%)
  Pallas kernels  21.5 us (27%)
  blocking collectives  9.34 us (12%)
  waiting for transfers between devices  7.83 us (10%)
  local copies, waits for them, and re-layouts  4.59 us (6%)
    pallas_call x6, Pallas kernels, call(): pl.pallas_call(body, out_shape=out_shape, in_specs=in_specs, out_specs=tu...  21.5 us
    all_to_all x2, starting transfers between devices, shards(): received = lax.all_to_all(sent, 'gx', 0, 0, tiled=True)  15.8 us
    ppermute x4, starting transfers between devices, shift(): return lax.ppermute(values, axis, pairs)  10 us
    all_to_all x1, blocking collectives, shards(): received = lax.all_to_all(sent, 'gy', 0, 0, tiled=True)  9.34 us
    all_to_all x1, starting transfers between devices, shards(): received = lax.all_to_all(sent, 'gy', 0, 0, tiled=True)  8.17 us
    all_to_all x2, waiting for transfers between devices, shards(): received = lax.all_to_all(sent, 'gx', 0, 0, tiled=True)  7.82 us
    unnamed x18, local copies, waits for them, and re-layouts  3.58 us
  transfers between devices with their start and end apart: 7, of which 1 were waited for; matrix products, arithmetic and copies ran while one was open for 1% of the time, Pallas kernels for 23%

profile of v5, /device:TPU:1, one launch (start us, length us, event | category | flops | bytes accessed | tf_op | source)
XLA Modules:
  0.0 77.6 jit_solution(7507106551720519676)
XLA Ops:
  0.0 2.3 %shard_map.100 = (f32[8,40,256]{2,1,0:T(8,128)}, f32[32,24,128]{2,1,0:T(8,128)}) custom-call(f32[36,4,512]{2,1,0:T(4,128)} %field_hbm.1, bf16[2,256,256]{2,1,0:T(8,128)(2,1)} %constant.21.clone.table_hbm), custom_call_target="tpu_custom_call" | custom-call | bytes 557056 | tf_op jit(solution)/shard_map/pallas_call | solution.py:92
  2.3 11.9 %all-to-all-start = ((f32[32,24,128]{2,1,0:T(8,128)}), f32[32,24,128]{2,1,0:T(8,128)S(1)}, u32[]{:S(2)}, u32[]{:S(2)}) async-start(f32[32,24,128]{2,1,0:T(8,128)} %get-tuple-element.11), calls=%async_computation | async-start | bytes 786432 | tf_op jit(solution)/shard_map/all_to_all | solution.py:383
  14.2 3.2 %collective-permute-start = (f32[8,40,256]{2,1,0:T(8,128)}, f32[8,40,256]{2,1,0:T(8,128)S(1)}, u32[]{:S(2)}, u32[]{:S(2)}) collective-permute-start(f32[8,40,256]{2,1,0:T(8,128)} %get-tuple-element.12.refs_2_), channel_id=1, source_target_pairs={{0,8},{8,16},{16,24},{24,32},{32,40},{40,48},{48,56},{56,64},{64,7... | collective-permute-start | bytes 983048 | tf_op jit(solution)/shard_map/ppermute | solution.py:352
  17.4 1.3 %collective-permute-start.1 = (f32[8,40,256]{2,1,0:T(8,128)}, f32[8,40,256]{2,1,0:T(8,128)S(1)}, u32[]{:S(2)}, u32[]{:S(2)}) collective-permute-start(f32[8,40,256]{2,1,0:T(8,128)} %get-tuple-element.12.refs_2_), channel_id=1, source_target_pairs={{8,0},{16,8},{24,16},{32,24},{40,32},{48,40},{56,48},{64,56},{72,6... | collective-permute-start | bytes 983048 | tf_op jit(solution)/shard_map/ppermute | solution.py:352
  18.7 0.1 pad_add_fusion.place.refs_5_
  18.8 1.0 %fusion.1 = (f32[3,40,256]{2,1,0:T(8,128)S(1)}, f32[3,40,256]{2,1,0:T(8,128)S(1)}) fusion(f32[8,40,256]{2,1,0:T(8,128)} %get-tuple-element.12.refs_2_), kind=kLoop, calls=%fused_computation.4 | loop fusion | bytes 491520 | tf_op jit(solution)/shard_map/slice | solution.py:391
  19.7 0.0 copy-start.5
  19.8 0.0 copy-start.6
  19.8 7.8 %all-to-all-done.received = f32[32,24,128]{2,1,0:T(8,128)S(1)} async-done(((f32[32,24,128]{2,1,0:T(8,128)}), f32[32,24,128]{2,1,0:T(8,128)S(1)}, u32[]{:S(2)}, u32[]{:S(2)}) %all-to-all-start) | async-done | bytes 393248 | tf_op jit(solution)/shard_map/all_to_all | solution.py:383
  27.6 0.9 %shard_map.101 = f32[8,24,128]{2,1,0:T(8,128)} custom-call(f32[32,24,128]{2,1,0:T(8,128)S(1)} %all-to-all-done.received, bf16[2,64,256]{2,1,0:T(8,128)(2,1)S(1)} %copy-done.3), custom_call_target="tpu_custom_call" | custom-call | bytes 458752 | tf_op jit(solution)/shard_map/pallas_call | solution.py:92
  28.5 8.2 %all-to-all-start.1 = ((f32[8,24,128]{2,1,0:T(8,128)}), f32[8,24,128]{2,1,0:T(8,128)S(1)}, u32[]{:S(2)}, u32[]{:S(2)}) async-start(f32[8,24,128]{2,1,0:T(8,128)} %shard_map.101), calls=%async_computation.1 | async-start | bytes 196608 | tf_op jit(solution)/shard_map/all_to_all | solution.py:388
  36.7 1.9 %collective-permute-start.3 = (f32[3,40,768]{2,1,0:T(8,128)S(1)}, f32[3,40,768]{2,1,0:T(8,128)}, u32[]{:S(2)}, u32[]{:S(2)}) collective-permute-start(f32[3,40,768]{2,1,0:T(8,128)S(1)} %pad_maximum_fusion.1), channel_id=1, source_target_pairs={{1,0},{2,1},{3,2},{4,3},{5,4},{6,5},{7,6},{9,8},{10,9},{11,10},{12... | collective-permute-start | bytes 1105928 | tf_op jit(solution)/shard_map/ppermute | solution.py:352
  38.7 3.6 %collective-permute-start.2 = (f32[3,40,768]{2,1,0:T(8,128)S(1)}, f32[3,40,768]{2,1,0:T(8,128)}, u32[]{:S(2)}, u32[]{:S(2)}) collective-permute-start(f32[3,40,768]{2,1,0:T(8,128)S(1)} %pad_maximum_fusion), channel_id=1, source_target_pairs={{0,1},{1,2},{2,3},{3,4},{4,5},{5,6},{6,7},{8,9},{9,10},{10,11},{11... | collective-permute-start | bytes 1105928 | tf_op jit(solution)/shard_map/ppermute | solution.py:352
  42.4 0.0 copy-start.7
  42.4 1.0 %copy-done.7 = bf16[2,256,512]{2,1,0:T(8,128)(2,1)S(1)} copy-done((bf16[2,256,512]{2,1,0:T(8,128)(2,1)S(1)}, bf16[2,256,512]{2,1,0:T(8,128)(2,1)}, u32[]{:S(2)}) %copy-start.7) | copy-done | bytes 524312
  43.4 1.0 %copy-done.8 = bf16[2,512,256]{2,1,0:T(8,128)(2,1)S(1)} copy-done((bf16[2,512,256]{2,1,0:T(8,128)(2,1)S(1)}, bf16[2,512,256]{2,1,0:T(8,128)(2,1)}, u32[]{:S(2)}) %copy-start.8) | copy-done | bytes 524312
  44.4 1.8 %shard_map.102 = f32[8,24,128]{2,1,0:T(8,128)S(1)} custom-call(f32[8,24,128]{2,1,0:T(8,128)S(1)} %all-to-all-done.1.received, f32[2,1296,128]{2,1,0:T(8,128)S(1)} %bitcast.4, s32[1,128]{1,0:T(1,128)S(1)} %bitcast.5, s32[2]{0:T(128)S(1)} %pad_add_fusion.place.refs_5_, bf16[2,256,512]{2,1,0:T(8,128)(2,1)S(1)} %copy-done.7, bf16[2,512,256]{2,1,0:T(8,128)(2,1)S(1)} %copy-done.8), custom_call_target="tpu_custom_call" | custom-call | flops 8589934592 | bytes 2474504 | tf_op jit(solution)/shard_map/pallas_call | solution.py:92
  46.3 9.3 %all_to_all.20.received = f32[8,24,128]{2,1,0:T(8,128)S(1)} all-to-all(f32[8,24,128]{2,1,0:T(8,128)S(1)} %shard_map.102), channel_id=1, replica_groups=mesh['gx'=32,'gy'=8] {'gy'}, dimensions={0} | all-to-all | bytes 196608 | tf_op jit(solution)/shard_map/all_to_all | solution.py:404
  55.6 1.0 %shard_map.103 = f32[32,24,128]{2,1,0:T(8,128)} custom-call(f32[8,24,128]{2,1,0:T(8,128)S(1)} %all_to_all.20.received, bf16[2,256,64]{2,1,0:T(8,128)(2,1)S(1)} %copy-done.2), custom_call_target="tpu_custom_call" | custom-call | bytes 163840 | tf_op jit(solution)/shard_map/pallas_call | solution.py:92
  56.7 3.9 %all-to-all-start.3 = ((f32[32,24,128]{2,1,0:T(8,128)}), f32[32,24,128]{2,1,0:T(8,128)S(1)}, u32[]{:S(2)}, u32[]{:S(2)}) async-start(f32[32,24,128]{2,1,0:T(8,128)} %shard_map.103), calls=%async_computation.3 | async-start | bytes 786432 | tf_op jit(solution)/shard_map/all_to_all | solution.py:407
  60.5 0.0 copy-start
  60.6 1.5 %copy-done.4 = f32[3,27,36,36]{3,2,1,0:T(8,128)S(1)} copy-done((f32[3,27,36,36]{3,2,1,0:T(8,128)S(1)}, f32[3,27,36,36]{3,2,1,0:T(8,128)}, u32[]{:S(2)}) %copy-start.4) | copy-done | bytes 419928
  62.1 14.3 %shard_map.104.third = f32[8,40,256]{2,1,0:T(8,128)S(1)} custom-call(f32[3,40,768]{2,1,0:T(8,128)} %collective-permute-done.2.refs_0_, f32[8,40,256]{2,1,0:T(8,128)S(1)} %collective-permute-done.refs_1_, f32[8,40,256]{2,1,0:T(8,128)S(1)} %copy-done.1, f32[8,40,256]{2,1,0:T(8,128)S(1)} %collective-permute-done.1.refs_3_, ...), custom_call_target="tpu_custom_call" | custom-call | flops 12884901888 | bytes 2140232 | tf_op jit(solution)/shard_map/pallas_call | solution.py:92
  76.4 1.2 %shard_map.105 = f32[36,4,512]{2,1,0:T(4,128)} custom-call(f32[32,24,128]{2,1,0:T(8,128)S(1)} %all-to-all-done.3.received, f32[8,40,256]{2,1,0:T(8,128)S(1)} %shard_map.104.third, bf16[2,256,256]{2,1,0:T(8,128)(2,1)S(1)} %copy-done), custom_call_target="tpu_custom_call" | custom-call | bytes 983040 | tf_op jit(solution)/shard_map/pallas_call | solution.py:92
  (20 shorter events, 0.1 us)
Async XLA Ops:
  0.0 27.6 %copy-start.3 = (bf16[2,64,256]{2,1,0:T(8,128)(2,1)S(1)}, bf16[2,64,256]{2,1,0:T(8,128)(2,1)}, u32[]{:S(2)}) copy-start(bf16[2,64,256]{2,1,0:T(8,128)(2,1)} %constant.22.clone.table) | copy-start | bytes 196612
  2.3 25.2 %all-to-all-start = ((f32[32,24,128]{2,1,0:T(8,128)}), f32[32,24,128]{2,1,0:T(8,128)S(1)}, u32[]{:S(2)}, u32[]{:S(2)}) async-start(f32[32,24,128]{2,1,0:T(8,128)} %get-tuple-element.11), calls=%async_computation | async-start | bytes 786432 | tf_op jit(solution)/shard_map/all_to_all | solution.py:383
  14.2 22.4 %collective-permute-start = (f32[8,40,256]{2,1,0:T(8,128)}, f32[8,40,256]{2,1,0:T(8,128)S(1)}, u32[]{:S(2)}, u32[]{:S(2)}) collective-permute-start(f32[8,40,256]{2,1,0:T(8,128)} %get-tuple-element.12.refs_2_), channel_id=1, source_target_pairs={{0,8},{8,16},{16,24},{24,32},{32,40},{40,48},{48,56},{56,64},{64,7... | collective-permute-start | bytes 983048 | tf_op jit(solution)/shard_map/ppermute | solution.py:352
  17.4 19.2 %collective-permute-start.1 = (f32[8,40,256]{2,1,0:T(8,128)}, f32[8,40,256]{2,1,0:T(8,128)S(1)}, u32[]{:S(2)}, u32[]{:S(2)}) collective-permute-start(f32[8,40,256]{2,1,0:T(8,128)} %get-tuple-element.12.refs_2_), channel_id=1, source_target_pairs={{8,0},{16,8},{24,16},{32,24},{40,32},{48,40},{56,48},{64,56},{72,6... | collective-permute-start | bytes 983048 | tf_op jit(solution)/shard_map/ppermute | solution.py:352
  19.7 22.6 %copy-start.5 = (f32[2,36,36,1,128]{4,3,2,1,0:T(1,128)S(1)}, f32[2,36,36,1,128]{4,3,2,1,0:T(1,128)}, u32[]{:S(2)}) copy-start(f32[2,36,36,1,128]{4,3,2,1,0:T(1,128)} %param.11) | copy-start | bytes 3981316
  19.8 22.6 %copy-start.6 = (s32[128]{0:T(128)S(1)}, s32[128]{0:T(128)}, u32[]{:S(2)}) copy-start(s32[128]{0:T(128)} %param.12) | copy-start | bytes 1540
  28.5 13.9 %all-to-all-start.1 = ((f32[8,24,128]{2,1,0:T(8,128)}), f32[8,24,128]{2,1,0:T(8,128)S(1)}, u32[]{:S(2)}, u32[]{:S(2)}) async-start(f32[8,24,128]{2,1,0:T(8,128)} %shard_map.101), calls=%async_computation.1 | async-start | bytes 196608 | tf_op jit(solution)/shard_map/all_to_all | solution.py:388
  36.7 23.9 %collective-permute-start.3 = (f32[3,40,768]{2,1,0:T(8,128)S(1)}, f32[3,40,768]{2,1,0:T(8,128)}, u32[]{:S(2)}, u32[]{:S(2)}) collective-permute-start(f32[3,40,768]{2,1,0:T(8,128)S(1)} %pad_maximum_fusion.1), channel_id=1, source_target_pairs={{1,0},{2,1},{3,2},{4,3},{5,4},{6,5},{7,6},{9,8},{10,9},{11,10},{12... | collective-permute-start | bytes 1105928 | tf_op jit(solution)/shard_map/ppermute | solution.py:352
  38.7 21.9 %collective-permute-start.2 = (f32[3,40,768]{2,1,0:T(8,128)S(1)}, f32[3,40,768]{2,1,0:T(8,128)}, u32[]{:S(2)}, u32[]{:S(2)}) collective-permute-start(f32[3,40,768]{2,1,0:T(8,128)S(1)} %pad_maximum_fusion), channel_id=1, source_target_pairs={{0,1},{1,2},{2,3},{3,4},{4,5},{5,6},{6,7},{8,9},{9,10},{10,11},{11... | collective-permute-start | bytes 1105928 | tf_op jit(solution)/shard_map/ppermute | solution.py:352
  42.4 1.0 %copy-start.7 = (bf16[2,256,512]{2,1,0:T(8,128)(2,1)S(1)}, bf16[2,256,512]{2,1,0:T(8,128)(2,1)}, u32[]{:S(2)}) copy-start(bf16[2,256,512]{2,1,0:T(8,128)(2,1)} %constant.23.clone.y_in) | copy-start | bytes 1572868
  43.4 1.0 %copy-start.8 = (bf16[2,512,256]{2,1,0:T(8,128)(2,1)S(1)}, bf16[2,512,256]{2,1,0:T(8,128)(2,1)}, u32[]{:S(2)}) copy-start(bf16[2,512,256]{2,1,0:T(8,128)(2,1)} %constant.24.clone.y_out) | copy-start | bytes 1572868
  44.4 11.2 %copy-start.2 = (bf16[2,256,64]{2,1,0:T(8,128)(2,1)S(1)}, bf16[2,256,64]{2,1,0:T(8,128)(2,1)}, u32[]{:S(2)}) copy-start(bf16[2,256,64]{2,1,0:T(8,128)(2,1)} %constant.25.clone.table) | copy-start | bytes 196612
  44.4 16.1 %copy-start.1 = (f32[8,40,256]{2,1,0:T(8,128)S(1)}, f32[8,40,256]{2,1,0:T(8,128)}, u32[]{:S(2)}) copy-start(f32[8,40,256]{2,1,0:T(8,128)} %get-tuple-element.12.refs_2_) | copy-start | bytes 983044
  56.7 19.7 %all-to-all-start.3 = ((f32[32,24,128]{2,1,0:T(8,128)}), f32[32,24,128]{2,1,0:T(8,128)S(1)}, u32[]{:S(2)}, u32[]{:S(2)}) async-start(f32[32,24,128]{2,1,0:T(8,128)} %shard_map.103), calls=%async_computation.3 | async-start | bytes 786432 | tf_op jit(solution)/shard_map/all_to_all | solution.py:407
  60.5 15.8 %copy-start = (bf16[2,256,256]{2,1,0:T(8,128)(2,1)S(1)}, bf16[2,256,256]{2,1,0:T(8,128)(2,1)}, u32[]{:S(2)}) copy-start(bf16[2,256,256]{2,1,0:T(8,128)(2,1)} %constant.26.clone.table) | copy-start | bytes 786436
  60.6 1.5 %copy-start.4 = (f32[3,27,36,36]{3,2,1,0:T(8,128)S(1)}, f32[3,27,36,36]{3,2,1,0:T(8,128)}, u32[]{:S(2)}) copy-start(f32[3,27,36,36]{3,2,1,0:T(8,128)} %refs_6_.1) | copy-start | bytes 1259716

commit v6 on v5

--- a/solution.py
+++ b/solution.py
@@ -12,6 +12,7 @@
 NZ = 64
 KY = 32
 MIX = 8192
+EARLY = 0
 CONV = 12288
 FULL = 60
 CP = 40
@@ -79,7 +80,8 @@
     y_in = y_in.reshape(2 * kx_local * KY, -1)
     y_out = np.einsum("pqlsy,jk->ysjpqkl", plus_y.reshape(shape), eye_j)
     y_out = y_out.reshape(cells_y * size_y * kx_local * 2, -1)
-    return [split_table(t) for t in (z_in, x_in, y_in, y_out, x_out, z_out)]
+    y_tables = np.concatenate(np.split(y_in, 2, axis=1) + [y_out], axis=0)
+    return [split_table(t) for t in (z_in, x_in, y_tables, x_out, z_out)]
 
 
 def call(body, out_shape, *args, scratch=(), flops=0, smem=(), hbm=(), out_hbm=(), vmem=24, light=False):
@@ -149,14 +151,19 @@
         out_ref[:, 8 * tile : 8 * tile + 8, :] = block.reshape(out_ref.shape[0], 8, LANES)
 
 
-def mix_body(received, weights, kept, place, y_in, y_out, out_ref, stacked, s_re, s_im):
+def mix_body(received, weights, kept, place, y_tables, out_ref, stacked, s_re, s_im):
     cells_y = received.shape[0]
     rows = load_payload(received)
     block = rows.shape[0]
     for y in range(cells_y):
         stacked[y * block : (y + 1) * block, :CP] = rows[:, CP * y : CP * y + CP]
         stacked[y * block : (y + 1) * block, CP:] = jnp.zeros((block, LANES - CP), F32)
-    modes = product(y_in, stacked[...], ((1,), (0,)))
+    size = y_tables.shape[2]
+    modes = 0.0
+    for half in range(2):
+        span = slice(half * size, half * size + size)
+        table = [y_tables[i, span] for i in range(2)]
+        modes += product(table, stacked[span], ((1,), (0,)))
     count = modes.shape[0] // 2
     s_re[...] = modes[:count].T
     s_im[...] = modes[count:].T
@@ -185,7 +192,8 @@
         return jnp.concatenate([jnp.where(keep, total, 0.0), jnp.zeros((CP - channels, count), F32)], axis=0)
 
     mixed = jnp.concatenate([fold(total_re), fold(total_im)], axis=1)
-    back = product(y_out, mixed, ((1,), (1,)))
+    table = [y_tables[i, 2 * size :] for i in range(2)]
+    back = product(table, mixed, ((1,), (1,)))
     lanes = jnp.concatenate([back[y * block : (y + 1) * block] for y in range(cells_y)], axis=1)
     store_payload(out_ref, lanes)
 
@@ -197,17 +205,18 @@
 ROW = 368
 
 
-def make_taps(kernels, which, out_ref, scratch):
+def taps_body(kernels, after, out_ref, scratch):
     channels = kernels.shape[2]
-    scratch[...] = jnp.zeros(scratch.shape, F32)
-    for tap in range(27):
-        row, lane = CP * (tap % 3), CP * (tap // 3)
-        scratch[row : row + channels, lane : lane + channels] = kernels[which, tap]
-    high, low = split(scratch[...].T[:ROW])
-    out_ref[:ROW, :128] = high
-    out_ref[:ROW, 128:] = high
-    out_ref[ROW:, :128] = low
-    out_ref[ROW:, 128:] = jnp.zeros((ROW, 128), BF16)
+    for r in range(3):
+        scratch[...] = jnp.zeros(scratch.shape, F32)
+        for tap in range(27):
+            row, lane = CP * (tap % 3), CP * (tap // 3)
+            scratch[row : row + channels, lane : lane + channels] = kernels[r, tap]
+        high, low = split(scratch[...].T[:ROW])
+        out_ref[r, :ROW, :128] = high
+        out_ref[r, :ROW, 128:] = high
+        out_ref[r, ROW:, :128] = low
+        out_ref[r, ROW:, 128:] = jnp.zeros((ROW, 128), BF16)
 
 
 def convolve_rows(load_row, rows_in, width, taps, refs, finish):
@@ -303,19 +312,34 @@
         target[first : first + count, :, width * i : width * i + width] = source[rows]
 
 
-def convolutions_body(sizes, before, left, own, right, after, place, kernels, out_ref, *refs):
-    rows, first, second, table, taps = refs[:5]
-    wide, narrow = refs[5:10], refs[10:]
-    make_taps(kernels, 0, taps, table)
+def early_body(sizes, before, left, own, right, place, taps, out_ref, rows, *refs):
     count = own.shape[0]
+    half = count // 2 + 1
     rows[0:3] = before[...]
-    join((left, own, right), slice(0, count), rows, 3)
-    rows[3 + count :] = after[...]
+    join((left, own, right), slice(0, half), rows, 3)
+    keep = inside(place, -2, sizes, 512)
+
+    def finish(row, tiles):
+        values = jnp.concatenate(tiles[1:5], axis=1)
+        out_ref[row] = jnp.where(keep(row - 2), gelu_exact(values), 0.0)
+
+    convolve_rows(lambda i: rows[i], half + 3, 768, taps.at[0], refs, finish)
+
+
+def later_body(sizes, early, left, own, right, after, place, taps, out_ref, *refs):
+    rows, first, second = refs[:3]
+    wide, narrow = refs[3:8], refs[8:]
+    count = own.shape[0]
+    half = count // 2 + 1
+    join((left, own, right), slice(count - half, count), rows, 0)
+    rows[half:] = after[...]
+    base = early.shape[0]
+    first[:base] = early[...]
     keep = inside(place, -2, sizes, 512)
 
     def finish_first(row, tiles):
         values = jnp.concatenate(tiles[1:5], axis=1)
-        first[row] = jnp.where(keep(row - 2), gelu_exact(values), 0.0)
+        first[base + row] = jnp.where(keep(base + row - 2), gelu_exact(values), 0.0)
 
     def finish_second(row, tiles):
         values = jnp.concatenate(tiles, axis=1)
@@ -324,11 +348,9 @@
     def finish_third(row, tiles):
         out_ref[row] = jnp.concatenate(tiles[1:3], axis=1)
 
-    convolve_rows(lambda i: rows[i], count + 6, 768, taps, wide, finish_first)
-    make_taps(kernels, 1, taps, table)
-    convolve_rows(lambda i: first[i], count + 4, 512, taps, narrow, finish_second)
-    make_taps(kernels, 2, taps, table)
-    convolve_rows(lambda i: second[i], count + 2, 512, taps, narrow, finish_third)
+    convolve_rows(lambda i: rows[i], half + 3, 768, taps.at[0], wide, finish_first)
+    convolve_rows(lambda i: first[i], count + 4, 512, taps.at[1], narrow, finish_second)
+    convolve_rows(lambda i: second[i], count + 2, 512, taps.at[2], narrow, finish_third)
 
 
 def last_body(received, third, table, out_ref):
@@ -363,7 +385,7 @@
     kx_local = mix_weights.shape[4] // KY
     modes_x = kx_local * size_y
     place = jnp.stack([lax.axis_index("gx"), lax.axis_index("gy")]).astype(jnp.int32)
-    z_in, x_in, y_in, y_out, x_out, z_out = [
+    z_in, x_in, y_tables, x_out, z_out = [
         jnp.asarray(t) for t in tables(size_x, size_y, cells_x, cells_y, modes_x, modes_z)
     ]
 
@@ -380,7 +402,13 @@
     )
     left = shift(grid, "gx", 1)
     right = shift(grid, "gx", -1)
+    behind, _ = lax.optimization_barrier((place, sent))
+    taps = call(
+        taps_body, jax.ShapeDtypeStruct((3, 2 * ROW, 256), BF16), conv_kernels, behind,
+        scratch=[pltpu.VMEM((128, 384), F32)], smem=(1,),
+    )
     received = lax.all_to_all(sent, "gx", 0, 0, tiled=True)
+    received, taps = lax.optimization_barrier((received, taps))
 
     sent = call(rows_body, jax.ShapeDtypeStruct((size_y, 24, LANES), F32), received, x_in)
 
@@ -396,25 +424,36 @@
     sent = call(
         mix_body,
         jax.ShapeDtypeStruct((size_y, 24, LANES), F32),
-        received, weights, kept_z.reshape(1, -1), place, y_in, y_out,
+        received, weights, kept_z.reshape(1, -1), place, y_tables,
         scratch=[pltpu.VMEM((cells_y * size_y * kx_local * 2, LANES), F32)]
         + [pltpu.VMEM((LANES, kx_local * KY), F32)] * 2,
         smem=(3,), flops=MIX << 20,
     )
+    before, _ = lax.optimization_barrier((before, sent))
     received = lax.all_to_all(sent, "gy", 0, 0, tiled=True)
+    half = cells_y // 2 + 1
+    early = call(
+        lambda *refs: early_body(sizes, *refs),
+        jax.ShapeDtypeStruct((half + 1, CP, 512), F32),
+        before, left, grid, right, place, taps,
+        scratch=[
+            pltpu.VMEM((half + 3, CP, 768), F32),
+        ]
+        + conv_scratch(768),
+        smem=(4,), flops=EARLY << 20,
+    )
+    early, received = lax.optimization_barrier((early, received))
     sent = call(rows_body, jax.ShapeDtypeStruct((size_x, 24, LANES), F32), received, x_out)
-    before, after, _ = lax.optimization_barrier((before, after, sent))
+    early, after, _ = lax.optimization_barrier((early, after, sent))
     received = lax.all_to_all(sent, "gx", 0, 0, tiled=True)
     third = call(
-        lambda *refs: convolutions_body(sizes, *refs),
+        lambda *refs: later_body(sizes, *refs),
         jax.ShapeDtypeStruct((cells_y, CP, cells_x * NZ), F32),
-        before, left, grid, right, after, place, conv_kernels,
+        early, left, grid, right, after, place, taps,
         scratch=[
-            pltpu.VMEM((cells_y + 6, CP, 768), F32),
+            pltpu.VMEM((half + 3, CP, 768), F32),
             pltpu.VMEM((cells_y + 4, CP, 512), F32),
             pltpu.VMEM((cells_y + 2, CP, 512), F32),
-            pltpu.VMEM((128, 384), F32),
-            pltpu.VMEM((2 * ROW, 256), BF16),
         ]
         + conv_scratch(768) + conv_scratch(512),
         smem=(5,), flops=CONV << 20,

time: 78.2 us -> 79.5 us (1.017)
  blocking collectives: 9.34 us -> 0 us
  starting transfers between devices: 33.9 us -> 38.6 us
  Pallas kernels: 21.5 us -> 24.1 us
  waiting for transfers between devices: 7.83 us -> 9.96 us
    all_to_all x1 -> x0, blocking collectives: 9.34 us -> none  [shards(): received = lax.all_to_all(sent, 'gy', 0, 0, tiled=True)]
    all_to_all x1 -> x2, starting transfers between devices: 8.17 us -> 12.9 us  [shards(): received = lax.all_to_all(sent, 'gy', 0, 0, tiled=True)]
    pallas_call x6 -> x8, Pallas kernels: 21.5 us -> 24.1 us  [call(): pl.pallas_call(body, out_shape=out_shape, in_specs=in_specs, out_specs=tu...]
    unnamed x18 -> x16, local copies, waits for them, and re-layouts: 3.58 us -> 4.94 us
    all_to_all x2, waiting for transfers between devices: 7.82 us -> 8.91 us  [shards(): received = lax.all_to_all(sent, 'gx', 0, 0, tiled=True)]
    all_to_all x1 -> x2, waiting for transfers between devices: 0.01 us -> 1.04 us  [shards(): received = lax.all_to_all(sent, 'gy', 0, 0, tiled=True)]
    slice x2, local copies, waits for them, and re-layouts: 1.01 us -> 0.05 us  [edge(): return jnp.concatenate([left[rows], grid[rows], right[rows]], axis=2)]
  transfers between devices with their start and end apart: 7 -> 8, of which waited for: 1 -> 3; matrix products, arithmetic and copies ran while one was open for 1% -> 1% of each run, Pallas kernels for 23% -> 26%
where the time goes in v6:
time: 79.5 us; the launch traced here: 78.7 us
  starting transfers between devices  38.6 us (49%)
  Pallas kernels  24.1 us (30%)
  waiting for transfers between devices  9.96 us (13%)
  local copies, waits for them, and re-layouts  5 us (6%)
  other arithmetic  0.86 us (1%)
    pallas_call x8, Pallas kernels, call(): pl.pallas_call(body, out_shape=out_shape, in_specs=in_specs, out_specs=tu...  24.1 us
    all_to_all x2, starting transfers between devices, shards(): received = lax.all_to_all(sent, 'gx', 0, 0, tiled=True)  15.8 us
    all_to_all x2, starting transfers between devices, shards(): received = lax.all_to_all(sent, 'gy', 0, 0, tiled=True)  12.9 us
    ppermute x4, starting transfers between devices, shift(): return lax.ppermute(values, axis, pairs)  10 us
    all_to_all x2, waiting for transfers between devices, shards(): received = lax.all_to_all(sent, 'gx', 0, 0, tiled=True)  8.91 us
    unnamed x16, local copies, waits for them, and re-layouts  4.94 us
  transfers between devices with their start and end apart: 8, of which 3 were waited for; matrix products, arithmetic and copies ran while one was open for 1% of the time, Pallas kernels for 26%

profile of v6, /device:TPU:1, one launch (start us, length us, event | category | flops | bytes accessed | tf_op | source)
XLA Modules:
  0.0 78.7 jit_solution(16601158231266690744)
XLA Ops:
  0.0 2.3 %shard_map.91 = (f32[8,40,256]{2,1,0:T(8,128)}, f32[32,24,128]{2,1,0:T(8,128)}) custom-call(f32[36,4,512]{2,1,0:T(4,128)} %field_hbm.1, bf16[2,256,256]{2,1,0:T(8,128)(2,1)} %constant.19.clone.table_hbm), custom_call_target="tpu_custom_call" | custom-call | bytes 557056 | tf_op jit(solution)/shard_map/pallas_call | solution.py:94
  2.3 11.9 %all-to-all-start = ((f32[32,24,128]{2,1,0:T(8,128)}), f32[32,24,128]{2,1,0:T(8,128)S(1)}, u32[]{:S(2)}, u32[]{:S(2)}) async-start(f32[32,24,128]{2,1,0:T(8,128)} %get-tuple-element.18), calls=%async_computation | async-start | bytes 786432 | tf_op jit(solution)/shard_map/all_to_all | solution.py:410
  14.2 3.2 %collective-permute-start = (f32[8,40,256]{2,1,0:T(8,128)}, f32[8,40,256]{2,1,0:T(8,128)S(1)}, u32[]{:S(2)}, u32[]{:S(2)}) collective-permute-start(f32[8,40,256]{2,1,0:T(8,128)} %get-tuple-element.17.refs_2_), channel_id=1, source_target_pairs={{0,8},{8,16},{16,24},{24,32},{32,40},{40,48},{48,56},{56,64},{64,7... | collective-permute-start | bytes 983048 | tf_op jit(solution)/shard_map/ppermute | solution.py:374
  17.4 1.3 %collective-permute-start.1 = (f32[8,40,256]{2,1,0:T(8,128)}, f32[8,40,256]{2,1,0:T(8,128)S(1)}, u32[]{:S(2)}, u32[]{:S(2)}) collective-permute-start(f32[8,40,256]{2,1,0:T(8,128)} %get-tuple-element.17.refs_2_), channel_id=1, source_target_pairs={{8,0},{16,8},{24,16},{32,24},{40,32},{48,40},{56,48},{64,56},{72,6... | collective-permute-start | bytes 983048 | tf_op jit(solution)/shard_map/ppermute | solution.py:374
  18.7 1.4 %copy-done = f32[3,27,36,36]{3,2,1,0:T(8,128)S(1)} copy-done((f32[3,27,36,36]{3,2,1,0:T(8,128)S(1)}, f32[3,27,36,36]{3,2,1,0:T(8,128)}, u32[]{:S(2)}) %copy-start) | copy-done | bytes 419928
  20.2 1.2 %shard_map.92.refs_5_.refs_6_ = bf16[3,736,256]{2,1,0:T(8,128)(2,1)S(1)} custom-call(f32[3,27,36,36]{3,2,1,0:T(8,128)S(1)} %copy-done, s32[2]{0:T(128)S(1)} %pad_add_fusion.after.place.refs_4_.refs_5_), custom_call_target="tpu_custom_call" | custom-call | bytes 419912 | tf_op jit(solution)/shard_map/pallas_call | solution.py:94
  21.5 6.1 %all-to-all-done.received = f32[32,24,128]{2,1,0:T(8,128)S(1)} async-done(((f32[32,24,128]{2,1,0:T(8,128)}), f32[32,24,128]{2,1,0:T(8,128)S(1)}, u32[]{:S(2)}, u32[]{:S(2)}) %all-to-all-start) | async-done | bytes 393248 | tf_op jit(solution)/shard_map/all_to_all | solution.py:410
  27.5 0.9 %shard_map.93 = f32[8,24,128]{2,1,0:T(8,128)} custom-call(f32[32,24,128]{2,1,0:T(8,128)S(1)} %all-to-all-done.received, bf16[2,64,256]{2,1,0:T(8,128)(2,1)S(1)} %copy-done.4), custom_call_target="tpu_custom_call" | custom-call | bytes 458752 | tf_op jit(solution)/shard_map/pallas_call | solution.py:94
  28.4 8.3 %all-to-all-start.1 = ((f32[8,24,128]{2,1,0:T(8,128)}), f32[8,24,128]{2,1,0:T(8,128)S(1)}, u32[]{:S(2)}, u32[]{:S(2)}) async-start(f32[8,24,128]{2,1,0:T(8,128)} %shard_map.93), calls=%async_computation.1 | async-start | bytes 196608 | tf_op jit(solution)/shard_map/all_to_all | solution.py:416
  36.8 0.8 pad_maximum_fusion.1
  37.5 1.9 %collective-permute-start.3 = (f32[3,40,768]{2,1,0:T(8,128)}, f32[3,40,768]{2,1,0:T(8,128)}, u32[]{:S(2)}, u32[]{:S(2)}) collective-permute-start(f32[3,40,768]{2,1,0:T(8,128)} %pad_maximum_fusion.1), channel_id=1, source_target_pairs={{1,0},{2,1},{3,2},{4,3},{5,4},{6,5},{7,6},{9,8},{10,9},{11,10},{12... | collective-permute-start | bytes 1105928 | tf_op jit(solution)/shard_map/ppermute | solution.py:374
  39.5 3.6 %collective-permute-start.2 = (f32[3,40,768]{2,1,0:T(8,128)S(1)}, f32[3,40,768]{2,1,0:T(8,128)S(1)}, u32[]{:S(2)}, u32[]{:S(2)}) collective-permute-start(f32[3,40,768]{2,1,0:T(8,128)S(1)} %pad_maximum_fusion), channel_id=1, source_target_pairs={{0,1},{1,2},{2,3},{3,4},{4,5},{5,6},{6,7},{8,9},{9,10},{10,11},{11... | collective-permute-start | bytes 1105928 | tf_op jit(solution)/shard_map/ppermute | solution.py:374
  43.2 1.3 %copy-done.5 = f32[2,36,36,1,128]{4,3,2,1,0:T(1,128)S(1)} copy-done((f32[2,36,36,1,128]{4,3,2,1,0:T(1,128)S(1)}, f32[2,36,36,1,128]{4,3,2,1,0:T(1,128)}, u32[]{:S(2)}) %copy-start.5) | copy-done | bytes 1327128
  44.5 1.2 %copy-done.7 = bf16[2,1024,256]{2,1,0:T(8,128)(2,1)S(1)} copy-done((bf16[2,1024,256]{2,1,0:T(8,128)(2,1)S(1)}, bf16[2,1024,256]{2,1,0:T(8,128)(2,1)}, u32[]{:S(2)}) %copy-start.7) | copy-done | bytes 1048600
  45.7 2.5 %shard_map.94 = f32[8,24,128]{2,1,0:T(8,128)} custom-call(f32[8,24,128]{2,1,0:T(8,128)S(1)} %all-to-all-done.1.received, f32[2,1296,128]{2,1,0:T(8,128)S(1)} %bitcast.4, s32[1,128]{1,0:T(1,128)S(1)} %bitcast.5, s32[2]{0:T(128)S(1)} %pad_add_fusion.after.place.refs_4_.refs_5_, bf16[2,1024,256]{2,1,0:T(8,128)(2,1)S(1)} %copy-done.7), custom_call_target="tpu_custom_call" | custom-call | flops 8589934592 | bytes 2474504 | tf_op jit(solution)/shard_map/pallas_call | solution.py:94
  48.2 4.6 %all-to-all-start.2 = ((f32[8,24,128]{2,1,0:T(8,128)}), f32[8,24,128]{2,1,0:T(8,128)S(1)}, u32[]{:S(2)}, u32[]{:S(2)}) async-start(f32[8,24,128]{2,1,0:T(8,128)} %shard_map.94), calls=%async_computation.2 | async-start | bytes 196608 | tf_op jit(solution)/shard_map/all_to_all | solution.py:433
  52.8 3.9 %shard_map.95.refs_0_ = f32[6,40,512]{2,1,0:T(8,128)S(1)} custom-call(f32[3,40,768]{2,1,0:T(8,128)S(1)} %collective-permute-done.2.refs_0_, f32[8,40,256]{2,1,0:T(8,128)S(1)} %collective-permute-done.refs_1_, f32[8,40,256]{2,1,0:T(8,128)S(1)} %copy-done.1, f32[8,40,256]{2,1,0:T(8,128)S(1)} %collective-permute-done.1.refs_3_, ...), custom_call_target="tpu_custom_call" | custom-call | bytes 2482184 | tf_op jit(solution)/shard_map/pallas_call | solution.py:94
  56.7 1.0 %all-to-all-done.2.received = f32[8,24,128]{2,1,0:T(8,128)S(1)} async-done(((f32[8,24,128]{2,1,0:T(8,128)}), f32[8,24,128]{2,1,0:T(8,128)S(1)}, u32[]{:S(2)}, u32[]{:S(2)}) %all-to-all-start.2) | async-done | bytes 98336 | tf_op jit(solution)/shard_map/all_to_all | solution.py:433
  57.7 1.1 %shard_map.96 = f32[32,24,128]{2,1,0:T(8,128)} custom-call(f32[8,24,128]{2,1,0:T(8,128)S(1)} %all-to-all-done.2.received, bf16[2,256,64]{2,1,0:T(8,128)(2,1)S(1)} %copy-done.3), custom_call_target="tpu_custom_call" | custom-call | bytes 163840 | tf_op jit(solution)/shard_map/pallas_call | solution.py:94
  58.8 3.9 %all-to-all-start.3 = ((f32[32,24,128]{2,1,0:T(8,128)}), f32[32,24,128]{2,1,0:T(8,128)S(1)}, u32[]{:S(2)}, u32[]{:S(2)}) async-start(f32[32,24,128]{2,1,0:T(8,128)} %shard_map.96), calls=%async_computation.3 | async-start | bytes 786432 | tf_op jit(solution)/shard_map/all_to_all | solution.py:448
  62.7 11.0 %shard_map.97.third = f32[8,40,256]{2,1,0:T(8,128)S(1)} custom-call(f32[6,40,512]{2,1,0:T(8,128)S(1)} %shard_map.95.refs_0_, f32[8,40,256]{2,1,0:T(8,128)S(1)} %collective-permute-done.refs_1_, f32[8,40,256]{2,1,0:T(8,128)S(1)} %copy-done.1, f32[8,40,256]{2,1,0:T(8,128)S(1)} %collective-permute-done.1.refs_3_, f32[3,40,768]{2,1,0:T(8,128)} %collective-permute-done.3.refs_4_, ...), custom_call_target="tpu_custom_call" | custom-call | flops 12884901888 | bytes 2973704 | tf_op jit(solution)/shard_map/pallas_call | solution.py:94
  73.7 2.8 %all-to-all-done.3.received = f32[32,24,128]{2,1,0:T(8,128)S(1)} async-done(((f32[32,24,128]{2,1,0:T(8,128)}), f32[32,24,128]{2,1,0:T(8,128)S(1)}, u32[]{:S(2)}, u32[]{:S(2)}) %all-to-all-start.3) | async-done | bytes 393248 | tf_op jit(solution)/shard_map/all_to_all | solution.py:448
  76.6 0.9 %copy-done.2 = bf16[2,256,256]{2,1,0:T(8,128)(2,1)S(1)} copy-done((bf16[2,256,256]{2,1,0:T(8,128)(2,1)S(1)}, bf16[2,256,256]{2,1,0:T(8,128)(2,1)}, u32[]{:S(2)}) %copy-start.2) | copy-done | bytes 262168
  77.5 1.2 %shard_map.98 = f32[36,4,512]{2,1,0:T(4,128)} custom-call(f32[32,24,128]{2,1,0:T(8,128)S(1)} %all-to-all-done.3.received, f32[8,40,256]{2,1,0:T(8,128)S(1)} %shard_map.97.third, bf16[2,256,256]{2,1,0:T(8,128)(2,1)S(1)} %copy-done.2), custom_call_target="tpu_custom_call" | custom-call | bytes 983040 | tf_op jit(solution)/shard_map/pallas_call | solution.py:94
  (21 shorter events, 0.2 us)
Async XLA Ops:
  2.3 25.2 %all-to-all-start = ((f32[32,24,128]{2,1,0:T(8,128)}), f32[32,24,128]{2,1,0:T(8,128)S(1)}, u32[]{:S(2)}, u32[]{:S(2)}) async-start(f32[32,24,128]{2,1,0:T(8,128)} %get-tuple-element.18), calls=%async_computation | async-start | bytes 786432 | tf_op jit(solution)/shard_map/all_to_all | solution.py:410
  14.2 22.5 %collective-permute-start = (f32[8,40,256]{2,1,0:T(8,128)}, f32[8,40,256]{2,1,0:T(8,128)S(1)}, u32[]{:S(2)}, u32[]{:S(2)}) collective-permute-start(f32[8,40,256]{2,1,0:T(8,128)} %get-tuple-element.17.refs_2_), channel_id=1, source_target_pairs={{0,8},{8,16},{16,24},{24,32},{32,40},{40,48},{48,56},{56,64},{64,7... | collective-permute-start | bytes 983048 | tf_op jit(solution)/shard_map/ppermute | solution.py:374
  17.4 19.4 %collective-permute-start.1 = (f32[8,40,256]{2,1,0:T(8,128)}, f32[8,40,256]{2,1,0:T(8,128)S(1)}, u32[]{:S(2)}, u32[]{:S(2)}) collective-permute-start(f32[8,40,256]{2,1,0:T(8,128)} %get-tuple-element.17.refs_2_), channel_id=1, source_target_pairs={{8,0},{16,8},{24,16},{32,24},{40,32},{48,40},{56,48},{64,56},{72,6... | collective-permute-start | bytes 983048 | tf_op jit(solution)/shard_map/ppermute | solution.py:374
  18.7 1.4 %copy-start = (f32[3,27,36,36]{3,2,1,0:T(8,128)S(1)}, f32[3,27,36,36]{3,2,1,0:T(8,128)}, u32[]{:S(2)}) copy-start(f32[3,27,36,36]{3,2,1,0:T(8,128)} %kernels.1) | copy-start | bytes 1259716
  20.2 1.3 %copy-start.1 = (f32[8,40,256]{2,1,0:T(8,128)S(1)}, f32[8,40,256]{2,1,0:T(8,128)}, u32[]{:S(2)}) copy-start(f32[8,40,256]{2,1,0:T(8,128)} %get-tuple-element.17.refs_2_) | copy-start | bytes 983044
  20.2 7.4 %copy-start.4 = (bf16[2,64,256]{2,1,0:T(8,128)(2,1)S(1)}, bf16[2,64,256]{2,1,0:T(8,128)(2,1)}, u32[]{:S(2)}) copy-start(bf16[2,64,256]{2,1,0:T(8,128)(2,1)} %constant.20.clone.table) | copy-start | bytes 196612
  28.4 14.7 %copy-start.6 = (s32[128]{0:T(128)S(1)}, s32[128]{0:T(128)}, u32[]{:S(2)}) copy-start(s32[128]{0:T(128)} %param.11) | copy-start | bytes 1540
  28.4 14.7 %all-to-all-start.1 = ((f32[8,24,128]{2,1,0:T(8,128)}), f32[8,24,128]{2,1,0:T(8,128)S(1)}, u32[]{:S(2)}, u32[]{:S(2)}) async-start(f32[8,24,128]{2,1,0:T(8,128)} %shard_map.93), calls=%async_computation.1 | async-start | bytes 196608 | tf_op jit(solution)/shard_map/all_to_all | solution.py:416
  37.5 25.1 %collective-permute-start.3 = (f32[3,40,768]{2,1,0:T(8,128)}, f32[3,40,768]{2,1,0:T(8,128)}, u32[]{:S(2)}, u32[]{:S(2)}) collective-permute-start(f32[3,40,768]{2,1,0:T(8,128)} %pad_maximum_fusion.1), channel_id=1, source_target_pairs={{1,0},{2,1},{3,2},{4,3},{5,4},{6,5},{7,6},{9,8},{10,9},{11,10},{12... | collective-permute-start | bytes 1105928 | tf_op jit(solution)/shard_map/ppermute | solution.py:374
  39.5 13.3 %collective-permute-start.2 = (f32[3,40,768]{2,1,0:T(8,128)S(1)}, f32[3,40,768]{2,1,0:T(8,128)S(1)}, u32[]{:S(2)}, u32[]{:S(2)}) collective-permute-start(f32[3,40,768]{2,1,0:T(8,128)S(1)} %pad_maximum_fusion), channel_id=1, source_target_pairs={{0,1},{1,2},{2,3},{3,4},{4,5},{5,6},{6,7},{8,9},{9,10},{10,11},{11... | collective-permute-start | bytes 1105928 | tf_op jit(solution)/shard_map/ppermute | solution.py:374
  43.2 1.3 %copy-start.5 = (f32[2,36,36,1,128]{4,3,2,1,0:T(1,128)S(1)}, f32[2,36,36,1,128]{4,3,2,1,0:T(1,128)}, u32[]{:S(2)}) copy-start(f32[2,36,36,1,128]{4,3,2,1,0:T(1,128)} %param.10) | copy-start | bytes 3981316
  44.5 1.2 %copy-start.7 = (bf16[2,1024,256]{2,1,0:T(8,128)(2,1)S(1)}, bf16[2,1024,256]{2,1,0:T(8,128)(2,1)}, u32[]{:S(2)}) copy-start(bf16[2,1024,256]{2,1,0:T(8,128)(2,1)} %constant.21.clone.y_tables) | copy-start | bytes 3145732
  48.2 9.5 %all-to-all-start.2 = ((f32[8,24,128]{2,1,0:T(8,128)}), f32[8,24,128]{2,1,0:T(8,128)S(1)}, u32[]{:S(2)}, u32[]{:S(2)}) async-start(f32[8,24,128]{2,1,0:T(8,128)} %shard_map.94), calls=%async_computation.2 | async-start | bytes 196608 | tf_op jit(solution)/shard_map/all_to_all | solution.py:433
  52.7 5.0 %copy-start.3 = (bf16[2,256,64]{2,1,0:T(8,128)(2,1)S(1)}, bf16[2,256,64]{2,1,0:T(8,128)(2,1)}, u32[]{:S(2)}) copy-start(bf16[2,256,64]{2,1,0:T(8,128)(2,1)} %constant.22.clone.table) | copy-start | bytes 196612
  58.8 17.8 %all-to-all-start.3 = ((f32[32,24,128]{2,1,0:T(8,128)}), f32[32,24,128]{2,1,0:T(8,128)S(1)}, u32[]{:S(2)}, u32[]{:S(2)}) async-start(f32[32,24,128]{2,1,0:T(8,128)} %shard_map.96), calls=%async_computation.3 | async-start | bytes 786432 | tf_op jit(solution)/shard_map/all_to_all | solution.py:448
  76.5 1.0 %copy-start.2 = (bf16[2,256,256]{2,1,0:T(8,128)(2,1)S(1)}, bf16[2,256,256]{2,1,0:T(8,128)(2,1)}, u32[]{:S(2)}) copy-start(bf16[2,256,256]{2,1,0:T(8,128)(2,1)} %constant.23.clone.table) | copy-start | bytes 786436

commit v7 on v5

--- a/solution.py
+++ b/solution.py
@@ -12,6 +12,7 @@
 NZ = 64
 KY = 32
 MIX = 8192
+XOUT = 8192
 CONV = 12288
 FULL = 60
 CP = 40
@@ -197,17 +198,18 @@
 ROW = 368
 
 
-def make_taps(kernels, which, out_ref, scratch):
+def taps_body(kernels, after, out_ref, scratch):
     channels = kernels.shape[2]
-    scratch[...] = jnp.zeros(scratch.shape, F32)
-    for tap in range(27):
-        row, lane = CP * (tap % 3), CP * (tap // 3)
-        scratch[row : row + channels, lane : lane + channels] = kernels[which, tap]
-    high, low = split(scratch[...].T[:ROW])
-    out_ref[:ROW, :128] = high
-    out_ref[:ROW, 128:] = high
-    out_ref[ROW:, :128] = low
-    out_ref[ROW:, 128:] = jnp.zeros((ROW, 128), BF16)
+    for r in range(3):
+        scratch[...] = jnp.zeros(scratch.shape, F32)
+        for tap in range(27):
+            row, lane = CP * (tap % 3), CP * (tap // 3)
+            scratch[row : row + channels, lane : lane + channels] = kernels[r, tap]
+        high, low = split(scratch[...].T[:ROW])
+        out_ref[r, :ROW, :128] = high
+        out_ref[r, :ROW, 128:] = high
+        out_ref[r, ROW:, :128] = low
+        out_ref[r, ROW:, 128:] = jnp.zeros((ROW, 128), BF16)
 
 
 def convolve_rows(load_row, rows_in, width, taps, refs, finish):
@@ -303,10 +305,9 @@
         target[first : first + count, :, width * i : width * i + width] = source[rows]
 
 
-def convolutions_body(sizes, before, left, own, right, after, place, kernels, out_ref, *refs):
-    rows, first, second, table, taps = refs[:5]
-    wide, narrow = refs[5:10], refs[10:]
-    make_taps(kernels, 0, taps, table)
+def convolutions_body(sizes, before, left, own, right, after, place, taps, out_ref, *refs):
+    rows, first, second = refs[:3]
+    wide, narrow = refs[3:8], refs[8:]
     count = own.shape[0]
     rows[0:3] = before[...]
     join((left, own, right), slice(0, count), rows, 3)
@@ -324,11 +325,9 @@
     def finish_third(row, tiles):
         out_ref[row] = jnp.concatenate(tiles[1:3], axis=1)
 
-    convolve_rows(lambda i: rows[i], count + 6, 768, taps, wide, finish_first)
-    make_taps(kernels, 1, taps, table)
-    convolve_rows(lambda i: first[i], count + 4, 512, taps, narrow, finish_second)
-    make_taps(kernels, 2, taps, table)
-    convolve_rows(lambda i: second[i], count + 2, 512, taps, narrow, finish_third)
+    convolve_rows(lambda i: rows[i], count + 6, 768, taps.at[0], wide, finish_first)
+    convolve_rows(lambda i: first[i], count + 4, 512, taps.at[1], narrow, finish_second)
+    convolve_rows(lambda i: second[i], count + 2, 512, taps.at[2], narrow, finish_third)
 
 
 def last_body(received, third, table, out_ref):
@@ -380,7 +379,13 @@
     )
     left = shift(grid, "gx", 1)
     right = shift(grid, "gx", -1)
+    behind, _ = lax.optimization_barrier((place, sent))
+    taps = call(
+        taps_body, jax.ShapeDtypeStruct((3, 2 * ROW, 256), BF16), conv_kernels, behind,
+        scratch=[pltpu.VMEM((128, 384), F32)], smem=(1,),
+    )
     received = lax.all_to_all(sent, "gx", 0, 0, tiled=True)
+    received, taps = lax.optimization_barrier((received, taps))
 
     sent = call(rows_body, jax.ShapeDtypeStruct((size_y, 24, LANES), F32), received, x_in)
 
@@ -391,7 +396,6 @@
         return jnp.concatenate([left[rows], grid[rows], right[rows]], axis=2)
 
     before = shift(edge(slice(cells_y - 3, cells_y)), "gy", 1)
-    after = shift(edge(slice(0, 3)), "gy", -1)
     weights = mix_weights.reshape(2, channels * channels, kx_local * KY)
     sent = call(
         mix_body,
@@ -401,20 +405,22 @@
         + [pltpu.VMEM((LANES, kx_local * KY), F32)] * 2,
         smem=(3,), flops=MIX << 20,
     )
+    left, right, _ = lax.optimization_barrier((left, right, sent))
+    after = shift(edge(slice(0, 3)), "gy", -1)
     received = lax.all_to_all(sent, "gy", 0, 0, tiled=True)
-    sent = call(rows_body, jax.ShapeDtypeStruct((size_x, 24, LANES), F32), received, x_out)
+    sent = call(
+        rows_body, jax.ShapeDtypeStruct((size_x, 24, LANES), F32), received, x_out, flops=XOUT << 20
+    )
     before, after, _ = lax.optimization_barrier((before, after, sent))
     received = lax.all_to_all(sent, "gx", 0, 0, tiled=True)
     third = call(
         lambda *refs: convolutions_body(sizes, *refs),
         jax.ShapeDtypeStruct((cells_y, CP, cells_x * NZ), F32),
-        before, left, grid, right, after, place, conv_kernels,
+        before, left, grid, right, after, place, taps,
         scratch=[
             pltpu.VMEM((cells_y + 6, CP, 768), F32),
             pltpu.VMEM((cells_y + 4, CP, 512), F32),
             pltpu.VMEM((cells_y + 2, CP, 512), F32),
-            pltpu.VMEM((128, 384), F32),
-            pltpu.VMEM((2 * ROW, 256), BF16),
         ]
         + conv_scratch(768) + conv_scratch(512),
         smem=(5,), flops=CONV << 20,

time: 78.2 us -> 77.5 us (level)
  blocking collectives: 9.34 us -> 0 us
  starting transfers between devices: 33.9 us -> 38.1 us
  waiting for transfers between devices: 7.83 us -> 9.51 us
  other arithmetic: 0.13 us -> 1.63 us
  Pallas kernels: 21.5 us -> 22.3 us
    all_to_all x1 -> x0, blocking collectives: 9.34 us -> none  [shards(): received = lax.all_to_all(sent, 'gy', 0, 0, tiled=True)]
    all_to_all x1 -> x2, starting transfers between devices: 8.17 us -> 12.4 us  [shards(): received = lax.all_to_all(sent, 'gy', 0, 0, tiled=True)]
    all_to_all x1 -> x2, waiting for transfers between devices: 0.01 us -> 2.8 us  [shards(): received = lax.all_to_all(sent, 'gy', 0, 0, tiled=True)]
    concatenate x2, other arithmetic: 0.05 us -> 1.55 us  [edge(): return jnp.concatenate([left[rows], grid[rows], right[rows]], axis=2)]
    unnamed x18, local copies, waits for them, and re-layouts: 3.58 us -> 4.87 us
    all_to_all x2, waiting for transfers between devices: 7.82 us -> 6.69 us  [shards(): received = lax.all_to_all(sent, 'gx', 0, 0, tiled=True)]
    slice x2 -> x5, local copies, waits for them, and re-layouts: 1.01 us -> 0.06 us  [edge(): return jnp.concatenate([left[rows], grid[rows], right[rows]], axis=2)]
    pallas_call x6 -> x7, Pallas kernels: 21.5 us -> 22.3 us  [call(): pl.pallas_call(body, out_shape=out_shape, in_specs=in_specs, out_specs=tu...]
  transfers between devices with their start and end apart: 7 -> 8, of which waited for: 1 -> 4; matrix products, arithmetic and copies ran while one was open for 1% -> 2% of each run, Pallas kernels for 23% -> 25%
where the time goes in v7:
time: 77.5 us; the launch traced here: 76.6 us
  starting transfers between devices  38.1 us (49%)
  Pallas kernels  22.3 us (29%)
  waiting for transfers between devices  9.51 us (12%)
  local copies, waits for them, and re-layouts  4.92 us (6%)
  other arithmetic  1.63 us (2%)
    pallas_call x7, Pallas kernels, call(): pl.pallas_call(body, out_shape=out_shape, in_specs=in_specs, out_specs=tu...  22.3 us
    all_to_all x2, starting transfers between devices, shards(): received = lax.all_to_all(sent, 'gx', 0, 0, tiled=True)  15.8 us
    all_to_all x2, starting transfers between devices, shards(): received = lax.all_to_all(sent, 'gy', 0, 0, tiled=True)  12.4 us
    ppermute x4, starting transfers between devices, shift(): return lax.ppermute(values, axis, pairs)  9.98 us
    all_to_all x2, waiting for transfers between devices, shards(): received = lax.all_to_all(sent, 'gx', 0, 0, tiled=True)  6.69 us
    unnamed x18, local copies, waits for them, and re-layouts  4.87 us
    all_to_all x2, waiting for transfers between devices, shards(): received = lax.all_to_all(sent, 'gy', 0, 0, tiled=True)  2.8 us
    concatenate x2, other arithmetic, edge(): return jnp.concatenate([left[rows], grid[rows], right[rows]], axis=2)  1.55 us
  transfers between devices with their start and end apart: 8, of which 4 were waited for; matrix products, arithmetic and copies ran while one was open for 2% of the time, Pallas kernels for 25%

profile of v7, /device:TPU:1, one launch (start us, length us, event | category | flops | bytes accessed | tf_op | source)
XLA Modules:
  0.0 76.6 jit_solution(7657016656358644455)
XLA Ops:
  0.0 2.3 %shard_map.100 = (f32[8,40,256]{2,1,0:T(8,128)}, f32[32,24,128]{2,1,0:T(8,128)}) custom-call(f32[36,4,512]{2,1,0:T(4,128)} %field_hbm.1, bf16[2,256,256]{2,1,0:T(8,128)(2,1)} %constant.21.clone.table_hbm), custom_call_target="tpu_custom_call" | custom-call | bytes 557056 | tf_op jit(solution)/shard_map/pallas_call | solution.py:93
  2.3 11.9 %all-to-all-start = ((f32[32,24,128]{2,1,0:T(8,128)}), f32[32,24,128]{2,1,0:T(8,128)S(1)}, u32[]{:S(2)}, u32[]{:S(2)}) async-start(f32[32,24,128]{2,1,0:T(8,128)} %get-tuple-element.16), calls=%async_computation | async-start | bytes 786432 | tf_op jit(solution)/shard_map/all_to_all | solution.py:387
  14.2 3.2 %collective-permute-start = (f32[8,40,256]{2,1,0:T(8,128)}, f32[8,40,256]{2,1,0:T(8,128)S(1)}, u32[]{:S(2)}, u32[]{:S(2)}) collective-permute-start(f32[8,40,256]{2,1,0:T(8,128)} %get-tuple-element.19.refs_2_), channel_id=1, source_target_pairs={{0,8},{8,16},{16,24},{24,32},{32,40},{40,48},{48,56},{56,64},{64,7... | collective-permute-start | bytes 983048 | tf_op jit(solution)/shard_map/ppermute | solution.py:351
  17.4 1.3 %collective-permute-start.1 = (f32[8,40,256]{2,1,0:T(8,128)}, f32[8,40,256]{2,1,0:T(8,128)S(1)}, u32[]{:S(2)}, u32[]{:S(2)}) collective-permute-start(f32[8,40,256]{2,1,0:T(8,128)} %get-tuple-element.19.refs_2_), channel_id=1, source_target_pairs={{8,0},{16,8},{24,16},{32,24},{40,32},{48,40},{56,48},{64,56},{72,6... | collective-permute-start | bytes 983048 | tf_op jit(solution)/shard_map/ppermute | solution.py:351
  18.7 1.4 %copy-done = f32[3,27,36,36]{3,2,1,0:T(8,128)S(1)} copy-done((f32[3,27,36,36]{3,2,1,0:T(8,128)S(1)}, f32[3,27,36,36]{3,2,1,0:T(8,128)}, u32[]{:S(2)}) %copy-start) | copy-done | bytes 419928
  20.2 1.2 %shard_map.101.refs_6_ = bf16[3,736,256]{2,1,0:T(8,128)(2,1)S(1)} custom-call(f32[3,27,36,36]{3,2,1,0:T(8,128)S(1)} %copy-done, s32[2]{0:T(128)S(1)} %pad_add_fusion.after.place.refs_5_), custom_call_target="tpu_custom_call" | custom-call | bytes 419912 | tf_op jit(solution)/shard_map/pallas_call | solution.py:93
  21.5 6.1 %all-to-all-done.received = f32[32,24,128]{2,1,0:T(8,128)S(1)} async-done(((f32[32,24,128]{2,1,0:T(8,128)}), f32[32,24,128]{2,1,0:T(8,128)S(1)}, u32[]{:S(2)}, u32[]{:S(2)}) %all-to-all-start) | async-done | bytes 393248 | tf_op jit(solution)/shard_map/all_to_all | solution.py:387
  27.5 0.9 %shard_map.102 = f32[8,24,128]{2,1,0:T(8,128)} custom-call(f32[32,24,128]{2,1,0:T(8,128)S(1)} %all-to-all-done.received, bf16[2,64,256]{2,1,0:T(8,128)(2,1)S(1)} %copy-done.3), custom_call_target="tpu_custom_call" | custom-call | bytes 458752 | tf_op jit(solution)/shard_map/pallas_call | solution.py:93
  28.4 8.2 %all-to-all-start.1 = ((f32[8,24,128]{2,1,0:T(8,128)}), f32[8,24,128]{2,1,0:T(8,128)S(1)}, u32[]{:S(2)}, u32[]{:S(2)}) async-start(f32[8,24,128]{2,1,0:T(8,128)} %shard_map.102), calls=%async_computation.1 | async-start | bytes 196608 | tf_op jit(solution)/shard_map/all_to_all | solution.py:393
  36.6 0.8 pad_maximum_fusion
  37.4 3.5 %collective-permute-start.2 = (f32[3,40,768]{2,1,0:T(8,128)}, f32[3,40,768]{2,1,0:T(8,128)S(1)}, u32[]{:S(2)}, u32[]{:S(2)}) collective-permute-start(f32[3,40,768]{2,1,0:T(8,128)} %pad_maximum_fusion), channel_id=1, source_target_pairs={{0,1},{1,2},{2,3},{3,4},{4,5},{5,6},{6,7},{8,9},{9,10},{10,11},{11... | collective-permute-start | bytes 1105928 | tf_op jit(solution)/shard_map/ppermute | solution.py:351
  40.9 0.6 all-to-all-done.1.received
  41.6 1.3 %copy-done.4 = f32[2,36,36,1,128]{4,3,2,1,0:T(1,128)S(1)} copy-done((f32[2,36,36,1,128]{4,3,2,1,0:T(1,128)S(1)}, f32[2,36,36,1,128]{4,3,2,1,0:T(1,128)}, u32[]{:S(2)}) %copy-start.4) | copy-done | bytes 1327128
  42.9 1.0 %copy-done.6 = bf16[2,256,512]{2,1,0:T(8,128)(2,1)S(1)} copy-done((bf16[2,256,512]{2,1,0:T(8,128)(2,1)S(1)}, bf16[2,256,512]{2,1,0:T(8,128)(2,1)}, u32[]{:S(2)}) %copy-start.6) | copy-done | bytes 524312
  43.9 1.0 %copy-done.7 = bf16[2,512,256]{2,1,0:T(8,128)(2,1)S(1)} copy-done((bf16[2,512,256]{2,1,0:T(8,128)(2,1)S(1)}, bf16[2,512,256]{2,1,0:T(8,128)(2,1)}, u32[]{:S(2)}) %copy-start.7) | copy-done | bytes 524312
  45.0 2.5 %shard_map.103 = f32[8,24,128]{2,1,0:T(8,128)} custom-call(f32[8,24,128]{2,1,0:T(8,128)S(1)} %all-to-all-done.1.received, f32[2,1296,128]{2,1,0:T(8,128)S(1)} %bitcast.4, s32[1,128]{1,0:T(1,128)S(1)} %bitcast.5, s32[2]{0:T(128)S(1)} %pad_add_fusion.after.place.refs_5_, bf16[2,256,512]{2,1,0:T(8,128)(2,1)S(1)} %copy-done.6, bf16[2,512,256]{2,1,0:T(8,128)(2,1)S(1)} %copy-done.7), custom_call_target="tpu_custom_call" | custom-call | flops 8589934592 | bytes 2474504 | tf_op jit(solution)/shard_map/pallas_call | solution.py:93
  47.4 4.2 %all-to-all-start.2 = ((f32[8,24,128]{2,1,0:T(8,128)}), f32[8,24,128]{2,1,0:T(8,128)S(1)}, u32[]{:S(2)}, u32[]{:S(2)}) async-start(f32[8,24,128]{2,1,0:T(8,128)} %shard_map.103), calls=%async_computation.2 | async-start | bytes 196608 | tf_op jit(solution)/shard_map/all_to_all | solution.py:410
  51.7 0.8 %pad_maximum_fusion.1 = f32[3,40,768]{2,1,0:T(8,128)} fusion(f32[3,40,256]{2,1,0:T(8,128)S(1)} %slice.23, f32[3,40,256]{2,1,0:T(8,128)S(1)} %get-tuple-element.27, f32[3,40,256]{2,1,0:T(8,128)S(1)} %slice.21), kind=kLoop, calls=%fused_computation.1 | loop fusion | flops 184320 | bytes 737280 | tf_op jit(solution)/shard_map/concatenate | solution.py:396
  52.5 2.0 %collective-permute-start.3 = (f32[3,40,768]{2,1,0:T(8,128)}, f32[3,40,768]{2,1,0:T(8,128)}, u32[]{:S(2)}, u32[]{:S(2)}) collective-permute-start(f32[3,40,768]{2,1,0:T(8,128)} %pad_maximum_fusion.1), channel_id=1, source_target_pairs={{1,0},{2,1},{3,2},{4,3},{5,4},{6,5},{7,6},{9,8},{10,9},{11,10},{12... | collective-permute-start | bytes 1105928 | tf_op jit(solution)/shard_map/ppermute | solution.py:351
  54.5 2.2 %all-to-all-done.2.received = f32[8,24,128]{2,1,0:T(8,128)S(1)} async-done(((f32[8,24,128]{2,1,0:T(8,128)}), f32[8,24,128]{2,1,0:T(8,128)S(1)}, u32[]{:S(2)}, u32[]{:S(2)}) %all-to-all-start.2) | async-done | bytes 98336 | tf_op jit(solution)/shard_map/all_to_all | solution.py:410
  56.7 1.0 %shard_map.104 = f32[32,24,128]{2,1,0:T(8,128)} custom-call(f32[8,24,128]{2,1,0:T(8,128)S(1)} %all-to-all-done.2.received, bf16[2,256,64]{2,1,0:T(8,128)(2,1)S(1)} %copy-done.8), custom_call_target="tpu_custom_call" | custom-call | flops 8589934592 | bytes 163840 | tf_op jit(solution)/shard_map/pallas_call | solution.py:93
  57.7 3.9 %all-to-all-start.3 = ((f32[32,24,128]{2,1,0:T(8,128)}), f32[32,24,128]{2,1,0:T(8,128)S(1)}, u32[]{:S(2)}, u32[]{:S(2)}) async-start(f32[32,24,128]{2,1,0:T(8,128)} %shard_map.104), calls=%async_computation.3 | async-start | bytes 786432 | tf_op jit(solution)/shard_map/all_to_all | solution.py:415
  61.6 13.2 %shard_map.105.third = f32[8,40,256]{2,1,0:T(8,128)S(1)} custom-call(f32[3,40,768]{2,1,0:T(8,128)S(1)} %collective-permute-done.2.refs_0_, f32[8,40,256]{2,1,0:T(8,128)S(1)} %collective-permute-done.refs_1_, f32[8,40,256]{2,1,0:T(8,128)S(1)} %copy-done.2, f32[8,40,256]{2,1,0:T(8,128)S(1)} %collective-permute-done.1.refs_3_, ...), custom_call_target="tpu_custom_call" | custom-call | flops 12884901888 | bytes 2850824 | tf_op jit(solution)/shard_map/pallas_call | solution.py:93
  75.5 1.2 %shard_map.106 = f32[36,4,512]{2,1,0:T(4,128)} custom-call(f32[32,24,128]{2,1,0:T(8,128)S(1)} %all-to-all-done.3.received, f32[8,40,256]{2,1,0:T(8,128)S(1)} %shard_map.105.third, bf16[2,256,256]{2,1,0:T(8,128)(2,1)S(1)} %copy-done.1), custom_call_target="tpu_custom_call" | custom-call | bytes 983040 | tf_op jit(solution)/shard_map/pallas_call | solution.py:93
  (25 shorter events, 0.8 us)
Async XLA Ops:
  2.3 25.2 %all-to-all-start = ((f32[32,24,128]{2,1,0:T(8,128)}), f32[32,24,128]{2,1,0:T(8,128)S(1)}, u32[]{:S(2)}, u32[]{:S(2)}) async-start(f32[32,24,128]{2,1,0:T(8,128)} %get-tuple-element.16), calls=%async_computation | async-start | bytes 786432 | tf_op jit(solution)/shard_map/all_to_all | solution.py:387
  14.2 22.4 %collective-permute-start = (f32[8,40,256]{2,1,0:T(8,128)}, f32[8,40,256]{2,1,0:T(8,128)S(1)}, u32[]{:S(2)}, u32[]{:S(2)}) collective-permute-start(f32[8,40,256]{2,1,0:T(8,128)} %get-tuple-element.19.refs_2_), channel_id=1, source_target_pairs={{0,8},{8,16},{16,24},{24,32},{32,40},{40,48},{48,56},{56,64},{64,7... | collective-permute-start | bytes 983048 | tf_op jit(solution)/shard_map/ppermute | solution.py:351
  17.4 19.2 %collective-permute-start.1 = (f32[8,40,256]{2,1,0:T(8,128)}, f32[8,40,256]{2,1,0:T(8,128)S(1)}, u32[]{:S(2)}, u32[]{:S(2)}) collective-permute-start(f32[8,40,256]{2,1,0:T(8,128)} %get-tuple-element.19.refs_2_), channel_id=1, source_target_pairs={{8,0},{16,8},{24,16},{32,24},{40,32},{48,40},{56,48},{64,56},{72,6... | collective-permute-start | bytes 983048 | tf_op jit(solution)/shard_map/ppermute | solution.py:351
  18.7 1.4 %copy-start = (f32[3,27,36,36]{3,2,1,0:T(8,128)S(1)}, f32[3,27,36,36]{3,2,1,0:T(8,128)}, u32[]{:S(2)}) copy-start(f32[3,27,36,36]{3,2,1,0:T(8,128)} %kernels.1) | copy-start | bytes 1259716
  20.2 1.3 %copy-start.2 = (f32[8,40,256]{2,1,0:T(8,128)S(1)}, f32[8,40,256]{2,1,0:T(8,128)}, u32[]{:S(2)}) copy-start(f32[8,40,256]{2,1,0:T(8,128)} %get-tuple-element.19.refs_2_) | copy-start | bytes 983044
  20.2 7.4 %copy-start.3 = (bf16[2,64,256]{2,1,0:T(8,128)(2,1)S(1)}, bf16[2,64,256]{2,1,0:T(8,128)(2,1)}, u32[]{:S(2)}) copy-start(bf16[2,64,256]{2,1,0:T(8,128)(2,1)} %constant.22.clone.table) | copy-start | bytes 196612
  21.4 20.1 %copy-start.5 = (s32[128]{0:T(128)S(1)}, s32[128]{0:T(128)}, u32[]{:S(2)}) copy-start(s32[128]{0:T(128)} %param.12) | copy-start | bytes 1540
  28.4 13.2 %all-to-all-start.1 = ((f32[8,24,128]{2,1,0:T(8,128)}), f32[8,24,128]{2,1,0:T(8,128)S(1)}, u32[]{:S(2)}, u32[]{:S(2)}) async-start(f32[8,24,128]{2,1,0:T(8,128)} %shard_map.102), calls=%async_computation.1 | async-start | bytes 196608 | tf_op jit(solution)/shard_map/all_to_all | solution.py:393
  37.4 24.2 %collective-permute-start.2 = (f32[3,40,768]{2,1,0:T(8,128)}, f32[3,40,768]{2,1,0:T(8,128)S(1)}, u32[]{:S(2)}, u32[]{:S(2)}) collective-permute-start(f32[3,40,768]{2,1,0:T(8,128)} %pad_maximum_fusion), channel_id=1, source_target_pairs={{0,1},{1,2},{2,3},{3,4},{4,5},{5,6},{6,7},{8,9},{9,10},{10,11},{11... | collective-permute-start | bytes 1105928 | tf_op jit(solution)/shard_map/ppermute | solution.py:351
  41.6 1.3 %copy-start.4 = (f32[2,36,36,1,128]{4,3,2,1,0:T(1,128)S(1)}, f32[2,36,36,1,128]{4,3,2,1,0:T(1,128)}, u32[]{:S(2)}) copy-start(f32[2,36,36,1,128]{4,3,2,1,0:T(1,128)} %param.11) | copy-start | bytes 3981316
  42.9 1.0 %copy-start.6 = (bf16[2,256,512]{2,1,0:T(8,128)(2,1)S(1)}, bf16[2,256,512]{2,1,0:T(8,128)(2,1)}, u32[]{:S(2)}) copy-start(bf16[2,256,512]{2,1,0:T(8,128)(2,1)} %constant.23.clone.y_in) | copy-start | bytes 1572868
  43.9 1.0 %copy-start.7 = (bf16[2,512,256]{2,1,0:T(8,128)(2,1)S(1)}, bf16[2,512,256]{2,1,0:T(8,128)(2,1)}, u32[]{:S(2)}) copy-start(bf16[2,512,256]{2,1,0:T(8,128)(2,1)} %constant.24.clone.y_out) | copy-start | bytes 1572868
  47.4 9.2 %copy-start.8 = (bf16[2,256,64]{2,1,0:T(8,128)(2,1)S(1)}, bf16[2,256,64]{2,1,0:T(8,128)(2,1)}, u32[]{:S(2)}) copy-start(bf16[2,256,64]{2,1,0:T(8,128)(2,1)} %constant.25.clone.table) | copy-start | bytes 196612
  47.4 9.2 %all-to-all-start.2 = ((f32[8,24,128]{2,1,0:T(8,128)}), f32[8,24,128]{2,1,0:T(8,128)S(1)}, u32[]{:S(2)}, u32[]{:S(2)}) async-start(f32[8,24,128]{2,1,0:T(8,128)} %shard_map.103), calls=%async_computation.2 | async-start | bytes 196608 | tf_op jit(solution)/shard_map/all_to_all | solution.py:410
  52.5 9.1 %collective-permute-start.3 = (f32[3,40,768]{2,1,0:T(8,128)}, f32[3,40,768]{2,1,0:T(8,128)}, u32[]{:S(2)}, u32[]{:S(2)}) collective-permute-start(f32[3,40,768]{2,1,0:T(8,128)} %pad_maximum_fusion.1), channel_id=1, source_target_pairs={{1,0},{2,1},{3,2},{4,3},{5,4},{6,5},{7,6},{9,8},{10,9},{11,10},{12... | collective-permute-start | bytes 1105928 | tf_op jit(solution)/shard_map/ppermute | solution.py:351
  57.7 17.8 %all-to-all-start.3 = ((f32[32,24,128]{2,1,0:T(8,128)}), f32[32,24,128]{2,1,0:T(8,128)S(1)}, u32[]{:S(2)}, u32[]{:S(2)}) async-start(f32[32,24,128]{2,1,0:T(8,128)} %shard_map.104), calls=%async_computation.3 | async-start | bytes 786432 | tf_op jit(solution)/shard_map/all_to_all | solution.py:415
  61.6 13.9 %copy-start.1 = (bf16[2,256,256]{2,1,0:T(8,128)(2,1)S(1)}, bf16[2,256,256]{2,1,0:T(8,128)(2,1)}, u32[]{:S(2)}) copy-start(bf16[2,256,256]{2,1,0:T(8,128)(2,1)} %constant.26.clone.table) | copy-start | bytes 786436

commit v8 on v7

--- a/solution.py
+++ b/solution.py
@@ -195,7 +195,8 @@
     return 0.5 * values * (1.0 + lax.erf(values * math.sqrt(0.5)))
 
 
-ROW = 368
+BLOCK = 112
+ROW = 3 * BLOCK
 
 
 def taps_body(kernels, after, out_ref, scratch):
@@ -203,7 +204,8 @@
     for r in range(3):
         scratch[...] = jnp.zeros(scratch.shape, F32)
         for tap in range(27):
-            row, lane = CP * (tap % 3), CP * (tap // 3)
+            shift_x, shift_y, shift_z = tap // 9, tap // 3 % 3, tap % 3
+            row, lane = CP * shift_z, BLOCK * shift_y + channels * shift_x
             scratch[row : row + channels, lane : lane + channels] = kernels[r, tap]
         high, low = split(scratch[...].T[:ROW])
         out_ref[r, :ROW, :128] = high
@@ -232,7 +234,7 @@
             stack[128:, LANES * t : LANES * t + LANES] = low
 
     def emit(row):
-        sums = [[whole[CP * a : CP * a + CP, LANES * t : LANES * t + LANES] for t in range(tiles)] for a in range(3)]
+        sums = [[whole[36 * a : 36 * a + CP, LANES * t : LANES * t + LANES] for t in range(tiles)] for a in range(3)]
         out = []
         for t in range(tiles):
             low_part = sums[0][t]
@@ -253,15 +255,13 @@
             terms = lax.dot_general(
                 taps[...], here[:, lanes], (((1,), (0,)), ((), ())), preferred_element_type=F32
             )
-            for a in range(3):
-                rows = slice(CP * a, CP * a + CP)
-                piece = []
-                for b in range(3):
-                    first = CP * (3 * a + b)
-                    piece.append(terms[first : first + CP] + terms[ROW + first : ROW + first + CP])
-                whole[rows, lanes] = second_sum[rows, lanes] + piece[2]
-                second_sum[rows, lanes] = first_sum[rows, lanes] + piece[1]
-                first_sum[rows, lanes] = piece[0]
+            piece = []
+            for b in range(3):
+                high = terms[BLOCK * b : BLOCK * b + BLOCK]
+                piece.append(high + terms[ROW + BLOCK * b : ROW + BLOCK * b + BLOCK])
+            whole[:, lanes] = second_sum[:, lanes] + piece[2]
+            second_sum[:, lanes] = first_sum[:, lanes] + piece[1]
+            first_sum[:, lanes] = piece[0]
 
     def pair(j, carry):
         step(2 * j, stack_a, stack_b)
@@ -274,7 +274,7 @@
 
 
 def conv_scratch(width):
-    return [pltpu.VMEM((256, width), BF16)] * 2 + [pltpu.VMEM((3 * CP, width), F32)] * 3
+    return [pltpu.VMEM((256, width), BF16)] * 2 + [pltpu.VMEM((BLOCK, width), F32)] * 3
 
 
 def inside(place, first_x, sizes, width):

time: 77.5 us -> 77.6 us (level)
  waiting for transfers between devices: 9.51 us -> 10.8 us
  transfers between devices with their start and end apart: 8 -> 8, of which waited for: 4 -> 4; matrix products, arithmetic and copies ran while one was open for 2% -> 1% of each run, Pallas kernels for 25% -> 24%
where the time goes in v8:
time: 77.6 us; the launch traced here: 76.7 us
  starting transfers between devices  38.2 us (49%)
  Pallas kernels  21.8 us (28%)
  waiting for transfers between devices  10.8 us (14%)
  local copies, waits for them, and re-layouts  4.93 us (6%)
  other arithmetic  0.87 us (1%)
    pallas_call x7, Pallas kernels, call(): pl.pallas_call(body, out_shape=out_shape, in_specs=in_specs, out_specs=tu...  21.8 us
    all_to_all x2, starting transfers between devices, shards(): received = lax.all_to_all(sent, 'gx', 0, 0, tiled=True)  15.9 us
    all_to_all x2, starting transfers between devices, shards(): received = lax.all_to_all(sent, 'gy', 0, 0, tiled=True)  12.3 us
    ppermute x4, starting transfers between devices, shift(): return lax.ppermute(values, axis, pairs)  9.99 us
    all_to_all x2, waiting for transfers between devices, shards(): received = lax.all_to_all(sent, 'gx', 0, 0, tiled=True)  7.26 us
    unnamed x18, local copies, waits for them, and re-layouts  4.87 us
    all_to_all x2, waiting for transfers between devices, shards(): received = lax.all_to_all(sent, 'gy', 0, 0, tiled=True)  3.55 us
  transfers between devices with their start and end apart: 8, of which 4 were waited for; matrix products, arithmetic and copies ran while one was open for 1% of the time, Pallas kernels for 24%

profile of v8, /device:TPU:1, one launch (start us, length us, event | category | flops | bytes accessed | tf_op | source)
XLA Modules:
  0.0 76.7 jit_solution(16770666659263425717)
XLA Ops:
  0.0 2.3 %shard_map.100 = (f32[8,40,256]{2,1,0:T(8,128)}, f32[32,24,128]{2,1,0:T(8,128)}) custom-call(f32[36,4,512]{2,1,0:T(4,128)} %field_hbm.1, bf16[2,256,256]{2,1,0:T(8,128)(2,1)} %constant.21.clone.table_hbm), custom_call_target="tpu_custom_call" | custom-call | bytes 557056 | tf_op jit(solution)/shard_map/pallas_call | solution.py:93
  2.3 12.0 %all-to-all-start = ((f32[32,24,128]{2,1,0:T(8,128)}), f32[32,24,128]{2,1,0:T(8,128)S(1)}, u32[]{:S(2)}, u32[]{:S(2)}) async-start(f32[32,24,128]{2,1,0:T(8,128)} %get-tuple-element.16), calls=%async_computation | async-start | bytes 786432 | tf_op jit(solution)/shard_map/all_to_all | solution.py:387
  14.3 3.2 %collective-permute-start = (f32[8,40,256]{2,1,0:T(8,128)}, f32[8,40,256]{2,1,0:T(8,128)S(1)}, u32[]{:S(2)}, u32[]{:S(2)}) collective-permute-start(f32[8,40,256]{2,1,0:T(8,128)} %get-tuple-element.19.refs_2_), channel_id=1, source_target_pairs={{0,8},{8,16},{16,24},{24,32},{32,40},{40,48},{48,56},{56,64},{64,7... | collective-permute-start | bytes 983048 | tf_op jit(solution)/shard_map/ppermute | solution.py:351
  17.5 1.3 %collective-permute-start.1 = (f32[8,40,256]{2,1,0:T(8,128)}, f32[8,40,256]{2,1,0:T(8,128)S(1)}, u32[]{:S(2)}, u32[]{:S(2)}) collective-permute-start(f32[8,40,256]{2,1,0:T(8,128)} %get-tuple-element.19.refs_2_), channel_id=1, source_target_pairs={{8,0},{16,8},{24,16},{32,24},{40,32},{48,40},{56,48},{64,56},{72,6... | collective-permute-start | bytes 983048 | tf_op jit(solution)/shard_map/ppermute | solution.py:351
  18.9 1.4 %copy-done = f32[3,27,36,36]{3,2,1,0:T(8,128)S(1)} copy-done((f32[3,27,36,36]{3,2,1,0:T(8,128)S(1)}, f32[3,27,36,36]{3,2,1,0:T(8,128)}, u32[]{:S(2)}) %copy-start) | copy-done | bytes 419928
  20.3 1.2 %shard_map.101.refs_6_ = bf16[3,672,256]{2,1,0:T(8,128)(2,1)S(1)} custom-call(f32[3,27,36,36]{3,2,1,0:T(8,128)S(1)} %copy-done, s32[2]{0:T(128)S(1)} %pad_add_fusion.after.place.refs_5_), custom_call_target="tpu_custom_call" | custom-call | bytes 419912 | tf_op jit(solution)/shard_map/pallas_call | solution.py:93
  21.6 6.1 %all-to-all-done.received = f32[32,24,128]{2,1,0:T(8,128)S(1)} async-done(((f32[32,24,128]{2,1,0:T(8,128)}), f32[32,24,128]{2,1,0:T(8,128)S(1)}, u32[]{:S(2)}, u32[]{:S(2)}) %all-to-all-start) | async-done | bytes 393248 | tf_op jit(solution)/shard_map/all_to_all | solution.py:387
  27.7 0.9 %shard_map.102 = f32[8,24,128]{2,1,0:T(8,128)} custom-call(f32[32,24,128]{2,1,0:T(8,128)S(1)} %all-to-all-done.received, bf16[2,64,256]{2,1,0:T(8,128)(2,1)S(1)} %copy-done.3), custom_call_target="tpu_custom_call" | custom-call | bytes 458752 | tf_op jit(solution)/shard_map/pallas_call | solution.py:93
  28.6 8.2 %all-to-all-start.1 = ((f32[8,24,128]{2,1,0:T(8,128)}), f32[8,24,128]{2,1,0:T(8,128)S(1)}, u32[]{:S(2)}, u32[]{:S(2)}) async-start(f32[8,24,128]{2,1,0:T(8,128)} %shard_map.102), calls=%async_computation.1 | async-start | bytes 196608 | tf_op jit(solution)/shard_map/all_to_all | solution.py:393
  36.8 3.5 %collective-permute-start.2 = (f32[3,40,768]{2,1,0:T(8,128)S(1)}, f32[3,40,768]{2,1,0:T(8,128)S(1)}, u32[]{:S(2)}, u32[]{:S(2)}) collective-permute-start(f32[3,40,768]{2,1,0:T(8,128)S(1)} %pad_maximum_fusion), channel_id=1, source_target_pairs={{0,1},{1,2},{2,3},{3,4},{4,5},{5,6},{6,7},{8,9},{9,10},{10,11},{11... | collective-permute-start | bytes 1105928 | tf_op jit(solution)/shard_map/ppermute | solution.py:351
  40.4 1.4 %all-to-all-done.1.received = f32[8,24,128]{2,1,0:T(8,128)S(1)} async-done(((f32[8,24,128]{2,1,0:T(8,128)}), f32[8,24,128]{2,1,0:T(8,128)S(1)}, u32[]{:S(2)}, u32[]{:S(2)}) %all-to-all-start.1) | async-done | bytes 98336 | tf_op jit(solution)/shard_map/all_to_all | solution.py:393
  41.7 1.3 %copy-done.4 = f32[2,36,36,1,128]{4,3,2,1,0:T(1,128)S(1)} copy-done((f32[2,36,36,1,128]{4,3,2,1,0:T(1,128)S(1)}, f32[2,36,36,1,128]{4,3,2,1,0:T(1,128)}, u32[]{:S(2)}) %copy-start.4) | copy-done | bytes 1327128
  43.1 1.0 %copy-done.6 = bf16[2,256,512]{2,1,0:T(8,128)(2,1)S(1)} copy-done((bf16[2,256,512]{2,1,0:T(8,128)(2,1)S(1)}, bf16[2,256,512]{2,1,0:T(8,128)(2,1)}, u32[]{:S(2)}) %copy-start.6) | copy-done | bytes 524312
  44.1 1.0 %copy-done.7 = bf16[2,512,256]{2,1,0:T(8,128)(2,1)S(1)} copy-done((bf16[2,512,256]{2,1,0:T(8,128)(2,1)S(1)}, bf16[2,512,256]{2,1,0:T(8,128)(2,1)}, u32[]{:S(2)}) %copy-start.7) | copy-done | bytes 524312
  45.1 2.5 %shard_map.103 = f32[8,24,128]{2,1,0:T(8,128)} custom-call(f32[8,24,128]{2,1,0:T(8,128)S(1)} %all-to-all-done.1.received, f32[2,1296,128]{2,1,0:T(8,128)S(1)} %bitcast.4, s32[1,128]{1,0:T(1,128)S(1)} %bitcast.5, s32[2]{0:T(128)S(1)} %pad_add_fusion.after.place.refs_5_, bf16[2,256,512]{2,1,0:T(8,128)(2,1)S(1)} %copy-done.6, bf16[2,512,256]{2,1,0:T(8,128)(2,1)S(1)} %copy-done.7), custom_call_target="tpu_custom_call" | custom-call | flops 8589934592 | bytes 2474504 | tf_op jit(solution)/shard_map/pallas_call | solution.py:93
  47.6 4.1 %all-to-all-start.2 = ((f32[8,24,128]{2,1,0:T(8,128)}), f32[8,24,128]{2,1,0:T(8,128)S(1)}, u32[]{:S(2)}, u32[]{:S(2)}) async-start(f32[8,24,128]{2,1,0:T(8,128)} %shard_map.103), calls=%async_computation.2 | async-start | bytes 196608 | tf_op jit(solution)/shard_map/all_to_all | solution.py:410
  51.7 0.8 pad_maximum_fusion.1
  52.5 2.0 %collective-permute-start.3 = (f32[3,40,768]{2,1,0:T(8,128)}, f32[3,40,768]{2,1,0:T(8,128)}, u32[]{:S(2)}, u32[]{:S(2)}) collective-permute-start(f32[3,40,768]{2,1,0:T(8,128)} %pad_maximum_fusion.1), channel_id=1, source_target_pairs={{1,0},{2,1},{3,2},{4,3},{5,4},{6,5},{7,6},{9,8},{10,9},{11,10},{12... | collective-permute-start | bytes 1105928 | tf_op jit(solution)/shard_map/ppermute | solution.py:351
  54.5 2.2 %all-to-all-done.2.received = f32[8,24,128]{2,1,0:T(8,128)S(1)} async-done(((f32[8,24,128]{2,1,0:T(8,128)}), f32[8,24,128]{2,1,0:T(8,128)S(1)}, u32[]{:S(2)}, u32[]{:S(2)}) %all-to-all-start.2) | async-done | bytes 98336 | tf_op jit(solution)/shard_map/all_to_all | solution.py:410
  56.7 1.1 %shard_map.104 = f32[32,24,128]{2,1,0:T(8,128)} custom-call(f32[8,24,128]{2,1,0:T(8,128)S(1)} %all-to-all-done.2.received, bf16[2,256,64]{2,1,0:T(8,128)(2,1)S(1)} %copy-done.8), custom_call_target="tpu_custom_call" | custom-call | flops 8589934592 | bytes 163840 | tf_op jit(solution)/shard_map/pallas_call | solution.py:93
  57.8 3.9 %all-to-all-start.3 = ((f32[32,24,128]{2,1,0:T(8,128)}), f32[32,24,128]{2,1,0:T(8,128)S(1)}, u32[]{:S(2)}, u32[]{:S(2)}) async-start(f32[32,24,128]{2,1,0:T(8,128)} %shard_map.104), calls=%async_computation.3 | async-start | bytes 786432 | tf_op jit(solution)/shard_map/all_to_all | solution.py:415
  61.7 12.7 %shard_map.105.third = f32[8,40,256]{2,1,0:T(8,128)S(1)} custom-call(f32[3,40,768]{2,1,0:T(8,128)S(1)} %collective-permute-done.2.refs_0_, f32[8,40,256]{2,1,0:T(8,128)S(1)} %collective-permute-done.refs_1_, f32[8,40,256]{2,1,0:T(8,128)S(1)} %copy-done.2, f32[8,40,256]{2,1,0:T(8,128)S(1)} %collective-permute-done.1.refs_3_, ...), custom_call_target="tpu_custom_call" | custom-call | flops 12884901888 | bytes 2752520 | tf_op jit(solution)/shard_map/pallas_call | solution.py:93
  74.4 1.2 %all-to-all-done.3.received = f32[32,24,128]{2,1,0:T(8,128)S(1)} async-done(((f32[32,24,128]{2,1,0:T(8,128)}), f32[32,24,128]{2,1,0:T(8,128)S(1)}, u32[]{:S(2)}, u32[]{:S(2)}) %all-to-all-start.3) | async-done | bytes 393248 | tf_op jit(solution)/shard_map/all_to_all | solution.py:415
  75.5 1.2 %shard_map.106 = f32[36,4,512]{2,1,0:T(4,128)} custom-call(f32[32,24,128]{2,1,0:T(8,128)S(1)} %all-to-all-done.3.received, f32[8,40,256]{2,1,0:T(8,128)S(1)} %shard_map.105.third, bf16[2,256,256]{2,1,0:T(8,128)(2,1)S(1)} %copy-done.1), custom_call_target="tpu_custom_call" | custom-call | bytes 983040 | tf_op jit(solution)/shard_map/pallas_call | solution.py:93
  (25 shorter events, 0.2 us)
Async XLA Ops:
  2.3 19.2 %copy-start.2 = (f32[8,40,256]{2,1,0:T(8,128)S(1)}, f32[8,40,256]{2,1,0:T(8,128)}, u32[]{:S(2)}) copy-start(f32[8,40,256]{2,1,0:T(8,128)} %get-tuple-element.19.refs_2_) | copy-start | bytes 983044
  2.3 25.4 %copy-start.3 = (bf16[2,64,256]{2,1,0:T(8,128)(2,1)S(1)}, bf16[2,64,256]{2,1,0:T(8,128)(2,1)}, u32[]{:S(2)}) copy-start(bf16[2,64,256]{2,1,0:T(8,128)(2,1)} %constant.22.clone.table) | copy-start | bytes 196612
  2.3 25.4 %all-to-all-start = ((f32[32,24,128]{2,1,0:T(8,128)}), f32[32,24,128]{2,1,0:T(8,128)S(1)}, u32[]{:S(2)}, u32[]{:S(2)}) async-start(f32[32,24,128]{2,1,0:T(8,128)} %get-tuple-element.16), calls=%async_computation | async-start | bytes 786432 | tf_op jit(solution)/shard_map/all_to_all | solution.py:387
  14.3 22.4 %collective-permute-start = (f32[8,40,256]{2,1,0:T(8,128)}, f32[8,40,256]{2,1,0:T(8,128)S(1)}, u32[]{:S(2)}, u32[]{:S(2)}) collective-permute-start(f32[8,40,256]{2,1,0:T(8,128)} %get-tuple-element.19.refs_2_), channel_id=1, source_target_pairs={{0,8},{8,16},{16,24},{24,32},{32,40},{40,48},{48,56},{56,64},{64,7... | collective-permute-start | bytes 983048 | tf_op jit(solution)/shard_map/ppermute | solution.py:351
  17.5 19.2 %collective-permute-start.1 = (f32[8,40,256]{2,1,0:T(8,128)}, f32[8,40,256]{2,1,0:T(8,128)S(1)}, u32[]{:S(2)}, u32[]{:S(2)}) collective-permute-start(f32[8,40,256]{2,1,0:T(8,128)} %get-tuple-element.19.refs_2_), channel_id=1, source_target_pairs={{8,0},{16,8},{24,16},{32,24},{40,32},{48,40},{56,48},{64,56},{72,6... | collective-permute-start | bytes 983048 | tf_op jit(solution)/shard_map/ppermute | solution.py:351
  18.9 1.4 %copy-start = (f32[3,27,36,36]{3,2,1,0:T(8,128)S(1)}, f32[3,27,36,36]{3,2,1,0:T(8,128)}, u32[]{:S(2)}) copy-start(f32[3,27,36,36]{3,2,1,0:T(8,128)} %kernels.1) | copy-start | bytes 1259716
  21.6 20.2 %copy-start.5 = (s32[128]{0:T(128)S(1)}, s32[128]{0:T(128)}, u32[]{:S(2)}) copy-start(s32[128]{0:T(128)} %param.12) | copy-start | bytes 1540
  28.6 13.2 %all-to-all-start.1 = ((f32[8,24,128]{2,1,0:T(8,128)}), f32[8,24,128]{2,1,0:T(8,128)S(1)}, u32[]{:S(2)}, u32[]{:S(2)}) async-start(f32[8,24,128]{2,1,0:T(8,128)} %shard_map.102), calls=%async_computation.1 | async-start | bytes 196608 | tf_op jit(solution)/shard_map/all_to_all | solution.py:393
  36.8 24.8 %collective-permute-start.2 = (f32[3,40,768]{2,1,0:T(8,128)S(1)}, f32[3,40,768]{2,1,0:T(8,128)S(1)}, u32[]{:S(2)}, u32[]{:S(2)}) collective-permute-start(f32[3,40,768]{2,1,0:T(8,128)S(1)} %pad_maximum_fusion), channel_id=1, source_target_pairs={{0,1},{1,2},{2,3},{3,4},{4,5},{5,6},{6,7},{8,9},{9,10},{10,11},{11... | collective-permute-start | bytes 1105928 | tf_op jit(solution)/shard_map/ppermute | solution.py:351
  41.7 1.3 %copy-start.4 = (f32[2,36,36,1,128]{4,3,2,1,0:T(1,128)S(1)}, f32[2,36,36,1,128]{4,3,2,1,0:T(1,128)}, u32[]{:S(2)}) copy-start(f32[2,36,36,1,128]{4,3,2,1,0:T(1,128)} %param.11) | copy-start | bytes 3981316
  43.1 1.0 %copy-start.6 = (bf16[2,256,512]{2,1,0:T(8,128)(2,1)S(1)}, bf16[2,256,512]{2,1,0:T(8,128)(2,1)}, u32[]{:S(2)}) copy-start(bf16[2,256,512]{2,1,0:T(8,128)(2,1)} %constant.23.clone.y_in) | copy-start | bytes 1572868
  44.1 1.0 %copy-start.7 = (bf16[2,512,256]{2,1,0:T(8,128)(2,1)S(1)}, bf16[2,512,256]{2,1,0:T(8,128)(2,1)}, u32[]{:S(2)}) copy-start(bf16[2,512,256]{2,1,0:T(8,128)(2,1)} %constant.24.clone.y_out) | copy-start | bytes 1572868
  45.1 11.6 %copy-start.8 = (bf16[2,256,64]{2,1,0:T(8,128)(2,1)S(1)}, bf16[2,256,64]{2,1,0:T(8,128)(2,1)}, u32[]{:S(2)}) copy-start(bf16[2,256,64]{2,1,0:T(8,128)(2,1)} %constant.25.clone.table) | copy-start | bytes 196612
  47.6 9.1 %all-to-all-start.2 = ((f32[8,24,128]{2,1,0:T(8,128)}), f32[8,24,128]{2,1,0:T(8,128)S(1)}, u32[]{:S(2)}, u32[]{:S(2)}) async-start(f32[8,24,128]{2,1,0:T(8,128)} %shard_map.103), calls=%async_computation.2 | async-start | bytes 196608 | tf_op jit(solution)/shard_map/all_to_all | solution.py:410
  52.5 9.2 %collective-permute-start.3 = (f32[3,40,768]{2,1,0:T(8,128)}, f32[3,40,768]{2,1,0:T(8,128)}, u32[]{:S(2)}, u32[]{:S(2)}) collective-permute-start(f32[3,40,768]{2,1,0:T(8,128)} %pad_maximum_fusion.1), channel_id=1, source_target_pairs={{1,0},{2,1},{3,2},{4,3},{5,4},{6,5},{7,6},{9,8},{10,9},{11,10},{12... | collective-permute-start | bytes 1105928 | tf_op jit(solution)/shard_map/ppermute | solution.py:351
  57.8 17.8 %all-to-all-start.3 = ((f32[32,24,128]{2,1,0:T(8,128)}), f32[32,24,128]{2,1,0:T(8,128)S(1)}, u32[]{:S(2)}, u32[]{:S(2)}) async-start(f32[32,24,128]{2,1,0:T(8,128)} %shard_map.104), calls=%async_computation.3 | async-start | bytes 786432 | tf_op jit(solution)/shard_map/all_to_all | solution.py:415
  61.7 13.9 %copy-start.1 = (bf16[2,256,256]{2,1,0:T(8,128)(2,1)S(1)}, bf16[2,256,256]{2,1,0:T(8,128)(2,1)}, u32[]{:S(2)}) copy-start(bf16[2,256,256]{2,1,0:T(8,128)(2,1)} %constant.26.clone.table) | copy-start | bytes 786436

commit v9 on v8

--- a/solution.py
+++ b/solution.py
@@ -150,13 +150,23 @@
         out_ref[:, 8 * tile : 8 * tile + 8, :] = block.reshape(out_ref.shape[0], 8, LANES)
 
 
-def mix_body(received, weights, kept, place, y_in, y_out, out_ref, stacked, s_re, s_im):
+def mix_body(received_hbm, weights_hbm, kept, place, y_in_hbm, y_out_hbm, out_ref, stacked, s_re, s_im, *refs):
+    received, weights, y_in, y_out, sems = refs
+    arrived = copies(
+        [(received_hbm, received)]
+        + [(y_in_hbm.at[i], y_in.at[i]) for i in range(2)]
+        + [(weights_hbm.at[i], weights.at[i]) for i in range(2)]
+        + [(y_out_hbm.at[i], y_out.at[i]) for i in range(2)],
+        sems,
+    )
+    wait(arrived[:1])
     cells_y = received.shape[0]
     rows = load_payload(received)
     block = rows.shape[0]
     for y in range(cells_y):
         stacked[y * block : (y + 1) * block, :CP] = rows[:, CP * y : CP * y + CP]
         stacked[y * block : (y + 1) * block, CP:] = jnp.zeros((block, LANES - CP), F32)
+    wait(arrived[1:3])
     modes = product(y_in, stacked[...], ((1,), (0,)))
     count = modes.shape[0] // 2
     s_re[...] = modes[:count].T
@@ -171,6 +181,7 @@
         middle = jnp.where(row < 4, first, second)
         return jnp.concatenate([first] * 4 + [middle] + [second] * 4, axis=0)
 
+    wait(arrived[3:5])
     total_re = jnp.zeros((pair, count), F32)
     total_im = jnp.zeros((pair, count), F32)
     for c in range(0, channels, 2):
@@ -186,6 +197,7 @@
         return jnp.concatenate([jnp.where(keep, total, 0.0), jnp.zeros((CP - channels, count), F32)], axis=0)
 
     mixed = jnp.concatenate([fold(total_re), fold(total_im)], axis=1)
+    wait(arrived[5:])
     back = product(y_out, mixed, ((1,), (1,)))
     lanes = jnp.concatenate([back[y * block : (y + 1) * block] for y in range(cells_y)], axis=1)
     store_payload(out_ref, lanes)
@@ -402,8 +414,10 @@
         jax.ShapeDtypeStruct((size_y, 24, LANES), F32),
         received, weights, kept_z.reshape(1, -1), place, y_in, y_out,
         scratch=[pltpu.VMEM((cells_y * size_y * kx_local * 2, LANES), F32)]
-        + [pltpu.VMEM((LANES, kx_local * KY), F32)] * 2,
-        smem=(3,), flops=MIX << 20,
+        + [pltpu.VMEM((LANES, kx_local * KY), F32)] * 2
+        + [pltpu.VMEM(a.shape, a.dtype) for a in (received, weights, y_in, y_out)]
+        + [pltpu.SemaphoreType.DMA((7,))],
+        smem=(3,), hbm=(0, 1, 4, 5), vmem=FULL, flops=MIX << 20,
     )
     left, right, _ = lax.optimization_barrier((left, right, sent))
     after = shift(edge(slice(0, 3)), "gy", -1)

time: 77.6 us -> 76 us (0.979)
  local copies, waits for them, and re-layouts: 4.93 us -> 2.16 us
  Pallas kernels: 21.8 us -> 22.9 us
    unnamed x18 -> x16, local copies, waits for them, and re-layouts: 4.87 us -> 2.11 us
    pallas_call x7, Pallas kernels: 21.8 us -> 22.9 us  [call(): pl.pallas_call(body, out_shape=out_shape, in_specs=in_specs, out_specs=tu...]
  transfers between devices with their start and end apart: 8 -> 8, of which waited for: 4 -> 5; matrix products, arithmetic and copies ran while one was open for 1% -> 1% of each run, Pallas kernels for 24% -> 26%
where the time goes in v9:
time: 76 us; the launch traced here: 75.2 us
  starting transfers between devices  38.3 us (50%)
  Pallas kernels  22.9 us (30%)
  waiting for transfers between devices  10.9 us (14%)
  local copies, waits for them, and re-layouts  2.16 us (3%)
  other arithmetic  0.87 us (1%)
    pallas_call x7, Pallas kernels, call(): pl.pallas_call(body, out_shape=out_shape, in_specs=in_specs, out_specs=tu...  22.9 us
    all_to_all x2, starting transfers between devices, shards(): received = lax.all_to_all(sent, 'gx', 0, 0, tiled=True)  15.9 us
    all_to_all x2, starting transfers between devices, shards(): received = lax.all_to_all(sent, 'gy', 0, 0, tiled=True)  12.3 us
    ppermute x4, starting transfers between devices, shift(): return lax.ppermute(values, axis, pairs)  10.1 us
    all_to_all x2, waiting for transfers between devices, shards(): received = lax.all_to_all(sent, 'gx', 0, 0, tiled=True)  7.34 us
    all_to_all x2, waiting for transfers between devices, shards(): received = lax.all_to_all(sent, 'gy', 0, 0, tiled=True)  3.4 us
    unnamed x16, local copies, waits for them, and re-layouts  2.11 us
  transfers between devices with their start and end apart: 8, of which 5 were waited for; matrix products, arithmetic and copies ran while one was open for 1% of the time, Pallas kernels for 26%

profile of v9, /device:TPU:1, one launch (start us, length us, event | category | flops | bytes accessed | tf_op | source)
XLA Modules:
  0.0 75.2 jit_solution(3654900646660368234)
XLA Ops:
  0.0 2.3 %shard_map.100 = (f32[8,40,256]{2,1,0:T(8,128)}, f32[32,24,128]{2,1,0:T(8,128)}) custom-call(f32[36,4,512]{2,1,0:T(4,128)} %field_hbm.1, bf16[2,256,256]{2,1,0:T(8,128)(2,1)} %constant.21.clone.table_hbm), custom_call_target="tpu_custom_call" | custom-call | bytes 557056 | tf_op jit(solution)/shard_map/pallas_call | solution.py:93
  2.3 12.0 %all-to-all-start = ((f32[32,24,128]{2,1,0:T(8,128)}), f32[32,24,128]{2,1,0:T(8,128)S(1)}, u32[]{:S(2)}, u32[]{:S(2)}) async-start(f32[32,24,128]{2,1,0:T(8,128)} %get-tuple-element.16), calls=%async_computation | async-start | bytes 786432 | tf_op jit(solution)/shard_map/all_to_all | solution.py:399
  14.3 3.2 %collective-permute-start = (f32[8,40,256]{2,1,0:T(8,128)}, f32[8,40,256]{2,1,0:T(8,128)S(1)}, u32[]{:S(2)}, u32[]{:S(2)}) collective-permute-start(f32[8,40,256]{2,1,0:T(8,128)} %get-tuple-element.19.refs_2_), channel_id=1, source_target_pairs={{0,8},{8,16},{16,24},{24,32},{32,40},{40,48},{48,56},{56,64},{64,7... | collective-permute-start | bytes 983048 | tf_op jit(solution)/shard_map/ppermute | solution.py:363
  17.5 1.3 %collective-permute-start.1 = (f32[8,40,256]{2,1,0:T(8,128)}, f32[8,40,256]{2,1,0:T(8,128)S(1)}, u32[]{:S(2)}, u32[]{:S(2)}) collective-permute-start(f32[8,40,256]{2,1,0:T(8,128)} %get-tuple-element.19.refs_2_), channel_id=1, source_target_pairs={{8,0},{16,8},{24,16},{32,24},{40,32},{48,40},{56,48},{64,56},{72,6... | collective-permute-start | bytes 983048 | tf_op jit(solution)/shard_map/ppermute | solution.py:363
  18.8 0.1 pad_add_fusion.after.place.refs_5_
  18.9 1.4 %copy-done = f32[3,27,36,36]{3,2,1,0:T(8,128)S(1)} copy-done((f32[3,27,36,36]{3,2,1,0:T(8,128)S(1)}, f32[3,27,36,36]{3,2,1,0:T(8,128)}, u32[]{:S(2)}) %copy-start) | copy-done | bytes 419928
  20.3 1.2 %shard_map.101.refs_6_ = bf16[3,672,256]{2,1,0:T(8,128)(2,1)S(1)} custom-call(f32[3,27,36,36]{3,2,1,0:T(8,128)S(1)} %copy-done, s32[2]{0:T(128)S(1)} %pad_add_fusion.after.place.refs_5_), custom_call_target="tpu_custom_call" | custom-call | bytes 419912 | tf_op jit(solution)/shard_map/pallas_call | solution.py:93
  21.6 6.1 %all-to-all-done.received = f32[32,24,128]{2,1,0:T(8,128)S(1)} async-done(((f32[32,24,128]{2,1,0:T(8,128)}), f32[32,24,128]{2,1,0:T(8,128)S(1)}, u32[]{:S(2)}, u32[]{:S(2)}) %all-to-all-start) | async-done | bytes 393248 | tf_op jit(solution)/shard_map/all_to_all | solution.py:399
  27.7 0.9 %shard_map.102 = f32[8,24,128]{2,1,0:T(8,128)} custom-call(f32[32,24,128]{2,1,0:T(8,128)S(1)} %all-to-all-done.received, bf16[2,64,256]{2,1,0:T(8,128)(2,1)S(1)} %copy-done.3), custom_call_target="tpu_custom_call" | custom-call | bytes 458752 | tf_op jit(solution)/shard_map/pallas_call | solution.py:93
  28.6 8.2 %all-to-all-start.1 = ((f32[8,24,128]{2,1,0:T(8,128)}), f32[8,24,128]{2,1,0:T(8,128)S(1)}, u32[]{:S(2)}, u32[]{:S(2)}) async-start(f32[8,24,128]{2,1,0:T(8,128)} %shard_map.102), calls=%async_computation.1 | async-start | bytes 196608 | tf_op jit(solution)/shard_map/all_to_all | solution.py:405
  36.8 3.5 %collective-permute-start.2 = (f32[3,40,768]{2,1,0:T(8,128)S(1)}, f32[3,40,768]{2,1,0:T(8,128)S(1)}, u32[]{:S(2)}, u32[]{:S(2)}) collective-permute-start(f32[3,40,768]{2,1,0:T(8,128)S(1)} %pad_maximum_fusion), channel_id=1, source_target_pairs={{0,1},{1,2},{2,3},{3,4},{4,5},{5,6},{6,7},{8,9},{9,10},{10,11},{11... | collective-permute-start | bytes 1105928 | tf_op jit(solution)/shard_map/ppermute | solution.py:363
  40.4 1.4 %all-to-all-done.1.received_hbm = f32[8,24,128]{2,1,0:T(8,128)S(1)} async-done(((f32[8,24,128]{2,1,0:T(8,128)}), f32[8,24,128]{2,1,0:T(8,128)S(1)}, u32[]{:S(2)}, u32[]{:S(2)}) %all-to-all-start.1) | async-done | bytes 98336 | tf_op jit(solution)/shard_map/all_to_all | solution.py:405
  41.7 0.6 copy-done.7
  42.4 3.8 %shard_map.103 = f32[8,24,128]{2,1,0:T(8,128)} custom-call(f32[8,24,128]{2,1,0:T(8,128)} %copy-done.7, f32[2,1296,128]{2,1,0:T(8,128)} %bitcast.4, s32[1,128]{1,0:T(1,128)} %bitcast.5, s32[2]{0:T(128)} %copy-done.4, bf16[2,256,512]{2,1,0:T(8,128)(2,1)} %constant.23.clone.y_in_hbm, bf16[2,512,256]{2,1,0:T(8,128)(2,1)} %constant.24.clone.y_out_hbm), custom_call_target="tpu_custom_call" | custom-call | flops 8589934592 | bytes 2474504 | tf_op jit(solution)/shard_map/pallas_call | solution.py:93
  46.1 4.1 %all-to-all-start.2 = ((f32[8,24,128]{2,1,0:T(8,128)}), f32[8,24,128]{2,1,0:T(8,128)S(1)}, u32[]{:S(2)}, u32[]{:S(2)}) async-start(f32[8,24,128]{2,1,0:T(8,128)} %shard_map.103), calls=%async_computation.2 | async-start | bytes 196608 | tf_op jit(solution)/shard_map/all_to_all | solution.py:424
  50.3 0.8 %pad_maximum_fusion.1 = f32[3,40,768]{2,1,0:T(8,128)} fusion(f32[3,40,256]{2,1,0:T(8,128)S(1)} %slice.23, f32[3,40,256]{2,1,0:T(8,128)S(1)} %get-tuple-element.27, f32[3,40,256]{2,1,0:T(8,128)S(1)} %slice.21), kind=kLoop, calls=%fused_computation.1 | loop fusion | flops 184320 | bytes 737280 | tf_op jit(solution)/shard_map/concatenate | solution.py:408
  51.1 2.1 %collective-permute-start.3 = (f32[3,40,768]{2,1,0:T(8,128)}, f32[3,40,768]{2,1,0:T(8,128)}, u32[]{:S(2)}, u32[]{:S(2)}) collective-permute-start(f32[3,40,768]{2,1,0:T(8,128)} %pad_maximum_fusion.1), channel_id=1, source_target_pairs={{1,0},{2,1},{3,2},{4,3},{5,4},{6,5},{7,6},{9,8},{10,9},{11,10},{12... | collective-permute-start | bytes 1105928 | tf_op jit(solution)/shard_map/ppermute | solution.py:363
  53.2 2.0 %all-to-all-done.2.received = f32[8,24,128]{2,1,0:T(8,128)S(1)} async-done(((f32[8,24,128]{2,1,0:T(8,128)}), f32[8,24,128]{2,1,0:T(8,128)S(1)}, u32[]{:S(2)}, u32[]{:S(2)}) %all-to-all-start.2) | async-done | bytes 98336 | tf_op jit(solution)/shard_map/all_to_all | solution.py:424
  55.3 1.0 %shard_map.104 = f32[32,24,128]{2,1,0:T(8,128)} custom-call(f32[8,24,128]{2,1,0:T(8,128)S(1)} %all-to-all-done.2.received, bf16[2,256,64]{2,1,0:T(8,128)(2,1)S(1)} %copy-done.6), custom_call_target="tpu_custom_call" | custom-call | flops 8589934592 | bytes 163840 | tf_op jit(solution)/shard_map/pallas_call | solution.py:93
  56.3 3.9 %all-to-all-start.3 = ((f32[32,24,128]{2,1,0:T(8,128)}), f32[32,24,128]{2,1,0:T(8,128)S(1)}, u32[]{:S(2)}, u32[]{:S(2)}) async-start(f32[32,24,128]{2,1,0:T(8,128)} %shard_map.104), calls=%async_computation.3 | async-start | bytes 786432 | tf_op jit(solution)/shard_map/all_to_all | solution.py:429
  60.2 0.1 collective-permute-done.3.refs_4_
  60.3 12.5 %shard_map.105.third = f32[8,40,256]{2,1,0:T(8,128)S(1)} custom-call(f32[3,40,768]{2,1,0:T(8,128)S(1)} %collective-permute-done.2.refs_0_, f32[8,40,256]{2,1,0:T(8,128)S(1)} %collective-permute-done.refs_1_, f32[8,40,256]{2,1,0:T(8,128)S(1)} %copy-done.2, f32[8,40,256]{2,1,0:T(8,128)S(1)} %collective-permute-done.1.refs_3_, ...), custom_call_target="tpu_custom_call" | custom-call | flops 12884901888 | bytes 2752520 | tf_op jit(solution)/shard_map/pallas_call | solution.py:93
  72.8 1.2 %all-to-all-done.3.received = f32[32,24,128]{2,1,0:T(8,128)S(1)} async-done(((f32[32,24,128]{2,1,0:T(8,128)}), f32[32,24,128]{2,1,0:T(8,128)S(1)}, u32[]{:S(2)}, u32[]{:S(2)}) %all-to-all-start.3) | async-done | bytes 393248 | tf_op jit(solution)/shard_map/all_to_all | solution.py:429
  74.1 1.2 %shard_map.106 = f32[36,4,512]{2,1,0:T(4,128)} custom-call(f32[32,24,128]{2,1,0:T(8,128)S(1)} %all-to-all-done.3.received, f32[8,40,256]{2,1,0:T(8,128)S(1)} %shard_map.105.third, bf16[2,256,256]{2,1,0:T(8,128)(2,1)S(1)} %copy-done.1), custom_call_target="tpu_custom_call" | custom-call | bytes 983040 | tf_op jit(solution)/shard_map/pallas_call | solution.py:93
  (23 shorter events, 0.1 us)
Async XLA Ops:
  2.3 19.2 %copy-start.2 = (f32[8,40,256]{2,1,0:T(8,128)S(1)}, f32[8,40,256]{2,1,0:T(8,128)}, u32[]{:S(2)}) copy-start(f32[8,40,256]{2,1,0:T(8,128)} %get-tuple-element.19.refs_2_) | copy-start | bytes 983044
  2.3 25.4 %copy-start.3 = (bf16[2,64,256]{2,1,0:T(8,128)(2,1)S(1)}, bf16[2,64,256]{2,1,0:T(8,128)(2,1)}, u32[]{:S(2)}) copy-start(bf16[2,64,256]{2,1,0:T(8,128)(2,1)} %constant.22.clone.table) | copy-start | bytes 196612
  2.3 25.4 %all-to-all-start = ((f32[32,24,128]{2,1,0:T(8,128)}), f32[32,24,128]{2,1,0:T(8,128)S(1)}, u32[]{:S(2)}, u32[]{:S(2)}) async-start(f32[32,24,128]{2,1,0:T(8,128)} %get-tuple-element.16), calls=%async_computation | async-start | bytes 786432 | tf_op jit(solution)/shard_map/all_to_all | solution.py:399
  14.3 22.4 %collective-permute-start = (f32[8,40,256]{2,1,0:T(8,128)}, f32[8,40,256]{2,1,0:T(8,128)S(1)}, u32[]{:S(2)}, u32[]{:S(2)}) collective-permute-start(f32[8,40,256]{2,1,0:T(8,128)} %get-tuple-element.19.refs_2_), channel_id=1, source_target_pairs={{0,8},{8,16},{16,24},{24,32},{32,40},{40,48},{48,56},{56,64},{64,7... | collective-permute-start | bytes 983048 | tf_op jit(solution)/shard_map/ppermute | solution.py:363
  17.5 19.2 %collective-permute-start.1 = (f32[8,40,256]{2,1,0:T(8,128)}, f32[8,40,256]{2,1,0:T(8,128)S(1)}, u32[]{:S(2)}, u32[]{:S(2)}) collective-permute-start(f32[8,40,256]{2,1,0:T(8,128)} %get-tuple-element.19.refs_2_), channel_id=1, source_target_pairs={{8,0},{16,8},{24,16},{32,24},{40,32},{48,40},{56,48},{64,56},{72,6... | collective-permute-start | bytes 983048 | tf_op jit(solution)/shard_map/ppermute | solution.py:363
  18.9 1.4 %copy-start = (f32[3,27,36,36]{3,2,1,0:T(8,128)S(1)}, f32[3,27,36,36]{3,2,1,0:T(8,128)}, u32[]{:S(2)}) copy-start(f32[3,27,36,36]{3,2,1,0:T(8,128)} %kernels.1) | copy-start | bytes 1259716
  20.3 8.2 %copy-start.4 = (s32[2]{0:T(128)}, s32[2]{0:T(128)S(1)}, u32[]{:S(2)}) copy-start(s32[2]{0:T(128)S(1)} %pad_add_fusion.after.place.refs_5_) | copy-start | bytes 28
  28.6 13.2 %all-to-all-start.1 = ((f32[8,24,128]{2,1,0:T(8,128)}), f32[8,24,128]{2,1,0:T(8,128)S(1)}, u32[]{:S(2)}, u32[]{:S(2)}) async-start(f32[8,24,128]{2,1,0:T(8,128)} %shard_map.102), calls=%async_computation.1 | async-start | bytes 196608 | tf_op jit(solution)/shard_map/all_to_all | solution.py:405
  36.8 23.4 %collective-permute-start.2 = (f32[3,40,768]{2,1,0:T(8,128)S(1)}, f32[3,40,768]{2,1,0:T(8,128)S(1)}, u32[]{:S(2)}, u32[]{:S(2)}) collective-permute-start(f32[3,40,768]{2,1,0:T(8,128)S(1)} %pad_maximum_fusion), channel_id=1, source_target_pairs={{0,1},{1,2},{2,3},{3,4},{4,5},{5,6},{6,7},{8,9},{9,10},{10,11},{11... | collective-permute-start | bytes 1105928 | tf_op jit(solution)/shard_map/ppermute | solution.py:363
  41.7 0.6 copy-start.7
  42.4 12.9 %copy-start.6 = (bf16[2,256,64]{2,1,0:T(8,128)(2,1)S(1)}, bf16[2,256,64]{2,1,0:T(8,128)(2,1)}, u32[]{:S(2)}) copy-start(bf16[2,256,64]{2,1,0:T(8,128)(2,1)} %constant.25.clone.table) | copy-start | bytes 196612
  46.1 9.1 %all-to-all-start.2 = ((f32[8,24,128]{2,1,0:T(8,128)}), f32[8,24,128]{2,1,0:T(8,128)S(1)}, u32[]{:S(2)}, u32[]{:S(2)}) async-start(f32[8,24,128]{2,1,0:T(8,128)} %shard_map.103), calls=%async_computation.2 | async-start | bytes 196608 | tf_op jit(solution)/shard_map/all_to_all | solution.py:424
  51.0 9.3 %copy-start.5 = (s32[2]{0:T(128)S(1)}, s32[2]{0:T(128)}, u32[]{:S(2)}) copy-start(s32[2]{0:T(128)} %copy-done.4) | copy-start | bytes 28
  51.1 9.3 %collective-permute-start.3 = (f32[3,40,768]{2,1,0:T(8,128)}, f32[3,40,768]{2,1,0:T(8,128)}, u32[]{:S(2)}, u32[]{:S(2)}) collective-permute-start(f32[3,40,768]{2,1,0:T(8,128)} %pad_maximum_fusion.1), channel_id=1, source_target_pairs={{1,0},{2,1},{3,2},{4,3},{5,4},{6,5},{7,6},{9,8},{10,9},{11,10},{12... | collective-permute-start | bytes 1105928 | tf_op jit(solution)/shard_map/ppermute | solution.py:363
  56.3 17.8 %all-to-all-start.3 = ((f32[32,24,128]{2,1,0:T(8,128)}), f32[32,24,128]{2,1,0:T(8,128)S(1)}, u32[]{:S(2)}, u32[]{:S(2)}) async-start(f32[32,24,128]{2,1,0:T(8,128)} %shard_map.104), calls=%async_computation.3 | async-start | bytes 786432 | tf_op jit(solution)/shard_map/all_to_all | solution.py:429
  60.2 13.9 %copy-start.1 = (bf16[2,256,256]{2,1,0:T(8,128)(2,1)S(1)}, bf16[2,256,256]{2,1,0:T(8,128)(2,1)}, u32[]{:S(2)}) copy-start(bf16[2,256,256]{2,1,0:T(8,128)(2,1)} %constant.26.clone.table) | copy-start | bytes 786436

commit v10 on v9

--- a/solution.py
+++ b/solution.py
@@ -226,7 +226,7 @@
         out_ref[r, ROW:, 128:] = jnp.zeros((ROW, 128), BF16)
 
 
-def convolve_rows(load_row, rows_in, width, taps, refs, finish):
+def convolve_rows(load_row, rows_in, width, taps, refs, finish, late=()):
     stack_a, stack_b, first_sum, second_sum, whole = refs
     z_position = lax.broadcasted_iota(jnp.int32, (CP, LANES), 1) % NZ
     has_lower = z_position >= 1
@@ -281,7 +281,11 @@
         return carry
 
     prepare(0, stack_a)
-    lax.fori_loop(0, rows_in // 2, pair, 0)
+    middle = (rows_in - 4) // 2 if late else 0
+    if late:
+        lax.fori_loop(0, middle, pair, 0)
+        wait(late)
+    lax.fori_loop(middle, rows_in // 2, pair, 0)
     emit(rows_in - 3)
 
 
@@ -318,12 +322,12 @@
 
 
 def convolutions_body(sizes, before, left, own, right, after, place, taps, out_ref, *refs):
-    rows, first, second = refs[:3]
-    wide, narrow = refs[3:8], refs[8:]
+    rows, first, second, sems = refs[:4]
+    wide, narrow = refs[4:9], refs[9:]
     count = own.shape[0]
+    late = copies([(after, rows.at[3 + count : 6 + count])], sems)
     rows[0:3] = before[...]
     join((left, own, right), slice(0, count), rows, 3)
-    rows[3 + count :] = after[...]
     keep = inside(place, -2, sizes, 512)
 
     def finish_first(row, tiles):
@@ -337,7 +341,7 @@
     def finish_third(row, tiles):
         out_ref[row] = jnp.concatenate(tiles[1:3], axis=1)
 
-    convolve_rows(lambda i: rows[i], count + 6, 768, taps.at[0], wide, finish_first)
+    convolve_rows(lambda i: rows[i], count + 6, 768, taps.at[0], wide, finish_first, late)
     convolve_rows(lambda i: first[i], count + 4, 512, taps.at[1], narrow, finish_second)
     convolve_rows(lambda i: second[i], count + 2, 512, taps.at[2], narrow, finish_third)
 
@@ -435,9 +439,10 @@
             pltpu.VMEM((cells_y + 6, CP, 768), F32),
             pltpu.VMEM((cells_y + 4, CP, 512), F32),
             pltpu.VMEM((cells_y + 2, CP, 512), F32),
+            pltpu.SemaphoreType.DMA((1,)),
         ]
         + conv_scratch(768) + conv_scratch(512),
-        smem=(5,), flops=CONV << 20,
+        smem=(5,), hbm=(4,), flops=CONV << 20,
     )
     return call(
         last_body, jax.ShapeDtypeStruct(field.shape, F32), received, third, z_out,

time: 76 us -> 76 us (level)
  transfers between devices with their start and end apart: 8 -> 8, of which waited for: 5 -> 5; matrix products, arithmetic and copies ran while one was open for 1% -> 1% of each run, Pallas kernels for 26% -> 25%
where the time goes in v10:
time: 76 us; the launch traced here: 75.2 us
  starting transfers between devices  38.3 us (50%)
  Pallas kernels  22.4 us (29%)
  waiting for transfers between devices  11.3 us (15%)
  local copies, waits for them, and re-layouts  2.16 us (3%)
  other arithmetic  0.87 us (1%)
    pallas_call x7, Pallas kernels, call(): pl.pallas_call(body, out_shape=out_shape, in_specs=in_specs, out_specs=tu...  22.4 us
    all_to_all x2, starting transfers between devices, shards(): received = lax.all_to_all(sent, 'gx', 0, 0, tiled=True)  15.9 us
    all_to_all x2, starting transfers between devices, shards(): received = lax.all_to_all(sent, 'gy', 0, 0, tiled=True)  12.3 us
    ppermute x4, starting transfers between devices, shift(): return lax.ppermute(values, axis, pairs)  10.1 us
    all_to_all x2, waiting for transfers between devices, shards(): received = lax.all_to_all(sent, 'gx', 0, 0, tiled=True)  7.76 us
    all_to_all x2, waiting for transfers between devices, shards(): received = lax.all_to_all(sent, 'gy', 0, 0, tiled=True)  3.4 us
    unnamed x16, local copies, waits for them, and re-layouts  2.11 us
  transfers between devices with their start and end apart: 8, of which 5 were waited for; matrix products, arithmetic and copies ran while one was open for 1% of the time, Pallas kernels for 25%

profile of v10, /device:TPU:1, one launch (start us, length us, event | category | flops | bytes accessed | tf_op | source)
XLA Modules:
  0.0 75.2 jit_solution(9733941080402554451)
XLA Ops:
  0.0 2.3 %shard_map.100 = (f32[8,40,256]{2,1,0:T(8,128)}, f32[32,24,128]{2,1,0:T(8,128)}) custom-call(f32[36,4,512]{2,1,0:T(4,128)} %field_hbm.1, bf16[2,256,256]{2,1,0:T(8,128)(2,1)} %constant.21.clone.table_hbm), custom_call_target="tpu_custom_call" | custom-call | bytes 557056 | tf_op jit(solution)/shard_map/pallas_call | solution.py:93
  2.3 12.0 %all-to-all-start = ((f32[32,24,128]{2,1,0:T(8,128)}), f32[32,24,128]{2,1,0:T(8,128)S(1)}, u32[]{:S(2)}, u32[]{:S(2)}) async-start(f32[32,24,128]{2,1,0:T(8,128)} %get-tuple-element.16), calls=%async_computation | async-start | bytes 786432 | tf_op jit(solution)/shard_map/all_to_all | solution.py:403
  14.3 3.2 %collective-permute-start = (f32[8,40,256]{2,1,0:T(8,128)}, f32[8,40,256]{2,1,0:T(8,128)S(1)}, u32[]{:S(2)}, u32[]{:S(2)}) collective-permute-start(f32[8,40,256]{2,1,0:T(8,128)} %get-tuple-element.19.refs_2_), channel_id=1, source_target_pairs={{0,8},{8,16},{16,24},{24,32},{32,40},{40,48},{48,56},{56,64},{64,7... | collective-permute-start | bytes 983048 | tf_op jit(solution)/shard_map/ppermute | solution.py:367
  17.5 1.3 %collective-permute-start.1 = (f32[8,40,256]{2,1,0:T(8,128)}, f32[8,40,256]{2,1,0:T(8,128)S(1)}, u32[]{:S(2)}, u32[]{:S(2)}) collective-permute-start(f32[8,40,256]{2,1,0:T(8,128)} %get-tuple-element.19.refs_2_), channel_id=1, source_target_pairs={{8,0},{16,8},{24,16},{32,24},{40,32},{48,40},{56,48},{64,56},{72,6... | collective-permute-start | bytes 983048 | tf_op jit(solution)/shard_map/ppermute | solution.py:367
  18.8 0.1 pad_add_fusion.after.place.refs_5_
  18.9 1.4 %copy-done = f32[3,27,36,36]{3,2,1,0:T(8,128)S(1)} copy-done((f32[3,27,36,36]{3,2,1,0:T(8,128)S(1)}, f32[3,27,36,36]{3,2,1,0:T(8,128)}, u32[]{:S(2)}) %copy-start) | copy-done | bytes 419928
  20.3 1.2 %shard_map.101.refs_6_ = bf16[3,672,256]{2,1,0:T(8,128)(2,1)S(1)} custom-call(f32[3,27,36,36]{3,2,1,0:T(8,128)S(1)} %copy-done, s32[2]{0:T(128)S(1)} %pad_add_fusion.after.place.refs_5_), custom_call_target="tpu_custom_call" | custom-call | bytes 419912 | tf_op jit(solution)/shard_map/pallas_call | solution.py:93
  21.6 6.1 %all-to-all-done.received = f32[32,24,128]{2,1,0:T(8,128)S(1)} async-done(((f32[32,24,128]{2,1,0:T(8,128)}), f32[32,24,128]{2,1,0:T(8,128)S(1)}, u32[]{:S(2)}, u32[]{:S(2)}) %all-to-all-start) | async-done | bytes 393248 | tf_op jit(solution)/shard_map/all_to_all | solution.py:403
  27.7 0.9 %shard_map.102 = f32[8,24,128]{2,1,0:T(8,128)} custom-call(f32[32,24,128]{2,1,0:T(8,128)S(1)} %all-to-all-done.received, bf16[2,64,256]{2,1,0:T(8,128)(2,1)S(1)} %copy-done.3), custom_call_target="tpu_custom_call" | custom-call | bytes 458752 | tf_op jit(solution)/shard_map/pallas_call | solution.py:93
  28.6 8.2 %all-to-all-start.1 = ((f32[8,24,128]{2,1,0:T(8,128)}), f32[8,24,128]{2,1,0:T(8,128)S(1)}, u32[]{:S(2)}, u32[]{:S(2)}) async-start(f32[8,24,128]{2,1,0:T(8,128)} %shard_map.102), calls=%async_computation.1 | async-start | bytes 196608 | tf_op jit(solution)/shard_map/all_to_all | solution.py:409
  36.8 3.5 %collective-permute-start.2 = (f32[3,40,768]{2,1,0:T(8,128)S(1)}, f32[3,40,768]{2,1,0:T(8,128)S(1)}, u32[]{:S(2)}, u32[]{:S(2)}) collective-permute-start(f32[3,40,768]{2,1,0:T(8,128)S(1)} %pad_maximum_fusion), channel_id=1, source_target_pairs={{0,1},{1,2},{2,3},{3,4},{4,5},{5,6},{6,7},{8,9},{9,10},{10,11},{11... | collective-permute-start | bytes 1105928 | tf_op jit(solution)/shard_map/ppermute | solution.py:367
  40.4 1.4 %all-to-all-done.1.received_hbm = f32[8,24,128]{2,1,0:T(8,128)S(1)} async-done(((f32[8,24,128]{2,1,0:T(8,128)}), f32[8,24,128]{2,1,0:T(8,128)S(1)}, u32[]{:S(2)}, u32[]{:S(2)}) %all-to-all-start.1) | async-done | bytes 98336 | tf_op jit(solution)/shard_map/all_to_all | solution.py:409
  41.7 0.6 copy-done.7
  42.4 3.8 %shard_map.103 = f32[8,24,128]{2,1,0:T(8,128)} custom-call(f32[8,24,128]{2,1,0:T(8,128)} %copy-done.7, f32[2,1296,128]{2,1,0:T(8,128)} %bitcast.4, s32[1,128]{1,0:T(1,128)} %bitcast.5, s32[2]{0:T(128)} %copy-done.4, bf16[2,256,512]{2,1,0:T(8,128)(2,1)} %constant.23.clone.y_in_hbm, bf16[2,512,256]{2,1,0:T(8,128)(2,1)} %constant.24.clone.y_out_hbm), custom_call_target="tpu_custom_call" | custom-call | flops 8589934592 | bytes 2474504 | tf_op jit(solution)/shard_map/pallas_call | solution.py:93
  46.1 4.1 %all-to-all-start.2 = ((f32[8,24,128]{2,1,0:T(8,128)}), f32[8,24,128]{2,1,0:T(8,128)S(1)}, u32[]{:S(2)}, u32[]{:S(2)}) async-start(f32[8,24,128]{2,1,0:T(8,128)} %shard_map.103), calls=%async_computation.2 | async-start | bytes 196608 | tf_op jit(solution)/shard_map/all_to_all | solution.py:428
  50.3 0.8 %pad_maximum_fusion.1 = f32[3,40,768]{2,1,0:T(8,128)} fusion(f32[3,40,256]{2,1,0:T(8,128)S(1)} %slice.23, f32[3,40,256]{2,1,0:T(8,128)S(1)} %get-tuple-element.27, f32[3,40,256]{2,1,0:T(8,128)S(1)} %slice.21), kind=kLoop, calls=%fused_computation.1 | loop fusion | flops 184320 | bytes 737280 | tf_op jit(solution)/shard_map/concatenate | solution.py:412
  51.1 2.1 %collective-permute-start.3 = (f32[3,40,768]{2,1,0:T(8,128)}, f32[3,40,768]{2,1,0:T(8,128)}, u32[]{:S(2)}, u32[]{:S(2)}) collective-permute-start(f32[3,40,768]{2,1,0:T(8,128)} %pad_maximum_fusion.1), channel_id=1, source_target_pairs={{1,0},{2,1},{3,2},{4,3},{5,4},{6,5},{7,6},{9,8},{10,9},{11,10},{12... | collective-permute-start | bytes 1105928 | tf_op jit(solution)/shard_map/ppermute | solution.py:367
  53.2 2.0 %all-to-all-done.2.received = f32[8,24,128]{2,1,0:T(8,128)S(1)} async-done(((f32[8,24,128]{2,1,0:T(8,128)}), f32[8,24,128]{2,1,0:T(8,128)S(1)}, u32[]{:S(2)}, u32[]{:S(2)}) %all-to-all-start.2) | async-done | bytes 98336 | tf_op jit(solution)/shard_map/all_to_all | solution.py:428
  55.3 1.0 %shard_map.104 = f32[32,24,128]{2,1,0:T(8,128)} custom-call(f32[8,24,128]{2,1,0:T(8,128)S(1)} %all-to-all-done.2.received, bf16[2,256,64]{2,1,0:T(8,128)(2,1)S(1)} %copy-done.6), custom_call_target="tpu_custom_call" | custom-call | flops 8589934592 | bytes 163840 | tf_op jit(solution)/shard_map/pallas_call | solution.py:93
  56.3 3.9 %all-to-all-start.3 = ((f32[32,24,128]{2,1,0:T(8,128)}), f32[32,24,128]{2,1,0:T(8,128)S(1)}, u32[]{:S(2)}, u32[]{:S(2)}) async-start(f32[32,24,128]{2,1,0:T(8,128)} %shard_map.104), calls=%async_computation.3 | async-start | bytes 786432 | tf_op jit(solution)/shard_map/all_to_all | solution.py:433
  60.2 0.1 collective-permute-done.3.refs_4_
  60.3 12.1 %shard_map.105.third = f32[8,40,256]{2,1,0:T(8,128)S(1)} custom-call(f32[3,40,768]{2,1,0:T(8,128)S(1)} %collective-permute-done.2.refs_0_, f32[8,40,256]{2,1,0:T(8,128)S(1)} %collective-permute-done.refs_1_, f32[8,40,256]{2,1,0:T(8,128)S(1)} %copy-done.2, f32[8,40,256]{2,1,0:T(8,128)S(1)} %collective-permute-done.1.refs_3_, ...), custom_call_target="tpu_custom_call" | custom-call | flops 12884901888 | bytes 2752520 | tf_op jit(solution)/shard_map/pallas_call | solution.py:93
  72.4 1.7 %all-to-all-done.3.received = f32[32,24,128]{2,1,0:T(8,128)S(1)} async-done(((f32[32,24,128]{2,1,0:T(8,128)}), f32[32,24,128]{2,1,0:T(8,128)S(1)}, u32[]{:S(2)}, u32[]{:S(2)}) %all-to-all-start.3) | async-done | bytes 393248 | tf_op jit(solution)/shard_map/all_to_all | solution.py:433
  74.1 1.2 %shard_map.106 = f32[36,4,512]{2,1,0:T(4,128)} custom-call(f32[32,24,128]{2,1,0:T(8,128)S(1)} %all-to-all-done.3.received, f32[8,40,256]{2,1,0:T(8,128)S(1)} %shard_map.105.third, bf16[2,256,256]{2,1,0:T(8,128)(2,1)S(1)} %copy-done.1), custom_call_target="tpu_custom_call" | custom-call | bytes 983040 | tf_op jit(solution)/shard_map/pallas_call | solution.py:93
  (23 shorter events, 0.1 us)
Async XLA Ops:
  2.3 19.2 %copy-start.2 = (f32[8,40,256]{2,1,0:T(8,128)S(1)}, f32[8,40,256]{2,1,0:T(8,128)}, u32[]{:S(2)}) copy-start(f32[8,40,256]{2,1,0:T(8,128)} %get-tuple-element.19.refs_2_) | copy-start | bytes 983044
  2.3 25.4 %copy-start.3 = (bf16[2,64,256]{2,1,0:T(8,128)(2,1)S(1)}, bf16[2,64,256]{2,1,0:T(8,128)(2,1)}, u32[]{:S(2)}) copy-start(bf16[2,64,256]{2,1,0:T(8,128)(2,1)} %constant.22.clone.table) | copy-start | bytes 196612
  2.3 25.4 %all-to-all-start = ((f32[32,24,128]{2,1,0:T(8,128)}), f32[32,24,128]{2,1,0:T(8,128)S(1)}, u32[]{:S(2)}, u32[]{:S(2)}) async-start(f32[32,24,128]{2,1,0:T(8,128)} %get-tuple-element.16), calls=%async_computation | async-start | bytes 786432 | tf_op jit(solution)/shard_map/all_to_all | solution.py:403
  14.3 22.4 %collective-permute-start = (f32[8,40,256]{2,1,0:T(8,128)}, f32[8,40,256]{2,1,0:T(8,128)S(1)}, u32[]{:S(2)}, u32[]{:S(2)}) collective-permute-start(f32[8,40,256]{2,1,0:T(8,128)} %get-tuple-element.19.refs_2_), channel_id=1, source_target_pairs={{0,8},{8,16},{16,24},{24,32},{32,40},{40,48},{48,56},{56,64},{64,7... | collective-permute-start | bytes 983048 | tf_op jit(solution)/shard_map/ppermute | solution.py:367
  17.5 19.2 %collective-permute-start.1 = (f32[8,40,256]{2,1,0:T(8,128)}, f32[8,40,256]{2,1,0:T(8,128)S(1)}, u32[]{:S(2)}, u32[]{:S(2)}) collective-permute-start(f32[8,40,256]{2,1,0:T(8,128)} %get-tuple-element.19.refs_2_), channel_id=1, source_target_pairs={{8,0},{16,8},{24,16},{32,24},{40,32},{48,40},{56,48},{64,56},{72,6... | collective-permute-start | bytes 983048 | tf_op jit(solution)/shard_map/ppermute | solution.py:367
  18.9 1.4 %copy-start = (f32[3,27,36,36]{3,2,1,0:T(8,128)S(1)}, f32[3,27,36,36]{3,2,1,0:T(8,128)}, u32[]{:S(2)}) copy-start(f32[3,27,36,36]{3,2,1,0:T(8,128)} %kernels.1) | copy-start | bytes 1259716
  20.3 8.2 %copy-start.4 = (s32[2]{0:T(128)}, s32[2]{0:T(128)S(1)}, u32[]{:S(2)}) copy-start(s32[2]{0:T(128)S(1)} %pad_add_fusion.after.place.refs_5_) | copy-start | bytes 28
  28.6 13.2 %all-to-all-start.1 = ((f32[8,24,128]{2,1,0:T(8,128)}), f32[8,24,128]{2,1,0:T(8,128)S(1)}, u32[]{:S(2)}, u32[]{:S(2)}) async-start(f32[8,24,128]{2,1,0:T(8,128)} %shard_map.102), calls=%async_computation.1 | async-start | bytes 196608 | tf_op jit(solution)/shard_map/all_to_all | solution.py:409
  36.8 23.4 %collective-permute-start.2 = (f32[3,40,768]{2,1,0:T(8,128)S(1)}, f32[3,40,768]{2,1,0:T(8,128)S(1)}, u32[]{:S(2)}, u32[]{:S(2)}) collective-permute-start(f32[3,40,768]{2,1,0:T(8,128)S(1)} %pad_maximum_fusion), channel_id=1, source_target_pairs={{0,1},{1,2},{2,3},{3,4},{4,5},{5,6},{6,7},{8,9},{9,10},{10,11},{11... | collective-permute-start | bytes 1105928 | tf_op jit(solution)/shard_map/ppermute | solution.py:367
  41.7 0.6 copy-start.7
  42.4 12.9 %copy-start.6 = (bf16[2,256,64]{2,1,0:T(8,128)(2,1)S(1)}, bf16[2,256,64]{2,1,0:T(8,128)(2,1)}, u32[]{:S(2)}) copy-start(bf16[2,256,64]{2,1,0:T(8,128)(2,1)} %constant.25.clone.table) | copy-start | bytes 196612
  46.1 9.1 %all-to-all-start.2 = ((f32[8,24,128]{2,1,0:T(8,128)}), f32[8,24,128]{2,1,0:T(8,128)S(1)}, u32[]{:S(2)}, u32[]{:S(2)}) async-start(f32[8,24,128]{2,1,0:T(8,128)} %shard_map.103), calls=%async_computation.2 | async-start | bytes 196608 | tf_op jit(solution)/shard_map/all_to_all | solution.py:428
  51.0 9.3 %copy-start.5 = (s32[2]{0:T(128)S(1)}, s32[2]{0:T(128)}, u32[]{:S(2)}) copy-start(s32[2]{0:T(128)} %copy-done.4) | copy-start | bytes 28
  51.1 9.3 %collective-permute-start.3 = (f32[3,40,768]{2,1,0:T(8,128)}, f32[3,40,768]{2,1,0:T(8,128)}, u32[]{:S(2)}, u32[]{:S(2)}) collective-permute-start(f32[3,40,768]{2,1,0:T(8,128)} %pad_maximum_fusion.1), channel_id=1, source_target_pairs={{1,0},{2,1},{3,2},{4,3},{5,4},{6,5},{7,6},{9,8},{10,9},{11,10},{12... | collective-permute-start | bytes 1105928 | tf_op jit(solution)/shard_map/ppermute | solution.py:367
  56.3 17.8 %all-to-all-start.3 = ((f32[32,24,128]{2,1,0:T(8,128)}), f32[32,24,128]{2,1,0:T(8,128)S(1)}, u32[]{:S(2)}, u32[]{:S(2)}) async-start(f32[32,24,128]{2,1,0:T(8,128)} %shard_map.104), calls=%async_computation.3 | async-start | bytes 786432 | tf_op jit(solution)/shard_map/all_to_all | solution.py:433
  60.2 13.9 %copy-start.1 = (bf16[2,256,256]{2,1,0:T(8,128)(2,1)S(1)}, bf16[2,256,256]{2,1,0:T(8,128)(2,1)}, u32[]{:S(2)}) copy-start(bf16[2,256,256]{2,1,0:T(8,128)(2,1)} %constant.26.clone.table) | copy-start | bytes 786436
